TPU v7x, 32 devices: a whole 2x2x4 slice. The times are simulated.
32 devices in a mesh: atm: 8 (over y, x, core), xg: 4 (over z).
Axes of the slice: x: 2, y: 2, z: 4, core: 2. Of those that a mesh axis runs over, the one named last changes fastest.
Arguments:
- fields_now: float32 [128, 48, 52, 128], P('atm', None, 'xg'), may hold values from -6 to 6
- upper: float32 [128, 48, 128], P(('atm', 'xg')), may hold values from 0.05 to 20
- lower: float32 [128, 48, 128], P(('atm', 'xg')), may hold values from 0.05 to 20
- surface_gain: float32 [128, 128], P(('atm', 'xg')), may hold values from 0.3 to 3
- route: int32 [8, 32, 2], P('atm'), may hold values from 0 to 16
- margin_slot: int32 [32, 96], P(('atm', 'xg')), may hold values from 0 to 15
- margin_block: int32 [32, 96], P(('atm', 'xg')), may hold values from 0 to 15
- margin_count: int32 [32], P(('atm', 'xg')), may hold values from 12 to 96, as said below
- margin_weight: float32 [32, 96, 128, 128], P(('atm', 'xg')), may hold values from 0 to 0.03
- surface_value: float32 [512, 52, 128], P(('atm', 'xg')), may hold values from -6 to 6
- exchange_coef: float32 [512, 128], P(('atm', 'xg')), may hold values from 0.05 to 2
- land_mask: int32 [512, 128], P(('atm', 'xg')), may hold values 0 or 1
- land_gain: float32 [512, 128], P(('atm', 'xg')), may hold values from 0.2 to 5
Outputs:
- fields_next: float32 [128, 48, 52, 128], P('atm', None, 'xg')
- surface_flux: float32 [512, 52, 128], P(('atm', 'xg'))
Inputs may be any that keep to these rules, and one draw needn't show every extreme that they name: `route`: the value 16 marks an empty slot; other values name a local column block of the sending atmosphere index. `margin_slot`: A value s names slot s % 2 from atmosphere index s // 2. `margin_count`: margins from this count on are padding; some owner has all 96 live.
All inputs are finite; a program needn't handle non-finite values. No bound on the sum of `land_mask` on one device may be relied on, other than what follows from the above.
Results may differ from a plain program's by a relative error of at most 0.0003.
Values sent between devices are 32-bit elements; how exact they have to be, the bound alone decides.
No kernel may reach another device: no remote copies, remote signals or barrier semaphores. Data moves between devices by JAX's collectives and lax.ppermute only.
A program may use at most 128 MiB of HBM per device.

v0:
```python
import jax
import jax.numpy as jnp
from jax import lax
from jax.sharding import PartitionSpec as P

HIGHEST = lax.Precision.HIGHEST


def factors(upper, lower):
    level_count = upper.shape[1]
    carried = jnp.zeros_like(upper[:, 0])
    inverses, multipliers, carries = ([], [], [])
    for height in range(level_count):
        from_above = upper[:, height] if height > 0 else jnp.zeros_like(carried)
        from_below = lower[:, height] if height < level_count - 1 else jnp.zeros_like(carried)
        inverse = 1.0 / (1.0 + from_above + from_below - from_above * carried)
        carried = from_below * inverse
        inverses.append(inverse)
        multipliers.append(from_above * inverse)
        carries.append(carried)
    return (jnp.stack(inverses, 1), jnp.stack(multipliers, 1), jnp.stack(carries, 1))


def per_device(
    fields_now,
    upper,
    lower,
    surface_gain,
    route,
    margin_slot,
    margin_block,
    margin_count,
    margin_weight,
    surface_value,
    exchange_coef,
    land_mask,
    land_gain,
):
    atm_count = lax.axis_size("atm")
    xg_count = lax.axis_size("xg")
    own_inverse, own_multiplier, own_carry = factors(upper, lower)
    own_bottom = surface_gain * own_inverse[:, -1]
    inverse, multiplier, carry_factor, bottom_gain = (
        lax.all_gather(own_inverse, "xg", axis=0, tiled=True),
        lax.all_gather(own_multiplier, "xg", axis=0, tiled=True),
        lax.all_gather(own_carry, "xg", axis=0, tiled=True),
        lax.all_gather(own_bottom, "xg", axis=0, tiled=True),
    )
    block_count = fields_now.shape[0]
    level_count = fields_now.shape[1]
    field_share = fields_now.shape[2]
    block_width = fields_now.shape[3]
    running = jnp.zeros_like(fields_now[:, 0])
    partials = []
    for height in range(level_count):
        running = (
            inverse[:, height, None, :] * fields_now[:, height]
            + multiplier[:, height, None, :] * running
        )
        partials.append(running)
    routing = route[0]
    pair_slots = routing.shape[1]
    quarter = block_width // xg_count
    send_value = jnp.concatenate(
        [running, jnp.zeros((1, field_share, block_width), jnp.float32)], 0
    )[routing]
    own_columns = lax.dynamic_slice_in_dim(bottom_gain, lax.axis_index("xg") * quarter, quarter, 1)
    send_gain = jnp.concatenate([own_columns, jnp.zeros((1, quarter), jnp.float32)], 0)[routing]
    got_value, got_gain = (
        lax.all_to_all(send_value, ("atm", "xg"), split_axis=0, concat_axis=0, tiled=True),
        lax.all_to_all(send_gain, ("atm", "xg"), split_axis=0, concat_axis=0, tiled=True),
    )
    got_value = got_value.reshape(atm_count, xg_count, pair_slots, field_share, block_width)
    got_gain = got_gain.reshape(atm_count, xg_count, pair_slots, quarter)
    slot_index = margin_slot[0]
    source = slot_index // pair_slots
    pair_index = slot_index % pair_slots
    margins = slot_index.shape[0]
    alive = (jnp.arange(margins, dtype=jnp.int32) < margin_count[0]).astype(jnp.float32)
    value_slots = got_value[source, :, pair_index].reshape(
        margins, xg_count * field_share, block_width
    )
    gain_slots = got_gain[source, :, pair_index].reshape(margins, block_width)
    weight = margin_weight[0]
    cell_blocks = surface_value.shape[0]
    select = (margin_block[0][None, :] == jnp.arange(cell_blocks, dtype=jnp.int32)[:, None]).astype(
        jnp.float32
    ) * alive[None, :]
    value_part = jnp.einsum("kxb,kfb->kfx", weight, value_slots, precision=HIGHEST)
    gain_part = jnp.einsum("kxb,kb->kx", weight, gain_slots, precision=HIGHEST)
    cell_value = jnp.einsum("jk,kfx->jfx", select, value_part, precision=HIGHEST)
    cell_gain = jnp.einsum("jk,kx->jx", select, gain_part, precision=HIGHEST)
    coupling = exchange_coef[:, None, :]
    land_total = land_mask.astype(jnp.float32) * land_gain
    surface_flux = (
        coupling
        * (surface_value - cell_value)
        / (1.0 + coupling * (cell_gain + land_total)[:, None, :])
    )
    returned = jnp.einsum("kxb,kfx->kfb", weight, surface_flux[margin_block[0]], precision=HIGHEST)
    returned = returned.reshape(margins, xg_count, field_share, block_width)
    by_source = (source[None, None, :] == jnp.arange(atm_count, dtype=jnp.int32)[:, None, None]) & (
        pair_index[None, None, :] == jnp.arange(pair_slots, dtype=jnp.int32)[None, :, None]
    )
    by_source = by_source.astype(jnp.float32) * alive[None, None, :]
    reply = jnp.einsum("apk,kgfb->agpfb", by_source, returned, precision=HIGHEST)
    answer = lax.all_to_all(
        reply.reshape(atm_count * xg_count, pair_slots, field_share, block_width),
        ("atm", "xg"),
        split_axis=0,
        concat_axis=0,
        tiled=True,
    )
    route_select = (
        routing[None, :, :] == jnp.arange(block_count, dtype=jnp.int32)[:, None, None]
    ).astype(jnp.float32)
    column_flux = jnp.einsum("rdp,dpfb->rfb", route_select, answer, precision=HIGHEST)
    state = running + bottom_gain[:, None, :] * column_flux
    outputs = [state]
    for height in range(level_count - 2, -1, -1):
        state = partials[height] + carry_factor[:, height, None, :] * state
        outputs.append(state)
    fields_next = jnp.stack(outputs[::-1], 1)
    return (fields_next, surface_flux)


def solution(mesh):
    in_specs = (
        P("atm", None, "xg", None),
        P(("atm", "xg"), None, None),
        P(("atm", "xg"), None, None),
        P(("atm", "xg"), None),
        P("atm", None, None),
        P(("atm", "xg"), None),
        P(("atm", "xg"), None),
        P(("atm", "xg")),
        P(("atm", "xg"), None, None, None),
        P(("atm", "xg"), None, None),
        P(("atm", "xg"), None),
        P(("atm", "xg"), None),
        P(("atm", "xg"), None),
    )
    out_specs = (P("atm", None, "xg", None), P(("atm", "xg"), None, None))
    return jax.shard_map(
        per_device, mesh=mesh, in_specs=in_specs, out_specs=out_specs, check_vma=False
    )
```

profile of v0, /device:TPU:0, one launch (start us, length us, event | category | flops | bytes accessed | tf_op | source)
XLA Modules:
  0.0 191.3 jit_solution(15118442074869055433)
XLA Ops:
  0.6 1.0 fusion.217
  1.6 1.2 fusion.213
  2.9 1.2 fusion.216
  4.1 1.2 fusion.218
  5.3 1.4 fusion.214
  6.7 1.2 fusion.215
  8.0 0.7 fusion.173
  8.6 0.7 compare_select_fusion
  9.3 0.1 copy.867
  9.4 0.1 reshape.318
  9.5 1.3 multiply_bitcast_fusion
  10.8 13.6 %all-gather = f32[4,4,128]{2,1,0:T(4,128)S(1)} all-gather(f32[1,4,128]{2,1,0:T(4,128)S(1)} %get-tuple-element.36), channel_id=1, replica_groups=mesh['atm'=8,'xg'=4] {'xg'}, dimensions={0}, use_global_device_ids=true | all-gather | bytes 10240 | tf_op jit(solution)/shard_map/all_gather | solution.py:47
  24.5 0.6 copy-done.67
  25.0 0.1 constant_dynamic-slice_fusion
  25.1 1.2 gather_fusion.2
  26.3 4.3 %all-to-all-start.1 = ((f32[32,2,32]{2,1,0:T(2,128)}), f32[32,2,32]{2,1,0:T(2,128)S(1)}, u32[]{:S(2)}, u32[]{:S(2)}) async-start(f32[32,2,32]{2,1,0:T(2,128)} %bitcast.394), calls=%async_computation.1 | async-start | bytes 65536 | tf_op jit(solution)/shard_map/all_to_all | solution.py:71
  30.7 0.7 fusion.174
  31.3 0.7 and_select_fusion.1
  32.9 14.9 %all_gather.13 = f32[16,48,128]{2,1,0:T(8,128)S(1)} all-gather(f32[4,48,128]{2,1,0:T(8,128)S(1)} %copy.818), channel_id=1, replica_groups=mesh['atm'=8,'xg'=4] {'xg'}, dimensions={0}, use_global_device_ids=true | all-gather | bytes 491520 | tf_op jit(solution)/shard_map/all_gather | solution.py:45
  47.9 0.1 fusion.208
  48.1 0.7 fusion.210
  48.9 0.2 stack.412
  49.1 15.5 %all_gather.12 = f32[16,48,128]{2,1,0:T(8,128)S(1)} all-gather(f32[4,48,128]{2,1,0:T(8,128)S(1)} %stack.412), channel_id=1, replica_groups=mesh['atm'=8,'xg'=4] {'xg'}, dimensions={0}, use_global_device_ids=true | all-gather | bytes 491520 | tf_op jit(solution)/shard_map/all_gather | solution.py:44
  64.6 0.7 fusion.211
  65.3 0.7 fusion.207
  66.0 0.7 fusion.209
  66.8 5.1 %fusion.203 = (f32[16,1,13,128]{3,1,2,0:T(1,128)S(1)}, f32[16,1,13,128]{3,1,2,0:T(1,128)S(1)}, f32[16,1,13,128]{3,1,2,0:T(1,128)S(1)}, f32[16,1,13,128]{3,1,2,0:...) fusion(f32[16,48,13,128]{3,1,2,0:T(8,128)} %param.13), kind=kLoop, calls=%fused_computation.526 | loop fusion | bytes 2129920 | tf_op jit(solution)/shard_map/slice | solution.py:57
  71.9 9.1 %fusion.202 = (f32[16,1,13,128]{3,1,2,0:T(1,128)S(1)}, f32[16,1,13,128]{3,1,2,0:T(1,128)S(1)}, f32[16,1,13,128]{3,1,2,0:T(1,128)S(1)}, f32[16,1,13,128]{3,1,2,0:...) fusion(f32[16,48,13,128]{3,1,2,0:T(8,128)} %param.13), kind=kLoop, calls=%fused_computation.525 | loop fusion | bytes 4046848 | tf_op jit(solution)/shard_map/slice | solution.py:57
  81.1 9.1 %fusion.201 = (f32[16,1,13,128]{3,1,2,0:T(1,128)S(1)}, f32[16,1,13,128]{3,1,2,0:T(1,128)S(1)}, f32[16,1,13,128]{3,1,2,0:T(1,128)S(1)}, f32[16,1,13,128]{3,1,2,0:...) fusion(f32[16,48,13,128]{3,1,2,0:T(8,128)} %param.13), kind=kLoop, calls=%fused_computation.524 | loop fusion | bytes 4046848 | tf_op jit(solution)/shard_map/slice | solution.py:57
  91.1 3.0 %fusion.24 = (f32[16,13,128]{2,0,1:T(8,128)S(1)}, f32[16,13,128]{2,0,1:T(8,128)S(1)}, f32[16,13,128]{2,0,1:T(8,128)S(1)}, f32[16,13,128]{2,0,1:T(8,128)S(1)}, f3...) fusion(f32[16,1,13,128]{3,1,2,0:T(1,128)S(1)} %get-tuple-elemen, ...), kind=kLoop, calls=%fused_computation.171 | loop fusion | flops 3807232 | bytes 8454144 | tf_op jit(solution)/shard_map/add | solution.py:57
  94.2 0.7 copy.819
  95.1 0.6 gather_fusion
  95.8 1.0 copy.869
  96.7 5.4 %all-to-all-start = ((f32[32,2,13,128]{3,1,2,0:T(2,128)}), f32[32,2,13,128]{3,1,2,0:T(2,128)S(1)}, u32[]{:S(2)}, u32[]{:S(2)}) async-start(f32[32,2,13,128]{3,1,2,0:T(2,128)} %copy.869), calls=%async_computation | async-start | bytes 851968 | tf_op jit(solution)/shard_map/all_to_all | solution.py:70
  102.1 1.2 gather_fusion.3
  103.3 0.1 copy.877
  103.4 0.1 copy.884
  103.5 11.8 %fusion.2 = f32[96,1,128]{2,1,0:T(1,128)S(1)} fusion(f32[96,128,1]{1,2,0:T(1,128)S(1)} %copy.884, f32[1,96,128,128]{3,2,1,0:T(8,128)} %param.21), kind=kOutput, calls=%fused_computation.7 | convolution fusion | flops 18874368 | bytes 6389760 | tf_op jit(solution)/shard_map/kxb,kb->kx/dot_general | solution.py:90
  115.4 0.1 fusion.21
  115.6 0.1 copy.871
  115.7 2.8 %gather_fusion.1 = f32[96,4,13,128]{3,1,2,0:T(4,128)S(1)} fusion(f32[8,4,2,13,128]{4,1,3,2,0:T(4,128)S(1)} %copy.871, s32[96]{0:T(128)S(1)} %fusion.174), kind=kCustom, calls=%fused_computation.1 | custom fusion | bytes 5112576 | tf_op jit(solution)/shard_map/gather | solution.py:80
  118.5 0.3 copy.872
  118.8 16.4 %fusion.4 = f32[96,52,128]{2,1,0:T(8,128)S(1)} fusion(f32[1,96,128,128]{3,2,1,0:T(8,128)} %param.21, f32[96,52,128]{2,0,1:T(8,128)S(1)} %bitcast.1218), kind=kOutput, calls=%fused_computation.9 | convolution fusion | flops 981467136 | bytes 11403264 | tf_op jit(solution)/shard_map/kxb,kfb->kfx/dot_general | solution.py:89
  135.2 1.6 fusion.15
  136.9 0.1 copy.878
  137.0 0.6 copy-done
  137.6 0.8 gather_fusion.4
  138.4 7.8 %fusion = f32[96,52,128]{2,1,0:T(8,128)S(1)} fusion(f32[96,52,128]{2,1,0:T(8,128)S(1)} %gather_fusion.4, f32[1,96,128,128]{3,2,1,0:T(8,128)} %param.21), kind=kOutput, calls=%fused_computation.5 | convolution fusion | flops 981467136 | bytes 11403264 | tf_op jit(solution)/shard_map/kxb,kfx->kfb/dot_general | solution.py:100
  146.5 0.5 copy.879
  147.0 1.5 convolution_bitcast_fusion
  148.5 0.2 copy.880
  148.6 1.1 copy.881
  149.7 5.7 %all-to-all-start.2 = ((f32[32,2,13,128]{3,1,2,0:T(2,128)}), f32[32,2,13,128]{3,1,2,0:T(2,128)S(1)}, u32[]{:S(2)}, u32[]{:S(2)}) async-start(f32[32,2,13,128]{3,1,2,0:T(2,128)} %copy.881), calls=%async_computation.2 | async-start | bytes 851968 | tf_op jit(solution)/shard_map/all_to_all | solution.py:107
  155.4 21.2 %all_gather.14 = f32[16,48,128]{2,1,0:T(8,128)S(1)} all-gather(f32[4,48,128]{2,1,0:T(8,128)} %copy.819), channel_id=1, replica_groups=mesh['atm'=8,'xg'=4] {'xg'}, dimensions={0}, use_global_device_ids=true | all-gather | bytes 491520 | tf_op jit(solution)/shard_map/all_gather | solution.py:46
  176.6 0.7 fusion.206
  177.3 0.8 fusion.204
  178.1 0.8 fusion.205
  179.2 3.5 %constant_dynamic-update-slice_fusion.143 = (f32[16,48,13,128]{3,0,2,1:T(8,128)S(1)}, f32[16,13,128]{2,0,1:T(8,128)S(1)}, f32[16,13,128]{2,0,1:T(8,128)S(1)}, f3...) fusion(f32[16,1,13,128]{3,1,2,0:T(1,128)S(1)} %copy-done.32, ...), kind=kOutput, calls=%fused_computation.168 | convolution fusion | flops 24894464 | bytes 8986880 | tf_op jit(solution)/shard_map/rdp,dpfb->rfb/dot_general | solution.py:117
  182.8 0.7 constant_dynamic-update-slice_fusion.141
  183.6 0.7 constant_dynamic-update-slice_fusion.139
  184.4 0.7 constant_dynamic-update-slice_fusion.133
  185.1 0.7 constant_dynamic-update-slice_fusion.131
  185.9 0.7 constant_dynamic-update-slice_fusion.129
  187.4 3.9 %copy.883 = f32[16,48,13,128]{3,1,2,0:T(8,128)} copy(f32[16,48,13,128]{3,0,2,1:T(8,128)S(1)} %constant_dynamic-update-slice_fusion.96) | data formatting | bytes 10223616
  (278 shorter events, 1.9 us)
Async XLA Ops:
  26.3 70.4 %all-to-all-start.1 = ((f32[32,2,32]{2,1,0:T(2,128)}), f32[32,2,32]{2,1,0:T(2,128)S(1)}, u32[]{:S(2)}, u32[]{:S(2)}) async-start(f32[32,2,32]{2,1,0:T(2,128)} %bitcast.394), calls=%async_computation.1 | async-start | bytes 65536 | tf_op jit(solution)/shard_map/all_to_all | solution.py:71
  47.8 43.1 %copy-start.68 = (f32[16,1,128]{2,1,0:T(1,128)}, f32[16,1,128]{2,1,0:T(1,128)S(1)}, u32[]{:S(2)}) copy-start(f32[16,1,128]{2,1,0:T(1,128)S(1)} %get-tuple-element.321) | copy-start | bytes 24580
  47.9 43.1 %copy-start.69 = (f32[16,1,128]{2,1,0:T(1,128)}, f32[16,1,128]{2,1,0:T(1,128)S(1)}, u32[]{:S(2)}) copy-start(f32[16,1,128]{2,1,0:T(1,128)S(1)} %get-tuple-element.323) | copy-start | bytes 24580
  47.9 43.1 %copy-start.70 = (f32[16,1,128]{2,1,0:T(1,128)}, f32[16,1,128]{2,1,0:T(1,128)S(1)}, u32[]{:S(2)}) copy-start(f32[16,1,128]{2,1,0:T(1,128)S(1)} %get-tuple-element.325) | copy-start | bytes 24580
  47.9 43.1 %copy-start.71 = (f32[16,1,128]{2,1,0:T(1,128)}, f32[16,1,128]{2,1,0:T(1,128)S(1)}, u32[]{:S(2)}) copy-start(f32[16,1,128]{2,1,0:T(1,128)S(1)} %get-tuple-element.327) | copy-start | bytes 24580
  47.9 43.1 %copy-start.72 = (f32[16,1,128]{2,1,0:T(1,128)}, f32[16,1,128]{2,1,0:T(1,128)S(1)}, u32[]{:S(2)}) copy-start(f32[16,1,128]{2,1,0:T(1,128)S(1)} %get-tuple-element.328) | copy-start | bytes 24580
  47.9 43.1 %copy-start.73 = (f32[16,1,128]{2,1,0:T(1,128)}, f32[16,1,128]{2,1,0:T(1,128)S(1)}, u32[]{:S(2)}) copy-start(f32[16,1,128]{2,1,0:T(1,128)S(1)} %get-tuple-element.329) | copy-start | bytes 24580
  48.0 43.0 %copy-start.74 = (f32[16,1,128]{2,1,0:T(1,128)}, f32[16,1,128]{2,1,0:T(1,128)S(1)}, u32[]{:S(2)}) copy-start(f32[16,1,128]{2,1,0:T(1,128)S(1)} %get-tuple-element.256) | copy-start | bytes 24580
  48.0 43.0 %copy-start.75 = (f32[16,1,128]{2,1,0:T(1,128)}, f32[16,1,128]{2,1,0:T(1,128)S(1)}, u32[]{:S(2)}) copy-start(f32[16,1,128]{2,1,0:T(1,128)S(1)} %get-tuple-element.258) | copy-start | bytes 24580
  48.0 43.0 %copy-start.76 = (f32[16,1,128]{2,1,0:T(1,128)}, f32[16,1,128]{2,1,0:T(1,128)S(1)}, u32[]{:S(2)}) copy-start(f32[16,1,128]{2,1,0:T(1,128)S(1)} %get-tuple-element.260) | copy-start | bytes 24580
  48.1 43.0 %copy-start.77 = (f32[16,1,128]{2,1,0:T(1,128)}, f32[16,1,128]{2,1,0:T(1,128)S(1)}, u32[]{:S(2)}) copy-start(f32[16,1,128]{2,1,0:T(1,128)S(1)} %get-tuple-element.262) | copy-start | bytes 24580
  48.1 43.0 %copy-start.78 = (f32[16,1,128]{2,1,0:T(1,128)}, f32[16,1,128]{2,1,0:T(1,128)S(1)}, u32[]{:S(2)}) copy-start(f32[16,1,128]{2,1,0:T(1,128)S(1)} %get-tuple-element.264) | copy-start | bytes 24580
  48.1 43.0 %copy-start.79 = (f32[16,1,128]{2,1,0:T(1,128)}, f32[16,1,128]{2,1,0:T(1,128)S(1)}, u32[]{:S(2)}) copy-start(f32[16,1,128]{2,1,0:T(1,128)S(1)} %get-tuple-element.266) | copy-start | bytes 24580
  48.1 43.0 %copy-start.80 = (f32[16,1,128]{2,1,0:T(1,128)}, f32[16,1,128]{2,1,0:T(1,128)S(1)}, u32[]{:S(2)}) copy-start(f32[16,1,128]{2,1,0:T(1,128)S(1)} %get-tuple-element.268) | copy-start | bytes 24580
  48.1 43.0 %copy-start.81 = (f32[16,1,128]{2,1,0:T(1,128)}, f32[16,1,128]{2,1,0:T(1,128)S(1)}, u32[]{:S(2)}) copy-start(f32[16,1,128]{2,1,0:T(1,128)S(1)} %get-tuple-element.270) | copy-start | bytes 24580
  48.9 42.2 %copy-start.82 = (f32[16,1,128]{2,1,0:T(1,128)}, f32[16,1,128]{2,1,0:T(1,128)S(1)}, u32[]{:S(2)}) copy-start(f32[16,1,128]{2,1,0:T(1,128)S(1)} %get-tuple-element.291) | copy-start | bytes 24580
  71.8 22.3 %copy-start.23 = (f32[16,1,13,128]{3,1,2,0:T(1,128)}, f32[16,1,13,128]{3,1,2,0:T(1,128)S(1)}, u32[]{:S(2)}) copy-start(f32[16,1,13,128]{3,1,2,0:T(1,128)S(1)} %get-tuple-element.179) | copy-start | bytes 319492
  71.8 22.3 %copy-start.25 = (f32[16,1,13,128]{3,1,2,0:T(1,128)}, f32[16,1,13,128]{3,1,2,0:T(1,128)S(1)}, u32[]{:S(2)}) copy-start(f32[16,1,13,128]{3,1,2,0:T(1,128)S(1)} %get-tuple-element.181) | copy-start | bytes 319492
  71.9 22.3 %copy-start.27 = (f32[16,1,13,128]{3,1,2,0:T(1,128)}, f32[16,1,13,128]{3,1,2,0:T(1,128)S(1)}, u32[]{:S(2)}) copy-start(f32[16,1,13,128]{3,1,2,0:T(1,128)S(1)} %get-tuple-element.183) | copy-start | bytes 319492
  71.9 22.3 %copy-start.29 = (f32[16,1,13,128]{3,1,2,0:T(1,128)}, f32[16,1,13,128]{3,1,2,0:T(1,128)S(1)}, u32[]{:S(2)}) copy-start(f32[16,1,13,128]{3,1,2,0:T(1,128)S(1)} %get-tuple-element.184) | copy-start | bytes 319492
  71.9 22.3 %copy-start.31 = (f32[16,1,13,128]{3,1,2,0:T(1,128)}, f32[16,1,13,128]{3,1,2,0:T(1,128)S(1)}, u32[]{:S(2)}) copy-start(f32[16,1,13,128]{3,1,2,0:T(1,128)S(1)} %get-tuple-element.185) | copy-start | bytes 319492
  81.0 13.2 %copy-start.35 = (f32[16,1,13,128]{3,1,2,0:T(1,128)}, f32[16,1,13,128]{3,1,2,0:T(1,128)S(1)}, u32[]{:S(2)}) copy-start(f32[16,1,13,128]{3,1,2,0:T(1,128)S(1)} %get-tuple-element.162) | copy-start | bytes 319492
  81.0 13.2 %copy-start.36 = (f32[16,1,13,128]{3,1,2,0:T(1,128)}, f32[16,1,13,128]{3,1,2,0:T(1,128)S(1)}, u32[]{:S(2)}) copy-start(f32[16,1,13,128]{3,1,2,0:T(1,128)S(1)} %get-tuple-element.164) | copy-start | bytes 319492
  81.0 13.2 %copy-start.37 = (f32[16,1,13,128]{3,1,2,0:T(1,128)}, f32[16,1,13,128]{3,1,2,0:T(1,128)S(1)}, u32[]{:S(2)}) copy-start(f32[16,1,13,128]{3,1,2,0:T(1,128)S(1)} %get-tuple-element.166) | copy-start | bytes 319492
  81.0 13.2 %copy-start.38 = (f32[16,1,13,128]{3,1,2,0:T(1,128)}, f32[16,1,13,128]{3,1,2,0:T(1,128)S(1)}, u32[]{:S(2)}) copy-start(f32[16,1,13,128]{3,1,2,0:T(1,128)S(1)} %get-tuple-element.168) | copy-start | bytes 319492
  81.0 13.2 %copy-start.39 = (f32[16,1,13,128]{3,1,2,0:T(1,128)}, f32[16,1,13,128]{3,1,2,0:T(1,128)S(1)}, u32[]{:S(2)}) copy-start(f32[16,1,13,128]{3,1,2,0:T(1,128)S(1)} %get-tuple-element.170) | copy-start | bytes 319492
  81.0 13.2 %copy-start.40 = (f32[16,1,13,128]{3,1,2,0:T(1,128)}, f32[16,1,13,128]{3,1,2,0:T(1,128)S(1)}, u32[]{:S(2)}) copy-start(f32[16,1,13,128]{3,1,2,0:T(1,128)S(1)} %get-tuple-element.172) | copy-start | bytes 319492
  81.0 13.2 %copy-start.41 = (f32[16,1,13,128]{3,1,2,0:T(1,128)}, f32[16,1,13,128]{3,1,2,0:T(1,128)S(1)}, u32[]{:S(2)}) copy-start(f32[16,1,13,128]{3,1,2,0:T(1,128)S(1)} %get-tuple-element.174) | copy-start | bytes 319492
  81.0 13.9 %copy-start.33 = (f32[16,1,13,128]{3,1,2,0:T(1,128)}, f32[16,1,13,128]{3,1,2,0:T(1,128)S(1)}, u32[]{:S(2)}) copy-start(f32[16,1,13,128]{3,1,2,0:T(1,128)S(1)} %get-tuple-element.158) | copy-start | bytes 319492
  81.1 13.9 %copy-start.34 = (f32[16,1,13,128]{3,1,2,0:T(1,128)}, f32[16,1,13,128]{3,1,2,0:T(1,128)S(1)}, u32[]{:S(2)}) copy-start(f32[16,1,13,128]{3,1,2,0:T(1,128)S(1)} %get-tuple-element.160) | copy-start | bytes 319492
  95.1 20.3 %copy-start.83 = (f32[16,128]{1,0:T(8,128)S(1)}, f32[16,128]{1,0:T(8,128)}, u32[]{:S(2)}) copy-start(f32[16,128]{1,0:T(8,128)} %param.23) | copy-start | bytes 24580
  95.1 20.3 %copy-start.84 = (f32[16,128]{1,0:T(8,128)S(1)}, f32[16,128]{1,0:T(8,128)}, u32[]{:S(2)}) copy-start(f32[16,128]{1,0:T(8,128)} %param.25) | copy-start | bytes 24580
  95.1 20.3 %copy-start.85 = (s32[16,128]{1,0:T(8,128)S(1)}, s32[16,128]{1,0:T(8,128)}, u32[]{:S(2)}) copy-start(s32[16,128]{1,0:T(8,128)} %param.24) | copy-start | bytes 24580
  95.1 20.3 %copy-start.87 = (s32[1,96]{1,0:T(1,128)S(1)}, s32[1,96]{1,0:T(1,128)}, u32[]{:S(2)}) copy-start(s32[1,96]{1,0:T(1,128)} %param.19) | copy-start | bytes 1156
  96.7 18.8 %all-to-all-start = ((f32[32,2,13,128]{3,1,2,0:T(2,128)}), f32[32,2,13,128]{3,1,2,0:T(2,128)S(1)}, u32[]{:S(2)}, u32[]{:S(2)}) async-start(f32[32,2,13,128]{3,1,2,0:T(2,128)} %copy.869), calls=%async_computation | async-start | bytes 851968 | tf_op jit(solution)/shard_map/all_to_all | solution.py:70
  118.8 16.4 %copy-start.52 = (f32[16,52,128]{2,0,1:T(8,128)S(1)}, f32[16,52,128]{2,0,1:T(8,128)}, u32[]{:S(2)}) copy-start(f32[16,52,128]{2,0,1:T(8,128)} %param.22) | copy-start | bytes 1277956
  146.2 32.6 %copy-start.1 = (f32[16,13,128]{2,0,1:T(8,128)S(1)}, f32[16,13,128]{2,0,1:T(8,128)}, u32[]{:S(2)}) copy-start(f32[16,13,128]{2,0,1:T(8,128)} %get-tuple-element.57) | copy-start | bytes 319492
  146.2 32.6 %copy-start.2 = (f32[16,13,128]{2,0,1:T(8,128)S(1)}, f32[16,13,128]{2,0,1:T(8,128)}, u32[]{:S(2)}) copy-start(f32[16,13,128]{2,0,1:T(8,128)} %get-tuple-element.58) | copy-start | bytes 319492
  146.3 32.6 %copy-start.3 = (f32[16,13,128]{2,0,1:T(8,128)S(1)}, f32[16,13,128]{2,0,1:T(8,128)}, u32[]{:S(2)}) copy-start(f32[16,13,128]{2,0,1:T(8,128)} %get-tuple-element.59) | copy-start | bytes 319492
  146.3 32.6 %copy-start.4 = (f32[16,13,128]{2,0,1:T(8,128)S(1)}, f32[16,13,128]{2,0,1:T(8,128)}, u32[]{:S(2)}) copy-start(f32[16,13,128]{2,0,1:T(8,128)} %get-tuple-element.60) | copy-start | bytes 319492
  146.3 32.6 %copy-start.5 = (f32[16,13,128]{2,0,1:T(8,128)S(1)}, f32[16,13,128]{2,0,1:T(8,128)}, u32[]{:S(2)}) copy-start(f32[16,13,128]{2,0,1:T(8,128)} %get-tuple-element.61) | copy-start | bytes 319492
  146.3 32.6 %copy-start.6 = (f32[16,13,128]{2,0,1:T(8,128)S(1)}, f32[16,13,128]{2,0,1:T(8,128)}, u32[]{:S(2)}) copy-start(f32[16,13,128]{2,0,1:T(8,128)} %get-tuple-element.62) | copy-start | bytes 319492
  146.3 32.6 %copy-start.7 = (f32[16,13,128]{2,0,1:T(8,128)S(1)}, f32[16,13,128]{2,0,1:T(8,128)}, u32[]{:S(2)}) copy-start(f32[16,13,128]{2,0,1:T(8,128)} %get-tuple-element.63) | copy-start | bytes 319492
  146.3 32.6 %copy-start.8 = (f32[16,13,128]{2,0,1:T(8,128)S(1)}, f32[16,13,128]{2,0,1:T(8,128)}, u32[]{:S(2)}) copy-start(f32[16,13,128]{2,0,1:T(8,128)} %get-tuple-element.64) | copy-start | bytes 319492
  146.3 32.6 %copy-start.9 = (f32[16,13,128]{2,0,1:T(8,128)S(1)}, f32[16,13,128]{2,0,1:T(8,128)}, u32[]{:S(2)}) copy-start(f32[16,13,128]{2,0,1:T(8,128)} %get-tuple-element.65) | copy-start | bytes 319492
  146.3 32.6 %copy-start.10 = (f32[16,13,128]{2,0,1:T(8,128)S(1)}, f32[16,13,128]{2,0,1:T(8,128)}, u32[]{:S(2)}) copy-start(f32[16,13,128]{2,0,1:T(8,128)} %get-tuple-element.66) | copy-start | bytes 319492
  146.3 32.6 %copy-start.11 = (f32[16,13,128]{2,0,1:T(8,128)S(1)}, f32[16,13,128]{2,0,1:T(8,128)}, u32[]{:S(2)}) copy-start(f32[16,13,128]{2,0,1:T(8,128)} %get-tuple-element.67) | copy-start | bytes 319492
  146.3 32.6 %copy-start.12 = (f32[16,13,128]{2,0,1:T(8,128)S(1)}, f32[16,13,128]{2,0,1:T(8,128)}, u32[]{:S(2)}) copy-start(f32[16,13,128]{2,0,1:T(8,128)} %get-tuple-element.68) | copy-start | bytes 319492
  146.4 32.6 %copy-start.13 = (f32[16,13,128]{2,0,1:T(8,128)S(1)}, f32[16,13,128]{2,0,1:T(8,128)}, u32[]{:S(2)}) copy-start(f32[16,13,128]{2,0,1:T(8,128)} %get-tuple-element.69) | copy-start | bytes 319492
  146.4 32.6 %copy-start.14 = (f32[16,13,128]{2,0,1:T(8,128)S(1)}, f32[16,13,128]{2,0,1:T(8,128)}, u32[]{:S(2)}) copy-start(f32[16,13,128]{2,0,1:T(8,128)} %get-tuple-element.70) | copy-start | bytes 319492
  146.4 32.6 %copy-start.15 = (f32[16,13,128]{2,0,1:T(8,128)S(1)}, f32[16,13,128]{2,0,1:T(8,128)}, u32[]{:S(2)}) copy-start(f32[16,13,128]{2,0,1:T(8,128)} %get-tuple-element.71) | copy-start | bytes 319492
  146.4 32.6 %copy-start.16 = (f32[16,13,128]{2,0,1:T(8,128)S(1)}, f32[16,13,128]{2,0,1:T(8,128)}, u32[]{:S(2)}) copy-start(f32[16,13,128]{2,0,1:T(8,128)} %get-tuple-element.72) | copy-start | bytes 319492
  146.4 32.6 %copy-start.17 = (f32[16,13,128]{2,0,1:T(8,128)S(1)}, f32[16,13,128]{2,0,1:T(8,128)}, u32[]{:S(2)}) copy-start(f32[16,13,128]{2,0,1:T(8,128)} %get-tuple-element.73) | copy-start | bytes 319492
  146.4 32.6 %copy-start.18 = (f32[16,13,128]{2,0,1:T(8,128)S(1)}, f32[16,13,128]{2,0,1:T(8,128)}, u32[]{:S(2)}) copy-start(f32[16,13,128]{2,0,1:T(8,128)} %get-tuple-element.74) | copy-start | bytes 319492
  146.4 32.6 %copy-start.19 = (f32[16,13,128]{2,0,1:T(8,128)S(1)}, f32[16,13,128]{2,0,1:T(8,128)}, u32[]{:S(2)}) copy-start(f32[16,13,128]{2,0,1:T(8,128)} %get-tuple-element.75) | copy-start | bytes 319492
  146.4 32.6 %copy-start.20 = (f32[16,13,128]{2,0,1:T(8,128)S(1)}, f32[16,13,128]{2,0,1:T(8,128)}, u32[]{:S(2)}) copy-start(f32[16,13,128]{2,0,1:T(8,128)} %get-tuple-element.76) | copy-start | bytes 319492
  146.4 32.6 %copy-start.22 = (f32[16,13,128]{2,0,1:T(8,128)S(1)}, f32[16,13,128]{2,0,1:T(8,128)}, u32[]{:S(2)}) copy-start(f32[16,13,128]{2,0,1:T(8,128)} %copy-done.21) | copy-start | bytes 319492
  146.4 32.6 %copy-start.24 = (f32[16,1,13,128]{3,1,2,0:T(1,128)S(1)}, f32[16,1,13,128]{3,1,2,0:T(1,128)}, u32[]{:S(2)}) copy-start(f32[16,1,13,128]{3,1,2,0:T(1,128)} %copy-done.23) | copy-start | bytes 319492
  146.5 32.6 %copy-start.26 = (f32[16,1,13,128]{3,1,2,0:T(1,128)S(1)}, f32[16,1,13,128]{3,1,2,0:T(1,128)}, u32[]{:S(2)}) copy-start(f32[16,1,13,128]{3,1,2,0:T(1,128)} %copy-done.25) | copy-start | bytes 319492
  146.5 32.6 %copy-start.28 = (f32[16,1,13,128]{3,1,2,0:T(1,128)S(1)}, f32[16,1,13,128]{3,1,2,0:T(1,128)}, u32[]{:S(2)}) copy-start(f32[16,1,13,128]{3,1,2,0:T(1,128)} %copy-done.27) | copy-start | bytes 319492
  146.5 32.6 %copy-start.30 = (f32[16,1,13,128]{3,1,2,0:T(1,128)S(1)}, f32[16,1,13,128]{3,1,2,0:T(1,128)}, u32[]{:S(2)}) copy-start(f32[16,1,13,128]{3,1,2,0:T(1,128)} %copy-done.29) | copy-start | bytes 319492
  146.5 32.6 %copy-start.32 = (f32[16,1,13,128]{3,1,2,0:T(1,128)S(1)}, f32[16,1,13,128]{3,1,2,0:T(1,128)}, u32[]{:S(2)}) copy-start(f32[16,1,13,128]{3,1,2,0:T(1,128)} %copy-done.31) | copy-start | bytes 319492
  146.5 32.6 %copy-start.86 = (s32[1,32,2]{1,2,0:T(2,128)S(1)}, s32[1,32,2]{1,2,0:T(2,128)}, u32[]{:S(2)}) copy-start(s32[1,32,2]{1,2,0:T(2,128)} %param.17) | copy-start | bytes 772
  149.7 29.1 %all-to-all-start.2 = ((f32[32,2,13,128]{3,1,2,0:T(2,128)}), f32[32,2,13,128]{3,1,2,0:T(2,128)S(1)}, u32[]{:S(2)}, u32[]{:S(2)}) async-start(f32[32,2,13,128]{3,1,2,0:T(2,128)} %copy.881), calls=%async_computation.2 | async-start | bytes 851968 | tf_op jit(solution)/shard_map/all_to_all | solution.py:107
  (27 other events, 133.1 us)
where the time goes:
time: 193 us; the launch traced here: 191 us
  blocking collectives  65.3 us (34%)
  local copies, waits for them, and re-layouts  52.7 us (27%)
  matrix products  42.8 us (22%)
  starting transfers between devices  15.4 us (8%)
  other arithmetic  11.8 us (6%)
  between operations  3.31 us (2%)
    slice x3, local copies, waits for them, and re-layouts, per_device(): fields_now[:, height]  23.2 us
    all_gather x1, blocking collectives, per_device(): lax.all_gather(own_carry, 'xg', axis=0, tiled=True)  21.2 us
    dot_general x1, matrix products, per_device(): jnp.einsum('kxb,kfb->kfx', weight, value_slots, precision=HIGHEST)  16.4 us
    all_gather x1, blocking collectives, per_device(): lax.all_gather(own_inverse, 'xg', axis=0, tiled=True)  15.5 us
    all_gather x1, blocking collectives, per_device(): lax.all_gather(own_multiplier, 'xg', axis=0, tiled=True)  14.9 us
    all_gather x1, blocking collectives, per_device(): lax.all_gather(own_bottom, 'xg', axis=0, tiled=True)  13.6 us
    dot_general x1, matrix products, per_device(): gain_part = jnp.einsum('kxb,kb->kx', weight, gain_slots, precision=HIGHEST)  11.8 us
    dot_general x1, matrix products, per_device(): jnp.einsum('kxb,kfx->kfb', weight, surface_flux[margin_block[0]], precisi...  7.85 us
  transfers between devices with their start and end apart: 3, of which 0 were waited for; matrix products, arithmetic and copies ran while one was open for 26% of the time, Pallas kernels for 0%

commit v1 on v0

v1 whole, which is shorter than its diff:
```python
import functools
import math

import jax
import jax.numpy as jnp
from jax import lax
from jax.experimental import pallas as pl
from jax.experimental.pallas import tpu as pltpu
from jax.sharding import PartitionSpec as P

F32 = jnp.float32
BF16 = jnp.bfloat16
ROWS = 8


def vmem():
    return pl.BlockSpec(memory_space=pltpu.VMEM)


def smem():
    return pl.BlockSpec(memory_space=pltpu.SMEM)


def hbm():
    return pl.BlockSpec(memory_space=pl.ANY)


def params(limit=None):
    return pltpu.CompilerParams(vmem_limit_bytes=limit)


def round_up(value, step):
    return -(-value // step) * step


def split(value):
    high = value.astype(BF16)
    low = (value - high.astype(F32)).astype(BF16)
    return high, low


def factor_kernel(levels, own, upper_ref, lower_ref, gain_ref, first_ref, second_ref, inverse_ref):
    carried = jnp.zeros(gain_ref.shape, F32)
    for k in range(levels):
        from_above = upper_ref[pl.ds(k, own, stride=levels), :] if k > 0 else jnp.zeros_like(carried)
        from_below = lower_ref[pl.ds(k, own, stride=levels), :] if k < levels - 1 else jnp.zeros_like(carried)
        inverse = 1.0 / (1.0 + from_above + from_below - from_above * carried)
        carried = from_below * inverse
        inverse_ref[k] = inverse
        second_ref[k] = from_above * inverse
        second_ref[levels + k] = carried
    product = inverse_ref[levels - 1]
    first_ref[levels] = gain_ref[...] * product
    first_ref[levels - 1] = product
    product = second_ref[levels - 1]
    for k in range(levels - 2, -1, -1):
        first_ref[k] = inverse_ref[k] * product
        product = product * second_ref[k]


def factors(upper, lower, surface_gain):
    own, levels, width = upper.shape
    return pl.pallas_call(
        functools.partial(factor_kernel, levels, own),
        out_shape=(
            jax.ShapeDtypeStruct((levels + 1, own, width), F32),
            jax.ShapeDtypeStruct((2 * levels, own, width), F32),
        ),
        in_specs=[vmem()] * 3,
        out_specs=(vmem(), vmem()),
        scratch_shapes=[pltpu.VMEM((levels, own, width), F32)],
        compiler_params=params(8 << 20),
        cost_estimate=pl.CostEstimate(flops=1000000, bytes_accessed=400000, transcendentals=30000),
        name="factors",
    )(upper.reshape(own * levels, width), lower.reshape(own * levels, width), surface_gain)


def fetch_fields(me, groups, own, fields_ref, held_ref, sem):
    shares = fields_ref.shape[1]
    for f in range(shares):
        for q in range(groups):
            base = lax.rem(me - q + groups, groups) * own
            for i in range(own):
                pltpu.make_async_copy(
                    fields_ref.at[base + i, f], held_ref.at[f, :, q * own + i, :], sem.at[f]
                ).start()


def bottom_kernel(groups, own, rows, me_ref, place_ref, *refs):
    parts, fields_ref, send_ref, held_ref, weight_ref, value_ref, sem = (
        refs[:groups], *refs[groups:]
    )
    fetch_fields(me_ref[0], groups, own, fields_ref, held_ref, sem)
    blocks = groups * own
    levels = held_ref.shape[1]
    shares = held_ref.shape[0]
    for q in range(groups):
        weight_ref[:, q * own:(q + 1) * own, :] = parts[q][...]
    value_ref[...] = jnp.zeros_like(value_ref)
    value_ref[pl.ds(shares, blocks, stride=rows), :] = weight_ref[levels]
    for f in range(shares):
        pltpu.make_async_copy(held_ref.at[f], held_ref.at[f], sem.at[f]).wait()
        sums = [None] * 4
        for k in range(levels):
            term = weight_ref[k] * held_ref[f, k]
            sums[k % 4] = term if sums[k % 4] is None else sums[k % 4] + term
        value_ref[pl.ds(f, blocks, stride=rows), :] = (sums[0] + sums[1]) + (sums[2] + sums[3])
    owners, slot_rows = send_ref.shape[:2]
    slots = slot_rows // rows
    for d in range(owners):
        for p in range(slots):
            start = pl.multiple_of(place_ref[d * slots + p] * rows, rows)
            send_ref[d, p * rows:(p + 1) * rows, :] = value_ref[pl.ds(start, rows), :]


def bottoms(me, place, parts, fields, owners, slots, rows):
    blocks, shares, levels, width = fields.shape
    groups = len(parts)
    own = blocks // groups
    return pl.pallas_call(
        functools.partial(bottom_kernel, groups, own, rows),
        out_shape=jax.ShapeDtypeStruct((owners, slots * rows, width), F32),
        in_specs=[smem(), smem()] + [vmem()] * groups + [hbm()],
        out_specs=vmem(),
        scratch_shapes=[
            pltpu.VMEM((shares, levels, blocks, width), F32),
            pltpu.VMEM((levels + 1, blocks, width), F32),
            pltpu.VMEM(((blocks + 1) * rows, width), F32),
            pltpu.SemaphoreType.DMA((shares,)),
        ],
        compiler_params=params(16 << 20),
        cost_estimate=pl.CostEstimate(flops=4000000, bytes_accessed=7000000, transcendentals=0),
        name="bottoms",
    )(me, place, *parts, fields)


def split_kernel(weight_ref, out_ref):
    high, low = split(weight_ref[...])
    size = weight_ref.shape[1]
    out_ref[:, :size, :] = high
    out_ref[:, size:, :] = low


def split_weights(weight, step=8):
    margins, cells, columns = weight.shape
    step = math.gcd(step, margins)
    return pl.pallas_call(
        split_kernel,
        grid=(margins // step,),
        out_shape=jax.ShapeDtypeStruct((margins, 2 * cells, columns), BF16),
        in_specs=[pl.BlockSpec((step, cells, columns), lambda i: (i, 0, 0))],
        out_specs=pl.BlockSpec((step, 2 * cells, columns), lambda i: (i, 0, 0)),
        compiler_params=params(8 << 20),
        cost_estimate=pl.CostEstimate(flops=5000000, bytes_accessed=13000000, transcendentals=0),
        name="split_weights",
    )(weight)


def margin_kernel(
    groups, rows, slots, gain_row, unroll,
    slot_ref, block_ref, count_ref, weight_hbm, got_ref, surface_ref, coef_ref, mask_ref, land_ref,
    reply_ref, flux_ref,
    weight_ref, value_ref, cell_ref, two_ref, back_ref, sem,
):
    margins = weight_ref.shape[0]
    chunks = sem.shape[0]
    size = margins // chunks
    for c in range(chunks):
        pltpu.make_async_copy(
            weight_hbm.at[pl.ds(c * size, size)], weight_ref.at[pl.ds(c * size, size)], sem.at[c]
        ).start()
    tall = groups * rows
    columns = weight_ref.shape[2]
    sources = value_ref.shape[0] // slots
    cells = surface_ref.shape[0]
    count = count_ref[0]
    for a in range(sources):
        for p in range(slots):
            for g in range(groups):
                high, low = split(got_ref[a * groups + g, p * rows:(p + 1) * rows, :])
                value_ref[a * slots + p, g * rows:(g + 1) * rows, :] = high
                value_ref[a * slots + p, tall + g * rows:tall + (g + 1) * rows, :] = low
    cell_ref[...] = jnp.zeros_like(cell_ref)
    back_ref[...] = jnp.zeros_like(back_ref)

    for c in range(chunks):
        pltpu.make_async_copy(
            weight_hbm.at[pl.ds(c * size, size)], weight_ref.at[pl.ds(c * size, size)], sem.at[c]
        ).wait()

        @pl.loop(0, size // unroll)
        def _(step):
            for u in range(unroll):
                k = c * size + step * unroll + u
                target = jnp.where(k < count, block_ref[k], cells)
                product = lax.dot_general(
                    value_ref[slot_ref[k]], weight_ref[k], (((1,), (1,)), ((), ())),
                    preferred_element_type=F32,
                )
                cell_ref[target] += (
                    product[:tall, :columns] + (product[tall:, :columns] + product[:tall, columns:])
                )

    for j in range(cells):
        cell = cell_ref[j]
        coef = coef_ref[j:j + 1, :]
        land = mask_ref[j:j + 1, :].astype(F32) * land_ref[j:j + 1, :]
        scale = coef / (1.0 + coef * (cell[gain_row:gain_row + 1, :] + land))
        flux = scale * (surface_ref[j] - cell)
        flux_ref[j] = flux
        high, low = split(flux)
        two_ref[j, :tall, :columns] = high
        two_ref[j, :tall, columns:] = high
        two_ref[j, tall:, :columns] = low
        two_ref[j, tall:, columns:] = low

    @pl.loop(0, margins // unroll)
    def _(step):
        for u in range(unroll):
            k = step * unroll + u
            target = jnp.where(k < count, slot_ref[k], sources * slots)
            product = lax.dot_general(
                two_ref[block_ref[k]], weight_ref[k], (((1,), (0,)), ((), ())),
                preferred_element_type=F32,
            )
            back_ref[target] += product[:tall] + product[tall:]

    for a in range(sources):
        for p in range(slots):
            for g in range(groups):
                reply_ref[a * groups + g, p * rows:(p + 1) * rows, :] = (
                    back_ref[a * slots + p, g * rows:(g + 1) * rows, :]
                )


def margins_stage(slot, block, count, weights, got, surface, coef, mask, land, groups, rows, slots, gain_row):
    margins, twice, columns = weights.shape
    owners, slot_rows, width = got.shape
    cells, tall, _ = surface.shape
    sources = owners // groups
    unroll = 4
    chunks = 6
    return pl.pallas_call(
        functools.partial(margin_kernel, groups, rows, slots, gain_row, unroll),
        out_shape=(
            jax.ShapeDtypeStruct(got.shape, F32),
            jax.ShapeDtypeStruct(surface.shape, F32),
        ),
        in_specs=[smem()] * 3 + [hbm()] + [vmem()] * 5,
        out_specs=(vmem(), vmem()),
        scratch_shapes=[
            pltpu.VMEM(weights.shape, BF16),
            pltpu.VMEM((sources * slots, 2 * tall, width), BF16),
            pltpu.VMEM((cells + 1, tall, width), F32),
            pltpu.VMEM((cells, 2 * tall, 2 * width), BF16),
            pltpu.VMEM((sources * slots + 1, tall, width), F32),
            pltpu.SemaphoreType.DMA((chunks,)),
        ],
        compiler_params=params(24 << 20),
        cost_estimate=pl.CostEstimate(flops=800000000, bytes_accessed=8000000, transcendentals=0),
        name="margins",
    )(slot, block, count, weights, got, surface, coef, mask, land)


def sweep_kernel(groups, own, me_ref, *refs):
    parts, gains, fields_ref, after_ref, still_ref, reach_ref, held_ref, factor_ref, sem, out_sem = (
        refs[:groups], refs[groups:2 * groups], *refs[2 * groups:]
    )
    fetch_fields(me_ref[0], groups, own, fields_ref, held_ref, sem)
    shares, levels, blocks, width = held_ref.shape
    for q in range(groups):
        factor_ref[levels:, q * own:(q + 1) * own, :] = parts[q][...]
        reach_ref[levels - 1, q * own:(q + 1) * own, :] = gains[q][levels]
    reach = reach_ref[levels - 1]
    for k in range(levels - 1, -1, -1):
        carry = factor_ref[2 * levels + k]
        above = factor_ref[2 * levels + k - 1] if k > 0 else jnp.zeros_like(carry)
        factor_ref[k] = 1.0 - carry - factor_ref[levels + k] * (1.0 - above)
        if k < levels - 1:
            reach = carry * reach
            reach_ref[k] = reach
    for f in range(shares):
        pltpu.make_async_copy(held_ref.at[f], held_ref.at[f], sem.at[f]).wait()
        partial = factor_ref[0] * held_ref[f, 0]
        held_ref[f, 0] = partial
        for k in range(1, levels):
            partial = factor_ref[k] * held_ref[f, k] + factor_ref[levels + k] * partial
            held_ref[f, k] = partial
        for k in range(levels - 2, -1, -1):
            partial = held_ref[f, k] + factor_ref[2 * levels + k] * partial
            held_ref[f, k] = partial
        pltpu.make_async_copy(held_ref.at[f], still_ref.at[f], out_sem.at[f]).start()
    for f in range(shares):
        pltpu.make_async_copy(held_ref.at[f], still_ref.at[f], out_sem.at[f]).wait()


def sweeps(me, parts, gains, fields, after):
    blocks, shares, levels, width = fields.shape
    groups = len(parts)
    own = blocks // groups
    return pl.pallas_call(
        functools.partial(sweep_kernel, groups, own),
        out_shape=(
            jax.ShapeDtypeStruct((shares, levels, blocks, width), F32),
            jax.ShapeDtypeStruct((levels, blocks, width), F32),
        ),
        in_specs=[smem()] + [vmem()] * (2 * groups) + [hbm(), hbm()],
        out_specs=(hbm(), vmem()),
        scratch_shapes=[
            pltpu.VMEM((shares, levels, blocks, width), F32),
            pltpu.VMEM((3 * levels, blocks, width), F32),
            pltpu.SemaphoreType.DMA((shares,)),
            pltpu.SemaphoreType.DMA((shares,)),
        ],
        compiler_params=params(16 << 20),
        cost_estimate=pl.CostEstimate(flops=8000000, bytes_accessed=12000000, transcendentals=0),
        name="sweeps",
    )(me, *parts, *gains, fields, after)


def finish_kernel(groups, own, rows, me_ref, place_ref, answer_ref, still_ref, reach_ref, out_ref,
                  held_ref, flux_ref, sem, out_sem):
    shares, levels, blocks, width = held_ref.shape
    for f in range(shares):
        pltpu.make_async_copy(still_ref.at[f], held_ref.at[f], sem.at[f]).start()
    flux_ref[...] = jnp.zeros_like(flux_ref)
    owners, slot_rows = answer_ref.shape[:2]
    slots = slot_rows // rows
    for d in range(owners):
        for p in range(slots):
            start = pl.multiple_of(place_ref[d * slots + p] * rows, rows)
            flux_ref[pl.ds(start, rows), :] += answer_ref[d, p * rows:(p + 1) * rows, :]
    me = me_ref[0]
    copies = []
    for f in range(shares):
        flux = flux_ref[pl.ds(f, blocks, stride=rows), :]
        pltpu.make_async_copy(still_ref.at[f], held_ref.at[f], sem.at[f]).wait()
        for k in range(levels):
            held_ref[f, k] = held_ref[f, k] + reach_ref[k] * flux
        for q in range(groups):
            base = lax.rem(me - q + groups, groups) * own
            for i in range(own):
                pltpu.make_async_copy(
                    held_ref.at[f, :, q * own + i, :], out_ref.at[base + i, f], out_sem.at[f]
                ).start()
    for f in range(shares):
        pltpu.make_async_copy(held_ref.at[f], held_ref.at[f], out_sem.at[f]).wait()


def finish(me, place, answer, still, reach, groups, rows):
    shares, levels, blocks, width = still.shape
    return pl.pallas_call(
        functools.partial(finish_kernel, groups, blocks // groups, rows),
        out_shape=jax.ShapeDtypeStruct((blocks, shares, levels, width), F32),
        in_specs=[smem(), smem(), vmem(), hbm(), vmem()],
        out_specs=hbm(),
        scratch_shapes=[
            pltpu.VMEM((shares, levels, blocks, width), F32),
            pltpu.VMEM(((blocks + 1) * rows, width), F32),
            pltpu.SemaphoreType.DMA((shares,)),
            pltpu.SemaphoreType.DMA((shares,)),
        ],
        compiler_params=params(16 << 20),
        cost_estimate=pl.CostEstimate(flops=4000000, bytes_accessed=12000000, transcendentals=0),
        name="finish",
    )(me, place, answer, still, reach)


def per_device(
    fields_now, upper, lower, surface_gain, route, margin_slot, margin_block, margin_count,
    margin_weight, surface_value, exchange_coef, land_mask, land_gain,
):
    groups = lax.axis_size("xg")
    me = lax.axis_index("xg").astype(jnp.int32)
    blocks, levels, shares, width = fields_now.shape
    own = blocks // groups
    rows = round_up(shares + 1, ROWS)
    owners, slots = route.shape[1:]
    cells = surface_value.shape[0]

    def shift(array, by):
        return lax.ppermute(array, "xg", [(i, (i + by) % groups) for i in range(groups)])

    def shared(array):
        return [array] + [shift(array, by) for by in range(1, groups)]

    fields = fields_now.transpose(0, 2, 1, 3)
    first, second = factors(upper, lower, surface_gain)
    firsts = shared(first)
    routing = route[0].reshape(owners * slots)
    place = jnp.where(
        routing < blocks,
        lax.rem(me - routing // own + groups, groups) * own + routing % own,
        blocks,
    ).astype(jnp.int32)
    me = me[None]
    weights = split_weights(margin_weight[0])
    surface = jnp.pad(
        surface_value.reshape(cells, groups, shares, width),
        ((0, 0), (0, 0), (0, rows - shares), (0, 0)),
    ).reshape(cells, groups * rows, width)
    send = bottoms(me, place, firsts, fields, owners, slots, rows)
    second, send = lax.optimization_barrier((second, send))
    got = lax.all_to_all(send, ("atm", "xg"), split_axis=0, concat_axis=0, tiled=True)
    seconds = shared(second)
    reply, flux = margins_stage(
        margin_slot[0], margin_block[0], margin_count, weights, got, surface,
        exchange_coef, land_mask, land_gain, groups, rows, slots, shares,
    )
    answer = lax.all_to_all(reply, ("atm", "xg"), split_axis=0, concat_axis=0, tiled=True)
    still, reach = sweeps(me, seconds, firsts, fields, reply)
    surface_flux = flux.reshape(cells, groups, rows, width)[:, :, :shares].reshape(
        cells, groups * shares, width
    )
    out = finish(me, place, answer, still, reach, groups, rows)
    return out.transpose(0, 2, 1, 3), surface_flux


def solution(mesh):
    in_specs = (
        P("atm", None, "xg", None),
        P(("atm", "xg"), None, None),
        P(("atm", "xg"), None, None),
        P(("atm", "xg"), None),
        P("atm", None, None),
        P(("atm", "xg"), None),
        P(("atm", "xg"), None),
        P(("atm", "xg")),
        P(("atm", "xg"), None, None, None),
        P(("atm", "xg"), None, None),
        P(("atm", "xg"), None),
        P(("atm", "xg"), None),
        P(("atm", "xg"), None),
    )
    out_specs = (P("atm", None, "xg", None), P(("atm", "xg"), None, None))
    return jax.shard_map(
        per_device, mesh=mesh, in_specs=in_specs, out_specs=out_specs, check_vma=False
    )
```

time: 193 us -> 120 us (0.62)
  blocking collectives: 65.3 us -> 0 us
  matrix products: 42.8 us -> 0 us
  waiting for transfers between devices: 0.01 us -> 39.9 us
  Pallas kernels: 0 us -> 35.5 us
  local copies, waits for them, and re-layouts: 52.7 us -> 22.4 us
  other arithmetic: 11.8 us -> 0.02 us
  starting transfers between devices: 15.4 us -> 19.6 us
    all_gather x4 -> x0, blocking collectives: 65.3 us -> none  [the longest x1 21.2 us: per_device(): lax.all_gather(own_carry, 'xg', axis=0, tiled=True)]
    dot_general x7 -> x0, matrix products: 42.8 us -> none  [the longest x1 16.4 us: per_device(): jnp.einsum('kxb,kfb->kfx', weight, value_slots, precision=HIGHEST)]
    pallas_call x0 -> x6, Pallas kernels: none -> 35.5 us  [the longest x1 13.3 us: margins_stage(): pl.pallas_call(functools.partial(margin_kernel, groups, rows, slots, gain...]
    slice x17 -> x1, local copies, waits for them, and re-layouts: 35.7 us -> 1.01 us  [per_device(): flux.reshape(cells, groups, rows, width)[:, :, :shares]]
    ppermute x0 -> x6, waiting for transfers between devices: none -> 33.1 us  [shift(): lax.ppermute(array, 'xg', [(i, (i + by) % groups) for i in range(groups)])]
    unnamed x201 -> x33, local copies, waits for them, and re-layouts: 5.72 us -> 21.1 us
    ppermute x0 -> x6, starting transfers between devices: none -> 10.9 us  [shift(): lax.ppermute(array, 'xg', [(i, (i + by) % groups) for i in range(groups)])]
    gather x8 -> x0, local copies, waits for them, and re-layouts: 7.94 us -> none  [the longest x2 3.12 us: per_device(): got_value[source, :, pair_index]]
  transfers between devices with their start and end apart: 3 -> 8, of which waited for: 0 -> 5; matrix products, arithmetic and copies ran while one was open for 26% -> 2% of each run, Pallas kernels for 0% -> 9%
where the time goes in v1:
time: 120 us; the launch traced here: 119 us
  waiting for transfers between devices  39.9 us (33%)
  Pallas kernels  35.5 us (30%)
  local copies, waits for them, and re-layouts  22.4 us (19%)
  starting transfers between devices  19.6 us (16%)
  between operations  1.6 us (1%)
    ppermute x6, waiting for transfers between devices, shift(): lax.ppermute(array, 'xg', [(i, (i + by) % groups) for i in range(groups)])  33.1 us
    unnamed x33, local copies, waits for them, and re-layouts  21.1 us
    pallas_call x1, Pallas kernels, margins_stage(): pl.pallas_call(functools.partial(margin_kernel, groups, rows, slots, gain...  13.3 us
    ppermute x6, starting transfers between devices, shift(): lax.ppermute(array, 'xg', [(i, (i + by) % groups) for i in range(groups)])  10.9 us
    pallas_call x1, Pallas kernels, sweeps(): pl.pallas_call(functools.partial(sweep_kernel, groups, own), out_shape=(j...  9.14 us
    all_to_all x1, waiting for transfers between devices, per_device(): lax.all_to_all(send, ('atm', 'xg'), split_axis=0, concat_axis=0, tiled=True)  6.84 us
    pallas_call x1, Pallas kernels, bottoms(): pl.pallas_call(functools.partial(bottom_kernel, groups, own, rows), out_s...  5.91 us
    pallas_call x1, Pallas kernels, finish(): pl.pallas_call(functools.partial(finish_kernel, groups, blocks // groups,...  5.64 us
  transfers between devices with their start and end apart: 8, of which 5 were waited for; matrix products, arithmetic and copies ran while one was open for 2% of the time, Pallas kernels for 9%

profile of v1, /device:TPU:0, one launch (start us, length us, event | category | flops | bytes accessed | tf_op | source)
XLA Modules:
  0.0 119.1 jit_solution(12491043068908032324)
XLA Ops:
  0.6 0.0 copy-start.7
  0.6 0.9 copy-done.7
  1.5 0.0 copy-start.8
  1.5 0.9 copy-done.8
  2.4 0.0 copy-start.12
  2.4 0.7 copy-done.12
  3.1 0.5 factors.1
  3.6 5.1 %collective-permute-start.2 = (f32[49,4,128]{2,1,0:T(4,128)S(1)}, f32[49,4,128]{2,1,0:T(4,128)S(1)}, u32[]{:S(2)}, u32[]{:S(2)}) collective-permute-start(f32[49,4,128]{2,1,0:T(4,128)S(1)} %get-tuple-element.11.refs_0_.refs_4_), channel_id=1, source_target_pairs={{0,3},{1,0},{2,1},{3,2},{4,7},{5,4},{6,5},{7,6},{8,11},{9,8},{10,9... | collective-permute-start | bytes 301064 | tf_op jit(solution)/shard_map/ppermute | solution.py:382
  8.7 0.0 collective-permute-start.1
  8.7 1.0 collective-permute-start
  9.7 0.8 copy.18
  10.5 0.1 reshape_squeeze.3
  10.6 1.3 %collective-permute-done.2.refs_3_.refs_7_ = f32[49,4,128]{2,1,0:T(4,128)S(1)} collective-permute-done((f32[49,4,128]{2,1,0:T(4,128)S(1)}, f32[49,4,128]{2,1,0:T(4,128)S(1)}, u32[]{:S(2)}, u32[]{:S(2)}) %collective-permute-start.2) | collective-permute-done | bytes 100384 | tf_op jit(solution)/shard_map/ppermute | solution.py:382
  11.9 5.7 %collective-permute-done.1.refs_2_.refs_6_ = f32[49,4,128]{2,1,0:T(4,128)S(1)} collective-permute-done((f32[49,4,128]{2,1,0:T(4,128)S(1)}, f32[49,4,128]{2,1,0:T(4,128)S(1)}, u32[]{:S(2)}, u32[]{:S(2)}) %collective-permute-start.1) | collective-permute-done | bytes 100384 | tf_op jit(solution)/shard_map/ppermute | solution.py:382
  17.6 0.0 collective-permute-done.refs_1_.refs_5_
  17.6 0.0 copy-start.2
  17.6 2.4 %copy-done.2 = f32[16,48,13,128]{3,1,2,0:T(8,128)S(1)} copy-done((f32[16,48,13,128]{3,1,2,0:T(8,128)S(1)}, f32[16,48,13,128]{3,1,2,0:T(8,128)}, u32[]{:S(2)}) %copy-start.2) | copy-done | bytes 5111832
  20.1 0.0 copy-start.15
  20.1 5.9 %bottoms.1 = f32[32,32,128]{2,1,0:T(8,128)} custom-call(s32[1]{0:T(128)} %bitcast.me_ref, s32[64]{0:T(128)S(1)} %compare_select_fusion.2.place_ref, f32[49,4,128]{2,1,0:T(4,128)S(1)} %get-tuple-element.11.refs_0_.refs_4_, f32[49,4,128]{2,1,0:T(4,128)S(1)} %collective-permute-done.refs_1_.refs_5_, f32[49,4,128]{2,1,0:T(4,128)S(1)} %collective-permute-done.1.refs_2_.refs_6_, ...), custom_call_target="tpu_custom_call" | custom-call | flops 4000000 | bytes 7000000 | tf_op jit(solution)/shard_map/bottoms/pallas_call | solution.py:120
  26.0 4.5 %all-to-all-start = ((f32[32,32,128]{2,1,0:T(8,128)}), f32[32,32,128]{2,1,0:T(8,128)S(1)}, u32[]{:S(2)}, u32[]{:S(2)}) async-start(f32[32,32,128]{2,1,0:T(8,128)} %bottoms.1), calls=%async_computation | async-start | bytes 1048576 | tf_op jit(solution)/shard_map/all_to_all | solution.py:404
  31.2 0.0 copy-done.15
  31.2 0.2 copy.19
  31.4 0.0 copy-start.4
  31.4 2.8 %copy-done.4 = f32[1,96,128,128]{3,2,1,0:T(8,128)S(1)} copy-done((f32[1,96,128,128]{3,2,1,0:T(8,128)S(1)}, f32[1,96,128,128]{3,2,1,0:T(8,128)}, u32[]{:S(2)}) %copy-start.4) | copy-done | bytes 6291480
  34.2 0.0 copy-start.9
  34.2 0.0 copy-start.10
  34.2 0.0 copy-start.11
  34.2 0.0 copy-start.13
  34.2 0.0 copy-start.14
  34.2 1.1 split_weights.1.weight_hbm
  35.3 0.0 copy-start
  35.3 2.6 %copy-done = bf16[96,256,128]{2,1,0:T(8,128)(2,1)} copy-done((bf16[96,256,128]{2,1,0:T(8,128)(2,1)}, bf16[96,256,128]{2,1,0:T(8,128)(2,1)S(1)}, u32[]{:S(2)}) %copy-start) | copy-done | bytes 6291480
  37.9 6.8 %all-to-all-done.got_ref = f32[32,32,128]{2,1,0:T(8,128)S(1)} async-done(((f32[32,32,128]{2,1,0:T(8,128)}), f32[32,32,128]{2,1,0:T(8,128)S(1)}, u32[]{:S(2)}, u32[]{:S(2)}) %all-to-all-start) | async-done | bytes 524320 | tf_op jit(solution)/shard_map/all_to_all | solution.py:404
  44.8 0.0 copy-done.9
  44.8 0.0 copy-done.10
  44.8 0.0 copy-done.11
  44.8 0.0 copy-done.13
  44.8 0.0 copy-done.14
  44.8 0.0 copy-start.1
  44.8 2.8 %copy-done.1 = bf16[96,256,128]{2,1,0:T(8,128)(2,1)S(1)} copy-done((bf16[96,256,128]{2,1,0:T(8,128)(2,1)S(1)}, bf16[96,256,128]{2,1,0:T(8,128)(2,1)}, u32[]{:S(2)}) %copy-start.1) | copy-done | bytes 6291480
  47.6 13.3 %margins.1 = (f32[32,32,128]{2,1,0:T(8,128)}, f32[16,64,128]{2,1,0:T(8,128)S(1)}) custom-call(s32[96]{0:T(128)S(1)} %bitcast.20, s32[96]{0:T(128)S(1)} %bitcast.21, s32[1]{0:T(128)S(6)} %copy.21.count_ref, bf16[96,256,128]{2,1,0:T(8,128)(2,1)S(1)} %copy-done.1, f32[32,32,128]{2,1,0:T(8,128)S(1)} %all-to-all-done.got_ref, f32[16,64,128]{2,1,0:T(8,128)S(1)} %bitcast.16, ...), custom_call_target="tpu_custom_call" | custom-call | flops 800000000 | bytes 8000000 | tf_op jit(solution)/shard_map/margins/pallas_call | solution.py:243
  60.9 4.2 %all-to-all-start.1 = ((f32[32,32,128]{2,1,0:T(8,128)}), f32[32,32,128]{2,1,0:T(8,128)S(1)}, u32[]{:S(2)}, u32[]{:S(2)}) async-start(f32[32,32,128]{2,1,0:T(8,128)} %get-tuple-element.13.refs_9_), calls=%async_computation.1 | async-start | bytes 1048576 | tf_op jit(solution)/shard_map/all_to_all | solution.py:410
  65.1 3.7 %collective-permute-start.5 = (f32[96,4,128]{2,1,0:T(4,128)S(1)}, f32[96,4,128]{2,1,0:T(4,128)S(1)}, u32[]{:S(2)}, u32[]{:S(2)}) collective-permute-start(f32[96,4,128]{2,1,0:T(4,128)S(1)} %get-tuple-element.14.refs_0_), channel_id=1, source_target_pairs={{0,3},{1,0},{2,1},{3,2},{4,7},{5,4},{6,5},{7,6},{8,11},{9,8},{10,9... | collective-permute-start | bytes 589832 | tf_op jit(solution)/shard_map/ppermute | solution.py:382
  68.7 0.0 collective-permute-start.4
  68.7 1.1 collective-permute-start.3
  69.8 1.0 copy.20
  70.8 9.7 %collective-permute-done.5.refs_3_ = f32[96,4,128]{2,1,0:T(4,128)S(1)} collective-permute-done((f32[96,4,128]{2,1,0:T(4,128)S(1)}, f32[96,4,128]{2,1,0:T(4,128)S(1)}, u32[]{:S(2)}, u32[]{:S(2)}) %collective-permute-start.5) | collective-permute-done | bytes 196640 | tf_op jit(solution)/shard_map/ppermute | solution.py:382
  80.5 16.4 %collective-permute-done.4.refs_2_ = f32[96,4,128]{2,1,0:T(4,128)S(1)} collective-permute-done((f32[96,4,128]{2,1,0:T(4,128)S(1)}, f32[96,4,128]{2,1,0:T(4,128)S(1)}, u32[]{:S(2)}, u32[]{:S(2)}) %collective-permute-start.4) | collective-permute-done | bytes 196640 | tf_op jit(solution)/shard_map/ppermute | solution.py:382
  96.9 0.0 collective-permute-done.3.refs_1_
  96.9 0.0 copy-start.3
  96.9 2.4 %copy-done.3 = f32[16,48,13,128]{3,1,2,0:T(8,128)S(1)} copy-done((f32[16,48,13,128]{3,1,2,0:T(8,128)S(1)}, f32[16,48,13,128]{3,1,2,0:T(8,128)}, u32[]{:S(2)}) %copy-start.3) | copy-done | bytes 5111832
  99.3 9.1 %sweeps.1 = (f32[13,48,16,128]{3,2,1,0:T(8,128)S(1)}, f32[48,16,128]{2,1,0:T(8,128)S(1)}) custom-call(s32[1]{0:T(128)} %bitcast.me_ref, f32[96,4,128]{2,1,0:T(4,128)S(1)} %get-tuple-element.14.refs_0_, f32[96,4,128]{2,1,0:T(4,128)S(1)} %collective-permute-done.3.refs_1_, f32[96,4,128]{2,1,0:T(4,128)S(1)} %collective-permute-done.4.refs_2_, ...), custom_call_target="tpu_custom_call" | custom-call | flops 8000000 | bytes 12000000 | tf_op jit(solution)/shard_map/sweeps/pallas_call | solution.py:301
  108.5 0.0 copy-start.5
  108.5 2.3 %copy-done.5 = f32[13,48,16,128]{3,2,1,0:T(8,128)} copy-done((f32[13,48,16,128]{3,2,1,0:T(8,128)}, f32[13,48,16,128]{3,2,1,0:T(8,128)S(1)}, u32[]{:S(2)}) %copy-start.5) | copy-done | bytes 5111832
  110.8 0.0 all-to-all-done.1.answer_ref
  110.8 0.0 copy-start.6
  110.8 2.4 %copy-done.6 = f32[13,48,16,128]{3,2,1,0:T(8,128)S(1)} copy-done((f32[13,48,16,128]{3,2,1,0:T(8,128)S(1)}, f32[13,48,16,128]{3,2,1,0:T(8,128)}, u32[]{:S(2)}) %copy-start.6) | copy-done | bytes 5111832
  113.3 5.6 %finish.1 = f32[16,13,48,128]{3,2,1,0:T(8,128)} custom-call(s32[1]{0:T(128)} %bitcast.me_ref, s32[64]{0:T(128)S(1)} %compare_select_fusion.2.place_ref, f32[32,32,128]{2,1,0:T(8,128)S(1)} %all-to-all-done.1.answer_ref, f32[13,48,16,128]{3,2,1,0:T(8,128)S(1)} %copy-done.6, f32[48,16,128]{2,1,0:T(8,128)S(1)} %get-tuple-element.16.reach_ref), custom_call_target="tpu_custom_call" | custom-call | flops 4000000 | bytes 12000000 | tf_op jit(solution)/shard_map/finish/pallas_call | solution.py:352
  (2 shorter events, 0.1 us)
Async XLA Ops:
  0.6 0.9 copy-start.7
  1.5 0.9 copy-start.8
  2.4 0.7 copy-start.12
  3.6 8.4 %collective-permute-start.2 = (f32[49,4,128]{2,1,0:T(4,128)S(1)}, f32[49,4,128]{2,1,0:T(4,128)S(1)}, u32[]{:S(2)}, u32[]{:S(2)}) collective-permute-start(f32[49,4,128]{2,1,0:T(4,128)S(1)} %get-tuple-element.11.refs_0_.refs_4_), channel_id=1, source_target_pairs={{0,3},{1,0},{2,1},{3,2},{4,7},{5,4},{6,5},{7,6},{8,11},{9,8},{10,9... | collective-permute-start | bytes 301064 | tf_op jit(solution)/shard_map/ppermute | solution.py:382
  8.7 8.9 %collective-permute-start.1 = (f32[49,4,128]{2,1,0:T(4,128)S(1)}, f32[49,4,128]{2,1,0:T(4,128)S(1)}, u32[]{:S(2)}, u32[]{:S(2)}) collective-permute-start(f32[49,4,128]{2,1,0:T(4,128)S(1)} %get-tuple-element.11.refs_0_.refs_4_), channel_id=1, source_target_pairs={{0,2},{1,3},{2,0},{3,1},{4,6},{5,7},{6,4},{7,5},{8,10},{9,11},{10,... | collective-permute-start | bytes 301064 | tf_op jit(solution)/shard_map/ppermute | solution.py:382
  8.7 8.9 %collective-permute-start = (f32[49,4,128]{2,1,0:T(4,128)S(1)}, f32[49,4,128]{2,1,0:T(4,128)S(1)}, u32[]{:S(2)}, u32[]{:S(2)}) collective-permute-start(f32[49,4,128]{2,1,0:T(4,128)S(1)} %get-tuple-element.11.refs_0_.refs_4_), channel_id=1, source_target_pairs={{0,1},{1,2},{2,3},{3,0},{4,5},{5,6},{6,7},{7,4},{8,9},{9,10},{10,1... | collective-permute-start | bytes 301064 | tf_op jit(solution)/shard_map/ppermute | solution.py:382
  17.6 2.5 %copy-start.2 = (f32[16,48,13,128]{3,1,2,0:T(8,128)S(1)}, f32[16,48,13,128]{3,1,2,0:T(8,128)}, u32[]{:S(2)}) copy-start(f32[16,48,13,128]{3,1,2,0:T(8,128)} %param.13) | copy-start | bytes 15335428
  20.1 11.1 %copy-start.15 = (f32[16,52,128]{2,0,1:T(8,128)S(1)}, f32[16,52,128]{2,0,1:T(8,128)}, u32[]{:S(2)}) copy-start(f32[16,52,128]{2,0,1:T(8,128)} %param.22) | copy-start | bytes 1277956
  26.0 18.8 %all-to-all-start = ((f32[32,32,128]{2,1,0:T(8,128)}), f32[32,32,128]{2,1,0:T(8,128)S(1)}, u32[]{:S(2)}, u32[]{:S(2)}) async-start(f32[32,32,128]{2,1,0:T(8,128)} %bottoms.1), calls=%async_computation | async-start | bytes 1048576 | tf_op jit(solution)/shard_map/all_to_all | solution.py:404
  31.4 2.8 %copy-start.4 = (f32[1,96,128,128]{3,2,1,0:T(8,128)S(1)}, f32[1,96,128,128]{3,2,1,0:T(8,128)}, u32[]{:S(2)}) copy-start(f32[1,96,128,128]{3,2,1,0:T(8,128)} %param.21) | copy-start | bytes 18874372
  34.2 10.6 %copy-start.9 = (f32[16,128]{1,0:T(8,128)S(1)}, f32[16,128]{1,0:T(8,128)}, u32[]{:S(2)}) copy-start(f32[16,128]{1,0:T(8,128)} %coef_ref.1) | copy-start | bytes 24580
  34.2 10.6 %copy-start.10 = (s32[16,128]{1,0:T(8,128)S(1)}, s32[16,128]{1,0:T(8,128)}, u32[]{:S(2)}) copy-start(s32[16,128]{1,0:T(8,128)} %mask_ref.1) | copy-start | bytes 24580
  34.2 10.6 %copy-start.11 = (f32[16,128]{1,0:T(8,128)S(1)}, f32[16,128]{1,0:T(8,128)}, u32[]{:S(2)}) copy-start(f32[16,128]{1,0:T(8,128)} %land_ref.1) | copy-start | bytes 24580
  34.2 10.6 %copy-start.13 = (s32[1,96]{1,0:T(1,128)S(1)}, s32[1,96]{1,0:T(1,128)}, u32[]{:S(2)}) copy-start(s32[1,96]{1,0:T(1,128)} %param.18) | copy-start | bytes 1156
  34.2 10.6 %copy-start.14 = (s32[1,96]{1,0:T(1,128)S(1)}, s32[1,96]{1,0:T(1,128)}, u32[]{:S(2)}) copy-start(s32[1,96]{1,0:T(1,128)} %param.19) | copy-start | bytes 1156
  35.3 2.6 %copy-start = (bf16[96,256,128]{2,1,0:T(8,128)(2,1)}, bf16[96,256,128]{2,1,0:T(8,128)(2,1)S(1)}, u32[]{:S(2)}) copy-start(bf16[96,256,128]{2,1,0:T(8,128)(2,1)S(1)} %split_weights.1.weight_hbm) | copy-start | bytes 18874372
  44.8 2.8 %copy-start.1 = (bf16[96,256,128]{2,1,0:T(8,128)(2,1)S(1)}, bf16[96,256,128]{2,1,0:T(8,128)(2,1)}, u32[]{:S(2)}) copy-start(bf16[96,256,128]{2,1,0:T(8,128)(2,1)} %copy-done) | copy-start | bytes 18874372
  60.9 49.9 %all-to-all-start.1 = ((f32[32,32,128]{2,1,0:T(8,128)}), f32[32,32,128]{2,1,0:T(8,128)S(1)}, u32[]{:S(2)}, u32[]{:S(2)}) async-start(f32[32,32,128]{2,1,0:T(8,128)} %get-tuple-element.13.refs_9_), calls=%async_computation.1 | async-start | bytes 1048576 | tf_op jit(solution)/shard_map/all_to_all | solution.py:410
  65.1 15.5 %collective-permute-start.5 = (f32[96,4,128]{2,1,0:T(4,128)S(1)}, f32[96,4,128]{2,1,0:T(4,128)S(1)}, u32[]{:S(2)}, u32[]{:S(2)}) collective-permute-start(f32[96,4,128]{2,1,0:T(4,128)S(1)} %get-tuple-element.14.refs_0_), channel_id=1, source_target_pairs={{0,3},{1,0},{2,1},{3,2},{4,7},{5,4},{6,5},{7,6},{8,11},{9,8},{10,9... | collective-permute-start | bytes 589832 | tf_op jit(solution)/shard_map/ppermute | solution.py:382
  68.7 28.1 %collective-permute-start.4 = (f32[96,4,128]{2,1,0:T(4,128)S(1)}, f32[96,4,128]{2,1,0:T(4,128)S(1)}, u32[]{:S(2)}, u32[]{:S(2)}) collective-permute-start(f32[96,4,128]{2,1,0:T(4,128)S(1)} %get-tuple-element.14.refs_0_), channel_id=1, source_target_pairs={{0,2},{1,3},{2,0},{3,1},{4,6},{5,7},{6,4},{7,5},{8,10},{9,11},{10,... | collective-permute-start | bytes 589832 | tf_op jit(solution)/shard_map/ppermute | solution.py:382
  68.7 28.1 %collective-permute-start.3 = (f32[96,4,128]{2,1,0:T(4,128)S(1)}, f32[96,4,128]{2,1,0:T(4,128)S(1)}, u32[]{:S(2)}, u32[]{:S(2)}) collective-permute-start(f32[96,4,128]{2,1,0:T(4,128)S(1)} %get-tuple-element.14.refs_0_), channel_id=1, source_target_pairs={{0,1},{1,2},{2,3},{3,0},{4,5},{5,6},{6,7},{7,4},{8,9},{9,10},{10,1... | collective-permute-start | bytes 589832 | tf_op jit(solution)/shard_map/ppermute | solution.py:382
  96.9 2.5 %copy-start.3 = (f32[16,48,13,128]{3,1,2,0:T(8,128)S(1)}, f32[16,48,13,128]{3,1,2,0:T(8,128)}, u32[]{:S(2)}) copy-start(f32[16,48,13,128]{3,1,2,0:T(8,128)} %param.13) | copy-start | bytes 15335428
  108.5 2.3 %copy-start.5 = (f32[13,48,16,128]{3,2,1,0:T(8,128)}, f32[13,48,16,128]{3,2,1,0:T(8,128)S(1)}, u32[]{:S(2)}) copy-start(f32[13,48,16,128]{3,2,1,0:T(8,128)S(1)} %get-tuple-element.15.still_ref) | copy-start | bytes 15335428
  110.8 2.5 %copy-start.6 = (f32[13,48,16,128]{3,2,1,0:T(8,128)S(1)}, f32[13,48,16,128]{3,2,1,0:T(8,128)}, u32[]{:S(2)}) copy-start(f32[13,48,16,128]{3,2,1,0:T(8,128)} %copy-done.5) | copy-start | bytes 15335428

commit v2 on v1

--- a/solution.py
+++ b/solution.py
@@ -11,6 +11,8 @@
 F32 = jnp.float32
 BF16 = jnp.bfloat16
 ROWS = 8
+MOST = 67043328
+ROOMY = 50 << 20
 
 
 def vmem():
@@ -22,10 +24,10 @@
 
 
 def hbm():
-    return pl.BlockSpec(memory_space=pl.ANY)
-
-
-def params(limit=None):
+    return pl.BlockSpec(memory_space=pltpu.HBM)
+
+
+def params(limit):
     return pltpu.CompilerParams(vmem_limit_bytes=limit)
 
 
@@ -39,7 +41,18 @@
     return high, low
 
 
-def factor_kernel(levels, own, upper_ref, lower_ref, gain_ref, first_ref, second_ref, inverse_ref):
+def factor_kernel(levels, own, upper_hbm, lower_hbm, gain_hbm, first_ref, second_ref,
+                  upper_ref, lower_ref, gain_ref, inverse_ref, sem):
+    copies = [
+        pltpu.make_async_copy(source, target, sem.at[i])
+        for i, (source, target) in enumerate(
+            ((upper_hbm, upper_ref), (lower_hbm, lower_ref), (gain_hbm, gain_ref))
+        )
+    ]
+    for copy in copies:
+        copy.start()
+    for copy in copies:
+        copy.wait()
     carried = jnp.zeros(gain_ref.shape, F32)
     for k in range(levels):
         from_above = upper_ref[pl.ds(k, own, stride=levels), :] if k > 0 else jnp.zeros_like(carried)
@@ -66,10 +79,16 @@
             jax.ShapeDtypeStruct((levels + 1, own, width), F32),
             jax.ShapeDtypeStruct((2 * levels, own, width), F32),
         ),
-        in_specs=[vmem()] * 3,
+        in_specs=[hbm()] * 3,
         out_specs=(vmem(), vmem()),
-        scratch_shapes=[pltpu.VMEM((levels, own, width), F32)],
-        compiler_params=params(8 << 20),
+        scratch_shapes=[
+            pltpu.VMEM((own * levels, width), F32),
+            pltpu.VMEM((own * levels, width), F32),
+            pltpu.VMEM((own, width), F32),
+            pltpu.VMEM((levels, own, width), F32),
+            pltpu.SemaphoreType.DMA((3,)),
+        ],
+        compiler_params=params(MOST),
         cost_estimate=pl.CostEstimate(flops=1000000, bytes_accessed=400000, transcendentals=30000),
         name="factors",
     )(upper.reshape(own * levels, width), lower.reshape(own * levels, width), surface_gain)
@@ -87,15 +106,19 @@
 
 
 def bottom_kernel(groups, own, rows, me_ref, place_ref, *refs):
-    parts, fields_ref, send_ref, held_ref, weight_ref, value_ref, sem = (
+    parts, fields_ref, send_ref, held_ref, weight_ref, value_ref, own_ref, sem, own_sem = (
         refs[:groups], *refs[groups:]
     )
+    fetch = pltpu.make_async_copy(parts[0], own_ref, own_sem)
+    fetch.start()
     fetch_fields(me_ref[0], groups, own, fields_ref, held_ref, sem)
     blocks = groups * own
     levels = held_ref.shape[1]
     shares = held_ref.shape[0]
-    for q in range(groups):
+    for q in range(1, groups):
         weight_ref[:, q * own:(q + 1) * own, :] = parts[q][...]
+    fetch.wait()
+    weight_ref[:, :own, :] = own_ref[...]
     value_ref[...] = jnp.zeros_like(value_ref)
     value_ref[pl.ds(shares, blocks, stride=rows), :] = weight_ref[levels]
     for f in range(shares):
@@ -120,15 +143,17 @@
     return pl.pallas_call(
         functools.partial(bottom_kernel, groups, own, rows),
         out_shape=jax.ShapeDtypeStruct((owners, slots * rows, width), F32),
-        in_specs=[smem(), smem()] + [vmem()] * groups + [hbm()],
+        in_specs=[smem(), smem(), hbm()] + [vmem()] * (groups - 1) + [hbm()],
         out_specs=vmem(),
         scratch_shapes=[
             pltpu.VMEM((shares, levels, blocks, width), F32),
             pltpu.VMEM((levels + 1, blocks, width), F32),
             pltpu.VMEM(((blocks + 1) * rows, width), F32),
+            pltpu.VMEM((levels + 1, own, width), F32),
             pltpu.SemaphoreType.DMA((shares,)),
+            pltpu.SemaphoreType.DMA(()),
         ],
-        compiler_params=params(16 << 20),
+        compiler_params=params(ROOMY),
         cost_estimate=pl.CostEstimate(flops=4000000, bytes_accessed=7000000, transcendentals=0),
         name="bottoms",
     )(me, place, *parts, fields)
@@ -150,7 +175,7 @@
         out_shape=jax.ShapeDtypeStruct((margins, 2 * cells, columns), BF16),
         in_specs=[pl.BlockSpec((step, cells, columns), lambda i: (i, 0, 0))],
         out_specs=pl.BlockSpec((step, 2 * cells, columns), lambda i: (i, 0, 0)),
-        compiler_params=params(8 << 20),
+        compiler_params=params(ROOMY),
         cost_estimate=pl.CostEstimate(flops=5000000, bytes_accessed=13000000, transcendentals=0),
         name="split_weights",
     )(weight)
@@ -234,8 +259,7 @@
 
 
 def margins_stage(slot, block, count, weights, got, surface, coef, mask, land, groups, rows, slots, gain_row):
-    margins, twice, columns = weights.shape
-    owners, slot_rows, width = got.shape
+    owners, _, width = got.shape
     cells, tall, _ = surface.shape
     sources = owners // groups
     unroll = 4
@@ -256,73 +280,27 @@
             pltpu.VMEM((sources * slots + 1, tall, width), F32),
             pltpu.SemaphoreType.DMA((chunks,)),
         ],
-        compiler_params=params(24 << 20),
+        compiler_params=params(ROOMY),
         cost_estimate=pl.CostEstimate(flops=800000000, bytes_accessed=8000000, transcendentals=0),
         name="margins",
     )(slot, block, count, weights, got, surface, coef, mask, land)
 
 
-def sweep_kernel(groups, own, me_ref, *refs):
-    parts, gains, fields_ref, after_ref, still_ref, reach_ref, held_ref, factor_ref, sem, out_sem = (
+def finish_kernel(groups, own, rows, me_ref, place_ref, answer_ref, *refs):
+    parts, gains, fields_ref, out_ref, held_ref, factor_ref, gain_ref, flux_ref, sem, out_sem = (
         refs[:groups], refs[groups:2 * groups], *refs[2 * groups:]
     )
-    fetch_fields(me_ref[0], groups, own, fields_ref, held_ref, sem)
+    me = me_ref[0]
+    fetch_fields(me, groups, own, fields_ref, held_ref, sem)
     shares, levels, blocks, width = held_ref.shape
     for q in range(groups):
         factor_ref[levels:, q * own:(q + 1) * own, :] = parts[q][...]
-        reach_ref[levels - 1, q * own:(q + 1) * own, :] = gains[q][levels]
-    reach = reach_ref[levels - 1]
-    for k in range(levels - 1, -1, -1):
+        gain_ref[q * own:(q + 1) * own, :] = gains[q][levels]
+    above = jnp.zeros((blocks, width), F32)
+    for k in range(levels):
         carry = factor_ref[2 * levels + k]
-        above = factor_ref[2 * levels + k - 1] if k > 0 else jnp.zeros_like(carry)
         factor_ref[k] = 1.0 - carry - factor_ref[levels + k] * (1.0 - above)
-        if k < levels - 1:
-            reach = carry * reach
-            reach_ref[k] = reach
-    for f in range(shares):
-        pltpu.make_async_copy(held_ref.at[f], held_ref.at[f], sem.at[f]).wait()
-        partial = factor_ref[0] * held_ref[f, 0]
-        held_ref[f, 0] = partial
-        for k in range(1, levels):
-            partial = factor_ref[k] * held_ref[f, k] + factor_ref[levels + k] * partial
-            held_ref[f, k] = partial
-        for k in range(levels - 2, -1, -1):
-            partial = held_ref[f, k] + factor_ref[2 * levels + k] * partial
-            held_ref[f, k] = partial
-        pltpu.make_async_copy(held_ref.at[f], still_ref.at[f], out_sem.at[f]).start()
-    for f in range(shares):
-        pltpu.make_async_copy(held_ref.at[f], still_ref.at[f], out_sem.at[f]).wait()
-
-
-def sweeps(me, parts, gains, fields, after):
-    blocks, shares, levels, width = fields.shape
-    groups = len(parts)
-    own = blocks // groups
-    return pl.pallas_call(
-        functools.partial(sweep_kernel, groups, own),
-        out_shape=(
-            jax.ShapeDtypeStruct((shares, levels, blocks, width), F32),
-            jax.ShapeDtypeStruct((levels, blocks, width), F32),
-        ),
-        in_specs=[smem()] + [vmem()] * (2 * groups) + [hbm(), hbm()],
-        out_specs=(hbm(), vmem()),
-        scratch_shapes=[
-            pltpu.VMEM((shares, levels, blocks, width), F32),
-            pltpu.VMEM((3 * levels, blocks, width), F32),
-            pltpu.SemaphoreType.DMA((shares,)),
-            pltpu.SemaphoreType.DMA((shares,)),
-        ],
-        compiler_params=params(16 << 20),
-        cost_estimate=pl.CostEstimate(flops=8000000, bytes_accessed=12000000, transcendentals=0),
-        name="sweeps",
-    )(me, *parts, *gains, fields, after)
-
-
-def finish_kernel(groups, own, rows, me_ref, place_ref, answer_ref, still_ref, reach_ref, out_ref,
-                  held_ref, flux_ref, sem, out_sem):
-    shares, levels, blocks, width = held_ref.shape
-    for f in range(shares):
-        pltpu.make_async_copy(still_ref.at[f], held_ref.at[f], sem.at[f]).start()
+        above = carry
     flux_ref[...] = jnp.zeros_like(flux_ref)
     owners, slot_rows = answer_ref.shape[:2]
     slots = slot_rows // rows
@@ -330,13 +308,20 @@
         for p in range(slots):
             start = pl.multiple_of(place_ref[d * slots + p] * rows, rows)
             flux_ref[pl.ds(start, rows), :] += answer_ref[d, p * rows:(p + 1) * rows, :]
-    me = me_ref[0]
-    copies = []
     for f in range(shares):
         flux = flux_ref[pl.ds(f, blocks, stride=rows), :]
-        pltpu.make_async_copy(still_ref.at[f], held_ref.at[f], sem.at[f]).wait()
-        for k in range(levels):
-            held_ref[f, k] = held_ref[f, k] + reach_ref[k] * flux
+        pltpu.make_async_copy(held_ref.at[f], held_ref.at[f], sem.at[f]).wait()
+        state = factor_ref[0] * held_ref[f, 0]
+        held_ref[f, 0] = state
+        for k in range(1, levels):
+            state = factor_ref[k] * held_ref[f, k] + factor_ref[levels + k] * state
+            if k < levels - 1:
+                held_ref[f, k] = state
+        state = state + gain_ref[...] * flux
+        held_ref[f, levels - 1] = state
+        for k in range(levels - 2, -1, -1):
+            state = held_ref[f, k] + factor_ref[2 * levels + k] * state
+            held_ref[f, k] = state
         for q in range(groups):
             base = lax.rem(me - q + groups, groups) * own
             for i in range(own):
@@ -347,23 +332,26 @@
         pltpu.make_async_copy(held_ref.at[f], held_ref.at[f], out_sem.at[f]).wait()
 
 
-def finish(me, place, answer, still, reach, groups, rows):
-    shares, levels, blocks, width = still.shape
+def finish(me, place, answer, parts, gains, fields, rows):
+    blocks, shares, levels, width = fields.shape
+    groups = len(parts)
     return pl.pallas_call(
         functools.partial(finish_kernel, groups, blocks // groups, rows),
         out_shape=jax.ShapeDtypeStruct((blocks, shares, levels, width), F32),
-        in_specs=[smem(), smem(), vmem(), hbm(), vmem()],
+        in_specs=[smem(), smem(), vmem()] + [vmem()] * (2 * groups) + [hbm()],
         out_specs=hbm(),
         scratch_shapes=[
             pltpu.VMEM((shares, levels, blocks, width), F32),
+            pltpu.VMEM((3 * levels, blocks, width), F32),
+            pltpu.VMEM((blocks, width), F32),
             pltpu.VMEM(((blocks + 1) * rows, width), F32),
             pltpu.SemaphoreType.DMA((shares,)),
             pltpu.SemaphoreType.DMA((shares,)),
         ],
-        compiler_params=params(16 << 20),
-        cost_estimate=pl.CostEstimate(flops=4000000, bytes_accessed=12000000, transcendentals=0),
+        compiler_params=params(ROOMY),
+        cost_estimate=pl.CostEstimate(flops=8000000, bytes_accessed=12000000, transcendentals=0),
         name="finish",
-    )(me, place, answer, still, reach)
+    )(me, place, answer, *parts, *gains, fields)
 
 
 def per_device(
@@ -372,7 +360,7 @@
 ):
     groups = lax.axis_size("xg")
     me = lax.axis_index("xg").astype(jnp.int32)
-    blocks, levels, shares, width = fields_now.shape
+    blocks, _, shares, width = fields_now.shape
     own = blocks // groups
     rows = round_up(shares + 1, ROWS)
     owners, slots = route.shape[1:]
@@ -400,7 +388,6 @@
         ((0, 0), (0, 0), (0, rows - shares), (0, 0)),
     ).reshape(cells, groups * rows, width)
     send = bottoms(me, place, firsts, fields, owners, slots, rows)
-    second, send = lax.optimization_barrier((second, send))
     got = lax.all_to_all(send, ("atm", "xg"), split_axis=0, concat_axis=0, tiled=True)
     seconds = shared(second)
     reply, flux = margins_stage(
@@ -408,11 +395,10 @@
         exchange_coef, land_mask, land_gain, groups, rows, slots, shares,
     )
     answer = lax.all_to_all(reply, ("atm", "xg"), split_axis=0, concat_axis=0, tiled=True)
-    still, reach = sweeps(me, seconds, firsts, fields, reply)
     surface_flux = flux.reshape(cells, groups, rows, width)[:, :, :shares].reshape(
         cells, groups * shares, width
     )
-    out = finish(me, place, answer, still, reach, groups, rows)
+    out = finish(me, place, answer, seconds, firsts, fields, rows)
     return out.transpose(0, 2, 1, 3), surface_flux
 
 

time: 120 us -> 94 us (0.78)
  local copies, waits for them, and re-layouts: 22.4 us -> 3 us
  waiting for transfers between devices: 39.9 us -> 30 us
  starting transfers between devices: 19.6 us -> 22.9 us
    unnamed x33 -> x19, local copies, waits for them, and re-layouts: 21.1 us -> 1.7 us
    pallas_call x1 -> x0, Pallas kernels: 9.14 us -> none  [sweeps(): pl.pallas_call(functools.partial(sweep_kernel, groups, own), out_shape=(j...]
    pallas_call x1, Pallas kernels: 1.07 us -> 9.49 us  [split_weights(): pl.pallas_call(split_kernel, grid=(margins // step,), out_shape=jax.Shape...]
    ppermute x6, waiting for transfers between devices: 33.1 us -> 26.2 us  [shift(): lax.ppermute(array, 'xg', [(i, (i + by) % groups) for i in range(groups)])]
    all_to_all x1, waiting for transfers between devices: 6.84 us -> 3.82 us  [per_device(): lax.all_to_all(send, ('atm', 'xg'), split_axis=0, concat_axis=0, tiled=True)]
    ppermute x6, starting transfers between devices: 10.9 us -> 12.7 us  [shift(): lax.ppermute(array, 'xg', [(i, (i + by) % groups) for i in range(groups)])]
    pallas_call x1, Pallas kernels: 5.91 us -> 4.18 us  [bottoms(): pl.pallas_call(functools.partial(bottom_kernel, groups, own, rows), out_s...]
    pallas_call x1, Pallas kernels: 0.48 us -> 2.11 us  [factors(): pl.pallas_call(functools.partial(factor_kernel, levels, own), out_shape=(...]
  transfers between devices with their start and end apart: 8 -> 8, of which waited for: 5 -> 5; matrix products, arithmetic and copies ran while one was open for 2% -> 2% of each run, Pallas kernels for 9% -> 10%
where the time goes in v2:
time: 94 us; the launch traced here: 92.2 us
  Pallas kernels  34.9 us (37%)
  waiting for transfers between devices  30 us (32%)
  starting transfers between devices  22.9 us (24%)
  local copies, waits for them, and re-layouts  3 us (3%)
  between operations  1.43 us (2%)
    ppermute x6, waiting for transfers between devices, shift(): lax.ppermute(array, 'xg', [(i, (i + by) % groups) for i in range(groups)])  26.2 us
    pallas_call x1, Pallas kernels, margins_stage(): pl.pallas_call(functools.partial(margin_kernel, groups, rows, slots, gain...  13.9 us
    ppermute x6, starting transfers between devices, shift(): lax.ppermute(array, 'xg', [(i, (i + by) % groups) for i in range(groups)])  12.7 us
    pallas_call x1, Pallas kernels, split_weights(): pl.pallas_call(split_kernel, grid=(margins // step,), out_shape=jax.Shape...  9.49 us
    all_to_all x1, starting transfers between devices, per_device(): lax.all_to_all(send, ('atm', 'xg'), split_axis=0, concat_axis=0, tiled=True)  5.91 us
    pallas_call x1, Pallas kernels, finish(): pl.pallas_call(functools.partial(finish_kernel, groups, blocks // groups,...  5.23 us
    all_to_all x1, starting transfers between devices, per_device(): lax.all_to_all(reply, ('atm', 'xg'), split_axis=0, concat_axis=0, tiled=T...  4.26 us
    pallas_call x1, Pallas kernels, bottoms(): pl.pallas_call(functools.partial(bottom_kernel, groups, own, rows), out_s...  4.18 us
  transfers between devices with their start and end apart: 8, of which 5 were waited for; matrix products, arithmetic and copies ran while one was open for 2% of the time, Pallas kernels for 10%

profile of v2, /device:TPU:0, one launch (start us, length us, event | category | flops | bytes accessed | tf_op | source)
XLA Modules:
  0.0 92.2 jit_solution(9067774993476340552)
XLA Ops:
  0.6 2.1 %factors.1 = (f32[49,4,128]{2,1,0:T(4,128)}, f32[96,4,128]{2,1,0:T(4,128)}) custom-call(f32[192,128]{1,0:T(8,128)} %bitcast.23, f32[192,128]{1,0:T(8,128)} %bitcast.24, f32[4,128]{1,0:T(4,128)} %gain_hbm.1), custom_call_target="tpu_custom_call" | custom-call | flops 1000000 | bytes 400000 | tf_op jit(solution)/shard_map/factors/pallas_call | solution.py:76
  2.7 3.1 %collective-permute-start = (f32[49,4,128]{2,1,0:T(4,128)}, f32[49,4,128]{2,1,0:T(4,128)S(1)}, u32[]{:S(2)}, u32[]{:S(2)}) collective-permute-start(f32[49,4,128]{2,1,0:T(4,128)} %get-tuple-element.6.refs_0_.refs_4_), channel_id=1, source_target_pairs={{0,1},{1,2},{2,3},{3,0},{4,5},{5,6},{6,7},{7,4},{8,9},{9,10},{10,1... | collective-permute-start | bytes 301064 | tf_op jit(solution)/shard_map/ppermute | solution.py:370
  5.9 2.6 %collective-permute-start.1 = (f32[49,4,128]{2,1,0:T(4,128)}, f32[49,4,128]{2,1,0:T(4,128)S(1)}, u32[]{:S(2)}, u32[]{:S(2)}) collective-permute-start(f32[49,4,128]{2,1,0:T(4,128)} %get-tuple-element.6.refs_0_.refs_4_), channel_id=1, source_target_pairs={{0,2},{1,3},{2,0},{3,1},{4,6},{5,7},{6,4},{7,5},{8,10},{9,11},{10,... | collective-permute-start | bytes 301064 | tf_op jit(solution)/shard_map/ppermute | solution.py:370
  8.4 1.3 %collective-permute-start.2 = (f32[49,4,128]{2,1,0:T(4,128)}, f32[49,4,128]{2,1,0:T(4,128)S(1)}, u32[]{:S(2)}, u32[]{:S(2)}) collective-permute-start(f32[49,4,128]{2,1,0:T(4,128)} %get-tuple-element.6.refs_0_.refs_4_), channel_id=1, source_target_pairs={{0,3},{1,0},{2,1},{3,2},{4,7},{5,4},{6,5},{7,6},{8,11},{9,8},{10,9... | collective-permute-start | bytes 301064 | tf_op jit(solution)/shard_map/ppermute | solution.py:370
  9.8 0.8 copy.18
  10.6 0.1 reshape_squeeze.3
  10.7 1.1 %collective-permute-done.refs_1_.refs_5_ = f32[49,4,128]{2,1,0:T(4,128)S(1)} collective-permute-done((f32[49,4,128]{2,1,0:T(4,128)}, f32[49,4,128]{2,1,0:T(4,128)S(1)}, u32[]{:S(2)}, u32[]{:S(2)}) %collective-permute-start) | collective-permute-done | bytes 100384 | tf_op jit(solution)/shard_map/ppermute | solution.py:370
  11.8 3.5 %collective-permute-done.1.refs_2_.refs_6_ = f32[49,4,128]{2,1,0:T(4,128)S(1)} collective-permute-done((f32[49,4,128]{2,1,0:T(4,128)}, f32[49,4,128]{2,1,0:T(4,128)S(1)}, u32[]{:S(2)}, u32[]{:S(2)}) %collective-permute-start.1) | collective-permute-done | bytes 100384 | tf_op jit(solution)/shard_map/ppermute | solution.py:370
  15.4 0.0 collective-permute-done.2.refs_3_.refs_7_
  15.4 0.0 copy-start
  15.4 0.9 copy-done
  16.3 0.0 copy-start.8
  16.3 4.2 %bottoms.1 = f32[32,32,128]{2,1,0:T(8,128)} custom-call(s32[1]{0:T(128)} %bitcast.me_ref, s32[64]{0:T(128)S(1)} %compare_select_fusion.2.place_ref, f32[49,4,128]{2,1,0:T(4,128)S(1)} %copy-done, f32[49,4,128]{2,1,0:T(4,128)S(1)} %collective-permute-done.refs_1_.refs_5_, f32[49,4,128]{2,1,0:T(4,128)S(1)} %collective-permute-done.1.refs_2_.refs_6_, ...), custom_call_target="tpu_custom_call" | custom-call | flops 4000000 | bytes 7000000 | tf_op jit(solution)/shard_map/bottoms/pallas_call | solution.py:143
  20.5 5.9 %all-to-all-start = ((f32[32,32,128]{2,1,0:T(8,128)}), f32[32,32,128]{2,1,0:T(8,128)S(1)}, u32[]{:S(2)}, u32[]{:S(2)}) async-start(f32[32,32,128]{2,1,0:T(8,128)} %bottoms.1), calls=%async_computation | async-start | bytes 1048576 | tf_op jit(solution)/shard_map/all_to_all | solution.py:391
  26.4 0.0 copy-done.8
  26.4 0.2 copy.19
  27.2 0.0 copy-start.3
  27.3 0.0 copy-start.4
  27.3 0.0 copy-start.5
  27.3 0.0 copy-start.6
  27.3 0.0 copy-start.7
  27.3 9.5 %split_weights.1.weight_hbm = bf16[96,256,128]{2,1,0:T(8,128)(2,1)} custom-call(f32[96,128,128]{2,1,0:T(8,128)} %bitcast.19), custom_call_target="tpu_custom_call" | custom-call | flops 5000000 | bytes 13000000 | tf_op jit(solution)/shard_map/split_weights/pallas_call | solution.py:172
  36.8 0.0 copy-start.2
  36.8 0.0 copy-start.1
  36.8 3.8 %all-to-all-done.got_ref = f32[32,32,128]{2,1,0:T(8,128)S(1)} async-done(((f32[32,32,128]{2,1,0:T(8,128)}), f32[32,32,128]{2,1,0:T(8,128)S(1)}, u32[]{:S(2)}, u32[]{:S(2)}) %all-to-all-start) | async-done | bytes 524320 | tf_op jit(solution)/shard_map/all_to_all | solution.py:391
  40.6 0.0 copy-done.3
  40.6 0.0 copy-done.4
  40.6 0.0 copy-done.5
  40.6 0.0 copy-done.6
  40.6 0.0 copy-done.7
  40.6 13.9 %margins.1 = (f32[32,32,128]{2,1,0:T(8,128)}, f32[16,64,128]{2,1,0:T(8,128)S(1)}) custom-call(s32[96]{0:T(128)S(1)} %bitcast.15, s32[96]{0:T(128)S(1)} %bitcast.16, s32[1]{0:T(128)S(6)} %copy.21.count_ref, bf16[96,256,128]{2,1,0:T(8,128)(2,1)} %split_weights.1.weight_hbm, f32[32,32,128]{2,1,0:T(8,128)S(1)} %all-to-all-done.got_ref, ...), custom_call_target="tpu_custom_call" | custom-call | flops 800000000 | bytes 8000000 | tf_op jit(solution)/shard_map/margins/pallas_call | solution.py:267
  54.5 4.3 %all-to-all-start.1 = ((f32[32,32,128]{2,1,0:T(8,128)}), f32[32,32,128]{2,1,0:T(8,128)S(1)}, u32[]{:S(2)}, u32[]{:S(2)}) async-start(f32[32,32,128]{2,1,0:T(8,128)} %get-tuple-element.7), calls=%async_computation.1 | async-start | bytes 1048576 | tf_op jit(solution)/shard_map/all_to_all | solution.py:397
  58.8 0.0 copy-done.2
  58.8 1.8 %collective-permute-start.3 = (f32[96,4,128]{2,1,0:T(4,128)S(1)}, f32[96,4,128]{2,1,0:T(4,128)S(1)}, u32[]{:S(2)}, u32[]{:S(2)}) collective-permute-start(f32[96,4,128]{2,1,0:T(4,128)S(1)} %copy-done.2), channel_id=1, source_target_pairs={{0,1},{1,2},{2,3},{3,0},{4,5},{5,6},{6,7},{7,4},{8,9},{9,10},{10,1... | collective-permute-start | bytes 589832 | tf_op jit(solution)/shard_map/ppermute | solution.py:370
  60.6 2.4 %collective-permute-start.4 = (f32[96,4,128]{2,1,0:T(4,128)S(1)}, f32[96,4,128]{2,1,0:T(4,128)S(1)}, u32[]{:S(2)}, u32[]{:S(2)}) collective-permute-start(f32[96,4,128]{2,1,0:T(4,128)S(1)} %copy-done.2), channel_id=1, source_target_pairs={{0,2},{1,3},{2,0},{3,1},{4,6},{5,7},{6,4},{7,5},{8,10},{9,11},{10,... | collective-permute-start | bytes 589832 | tf_op jit(solution)/shard_map/ppermute | solution.py:370
  63.0 1.4 %collective-permute-start.5 = (f32[96,4,128]{2,1,0:T(4,128)S(1)}, f32[96,4,128]{2,1,0:T(4,128)S(1)}, u32[]{:S(2)}, u32[]{:S(2)}) collective-permute-start(f32[96,4,128]{2,1,0:T(4,128)S(1)} %copy-done.2), channel_id=1, source_target_pairs={{0,3},{1,0},{2,1},{3,2},{4,7},{5,4},{6,5},{7,6},{8,11},{9,8},{10,9... | collective-permute-start | bytes 589832 | tf_op jit(solution)/shard_map/ppermute | solution.py:370
  64.4 1.0 %copy.20 = f32[16,4,13,128]{3,0,2,1:T(8,128)} copy(f32[16,4,13,128]{3,2,1,0:T(8,128)S(1)} %bitcast.14) | data formatting | bytes 851968 | tf_op jit(solution)/shard_map/slice | solution.py:398
  65.4 11.2 %collective-permute-done.3.refs_1_ = f32[96,4,128]{2,1,0:T(4,128)S(1)} collective-permute-done((f32[96,4,128]{2,1,0:T(4,128)S(1)}, f32[96,4,128]{2,1,0:T(4,128)S(1)}, u32[]{:S(2)}, u32[]{:S(2)}) %collective-permute-start.3) | collective-permute-done | bytes 196640 | tf_op jit(solution)/shard_map/ppermute | solution.py:370
  76.7 10.3 %collective-permute-done.4.refs_2_ = f32[96,4,128]{2,1,0:T(4,128)S(1)} collective-permute-done((f32[96,4,128]{2,1,0:T(4,128)S(1)}, f32[96,4,128]{2,1,0:T(4,128)S(1)}, u32[]{:S(2)}, u32[]{:S(2)}) %collective-permute-start.4) | collective-permute-done | bytes 196640 | tf_op jit(solution)/shard_map/ppermute | solution.py:370
  87.0 0.0 collective-permute-done.5.refs_3_
  87.0 0.0 all-to-all-done.1.answer_ref
  87.0 0.0 copy-done.1
  87.0 5.2 %finish.1 = f32[16,13,48,128]{3,2,1,0:T(8,128)} custom-call(s32[1]{0:T(128)} %bitcast.me_ref, s32[64]{0:T(128)S(1)} %compare_select_fusion.2.place_ref, f32[32,32,128]{2,1,0:T(8,128)S(1)} %all-to-all-done.1.answer_ref, f32[96,4,128]{2,1,0:T(4,128)S(1)} %copy-done.2, f32[96,4,128]{2,1,0:T(4,128)S(1)} %collective-permute-done.3.refs_1_, ...), custom_call_target="tpu_custom_call" | custom-call | flops 8000000 | bytes 12000000 | tf_op jit(solution)/shard_map/finish/pallas_call | solution.py:338
  (2 shorter events, 0.1 us)
Async XLA Ops:
  2.7 9.1 %collective-permute-start = (f32[49,4,128]{2,1,0:T(4,128)}, f32[49,4,128]{2,1,0:T(4,128)S(1)}, u32[]{:S(2)}, u32[]{:S(2)}) collective-permute-start(f32[49,4,128]{2,1,0:T(4,128)} %get-tuple-element.6.refs_0_.refs_4_), channel_id=1, source_target_pairs={{0,1},{1,2},{2,3},{3,0},{4,5},{5,6},{6,7},{7,4},{8,9},{9,10},{10,1... | collective-permute-start | bytes 301064 | tf_op jit(solution)/shard_map/ppermute | solution.py:370
  5.9 9.5 %collective-permute-start.1 = (f32[49,4,128]{2,1,0:T(4,128)}, f32[49,4,128]{2,1,0:T(4,128)S(1)}, u32[]{:S(2)}, u32[]{:S(2)}) collective-permute-start(f32[49,4,128]{2,1,0:T(4,128)} %get-tuple-element.6.refs_0_.refs_4_), channel_id=1, source_target_pairs={{0,2},{1,3},{2,0},{3,1},{4,6},{5,7},{6,4},{7,5},{8,10},{9,11},{10,... | collective-permute-start | bytes 301064 | tf_op jit(solution)/shard_map/ppermute | solution.py:370
  8.4 6.9 %collective-permute-start.2 = (f32[49,4,128]{2,1,0:T(4,128)}, f32[49,4,128]{2,1,0:T(4,128)S(1)}, u32[]{:S(2)}, u32[]{:S(2)}) collective-permute-start(f32[49,4,128]{2,1,0:T(4,128)} %get-tuple-element.6.refs_0_.refs_4_), channel_id=1, source_target_pairs={{0,3},{1,0},{2,1},{3,2},{4,7},{5,4},{6,5},{7,6},{8,11},{9,8},{10,9... | collective-permute-start | bytes 301064 | tf_op jit(solution)/shard_map/ppermute | solution.py:370
  15.4 0.9 copy-start
  16.3 10.1 %copy-start.8 = (f32[16,52,128]{2,0,1:T(8,128)S(1)}, f32[16,52,128]{2,0,1:T(8,128)}, u32[]{:S(2)}) copy-start(f32[16,52,128]{2,0,1:T(8,128)} %param.22) | copy-start | bytes 1277956
  20.5 20.2 %all-to-all-start = ((f32[32,32,128]{2,1,0:T(8,128)}), f32[32,32,128]{2,1,0:T(8,128)S(1)}, u32[]{:S(2)}, u32[]{:S(2)}) async-start(f32[32,32,128]{2,1,0:T(8,128)} %bottoms.1), calls=%async_computation | async-start | bytes 1048576 | tf_op jit(solution)/shard_map/all_to_all | solution.py:391
  27.2 13.4 %copy-start.3 = (f32[16,128]{1,0:T(8,128)S(1)}, f32[16,128]{1,0:T(8,128)}, u32[]{:S(2)}) copy-start(f32[16,128]{1,0:T(8,128)} %coef_ref.1) | copy-start | bytes 24580
  27.3 13.4 %copy-start.4 = (s32[16,128]{1,0:T(8,128)S(1)}, s32[16,128]{1,0:T(8,128)}, u32[]{:S(2)}) copy-start(s32[16,128]{1,0:T(8,128)} %mask_ref.1) | copy-start | bytes 24580
  27.3 13.4 %copy-start.5 = (f32[16,128]{1,0:T(8,128)S(1)}, f32[16,128]{1,0:T(8,128)}, u32[]{:S(2)}) copy-start(f32[16,128]{1,0:T(8,128)} %land_ref.1) | copy-start | bytes 24580
  27.3 13.4 %copy-start.6 = (s32[1,96]{1,0:T(1,128)S(1)}, s32[1,96]{1,0:T(1,128)}, u32[]{:S(2)}) copy-start(s32[1,96]{1,0:T(1,128)} %param.18) | copy-start | bytes 1156
  27.3 13.3 %copy-start.7 = (s32[1,96]{1,0:T(1,128)S(1)}, s32[1,96]{1,0:T(1,128)}, u32[]{:S(2)}) copy-start(s32[1,96]{1,0:T(1,128)} %param.19) | copy-start | bytes 1156
  36.8 22.0 %copy-start.2 = (f32[96,4,128]{2,1,0:T(4,128)S(1)}, f32[96,4,128]{2,1,0:T(4,128)}, u32[]{:S(2)}) copy-start(f32[96,4,128]{2,1,0:T(4,128)} %get-tuple-element.8.refs_0_) | copy-start | bytes 589828
  36.8 50.2 %copy-start.1 = (f32[49,4,128]{2,1,0:T(4,128)S(1)}, f32[49,4,128]{2,1,0:T(4,128)}, u32[]{:S(2)}) copy-start(f32[49,4,128]{2,1,0:T(4,128)} %get-tuple-element.6.refs_0_.refs_4_) | copy-start | bytes 301060
  54.5 32.5 %all-to-all-start.1 = ((f32[32,32,128]{2,1,0:T(8,128)}), f32[32,32,128]{2,1,0:T(8,128)S(1)}, u32[]{:S(2)}, u32[]{:S(2)}) async-start(f32[32,32,128]{2,1,0:T(8,128)} %get-tuple-element.7), calls=%async_computation.1 | async-start | bytes 1048576 | tf_op jit(solution)/shard_map/all_to_all | solution.py:397
  58.8 17.9 %collective-permute-start.3 = (f32[96,4,128]{2,1,0:T(4,128)S(1)}, f32[96,4,128]{2,1,0:T(4,128)S(1)}, u32[]{:S(2)}, u32[]{:S(2)}) collective-permute-start(f32[96,4,128]{2,1,0:T(4,128)S(1)} %copy-done.2), channel_id=1, source_target_pairs={{0,1},{1,2},{2,3},{3,0},{4,5},{5,6},{6,7},{7,4},{8,9},{9,10},{10,1... | collective-permute-start | bytes 589832 | tf_op jit(solution)/shard_map/ppermute | solution.py:370
  60.6 26.3 %collective-permute-start.4 = (f32[96,4,128]{2,1,0:T(4,128)S(1)}, f32[96,4,128]{2,1,0:T(4,128)S(1)}, u32[]{:S(2)}, u32[]{:S(2)}) collective-permute-start(f32[96,4,128]{2,1,0:T(4,128)S(1)} %copy-done.2), channel_id=1, source_target_pairs={{0,2},{1,3},{2,0},{3,1},{4,6},{5,7},{6,4},{7,5},{8,10},{9,11},{10,... | collective-permute-start | bytes 589832 | tf_op jit(solution)/shard_map/ppermute | solution.py:370
  63.0 23.9 %collective-permute-start.5 = (f32[96,4,128]{2,1,0:T(4,128)S(1)}, f32[96,4,128]{2,1,0:T(4,128)S(1)}, u32[]{:S(2)}, u32[]{:S(2)}) collective-permute-start(f32[96,4,128]{2,1,0:T(4,128)S(1)} %copy-done.2), channel_id=1, source_target_pairs={{0,3},{1,0},{2,1},{3,2},{4,7},{5,4},{6,5},{7,6},{8,11},{9,8},{10,9... | collective-permute-start | bytes 589832 | tf_op jit(solution)/shard_map/ppermute | solution.py:370

commit v3 on v2

--- a/solution.py
+++ b/solution.py
@@ -166,34 +166,42 @@
     out_ref[:, size:, :] = low
 
 
-def split_weights(weight, step=8):
+def split_weights(weight, part, parts, step=8):
     margins, cells, columns = weight.shape
-    step = math.gcd(step, margins)
+    count = margins // parts
+    step = math.gcd(step, count)
+    first = part * (count // step)
     return pl.pallas_call(
         split_kernel,
-        grid=(margins // step,),
-        out_shape=jax.ShapeDtypeStruct((margins, 2 * cells, columns), BF16),
-        in_specs=[pl.BlockSpec((step, cells, columns), lambda i: (i, 0, 0))],
+        grid=(count // step,),
+        out_shape=jax.ShapeDtypeStruct((count, 2 * cells, columns), BF16),
+        in_specs=[pl.BlockSpec((step, cells, columns), lambda i: (first + i, 0, 0))],
         out_specs=pl.BlockSpec((step, 2 * cells, columns), lambda i: (i, 0, 0)),
         compiler_params=params(ROOMY),
-        cost_estimate=pl.CostEstimate(flops=5000000, bytes_accessed=13000000, transcendentals=0),
+        cost_estimate=pl.CostEstimate(flops=2500000, bytes_accessed=6500000, transcendentals=0),
         name="split_weights",
     )(weight)
 
 
 def margin_kernel(
     groups, rows, slots, gain_row, unroll,
-    slot_ref, block_ref, count_ref, weight_hbm, got_ref, surface_ref, coef_ref, mask_ref, land_ref,
+    slot_ref, block_ref, count_ref, weight_a, weight_b, got_ref, surface_ref, coef_ref, mask_ref, land_ref,
     reply_ref, flux_ref,
     weight_ref, value_ref, cell_ref, two_ref, back_ref, sem,
 ):
     margins = weight_ref.shape[0]
     chunks = sem.shape[0]
     size = margins // chunks
+    half = chunks // 2
+
+    def fetch(c):
+        source = weight_a if c < half else weight_b
+        return pltpu.make_async_copy(
+            source.at[pl.ds(c % half * size, size)], weight_ref.at[pl.ds(c * size, size)], sem.at[c]
+        )
+
     for c in range(chunks):
-        pltpu.make_async_copy(
-            weight_hbm.at[pl.ds(c * size, size)], weight_ref.at[pl.ds(c * size, size)], sem.at[c]
-        ).start()
+        fetch(c).start()
     tall = groups * rows
     columns = weight_ref.shape[2]
     sources = value_ref.shape[0] // slots
@@ -209,22 +217,22 @@
     back_ref[...] = jnp.zeros_like(back_ref)
 
     for c in range(chunks):
-        pltpu.make_async_copy(
-            weight_hbm.at[pl.ds(c * size, size)], weight_ref.at[pl.ds(c * size, size)], sem.at[c]
-        ).wait()
+        fetch(c).wait()
 
         @pl.loop(0, size // unroll)
         def _(step):
             for u in range(unroll):
                 k = c * size + step * unroll + u
                 target = jnp.where(k < count, block_ref[k], cells)
-                product = lax.dot_general(
-                    value_ref[slot_ref[k]], weight_ref[k], (((1,), (1,)), ((), ())),
+                one = lax.dot_general(
+                    value_ref[slot_ref[k]], weight_ref[k, :columns], (((1,), (1,)), ((), ())),
                     preferred_element_type=F32,
                 )
-                cell_ref[target] += (
-                    product[:tall, :columns] + (product[tall:, :columns] + product[:tall, columns:])
+                two = lax.dot_general(
+                    value_ref[slot_ref[k], :tall], weight_ref[k, columns:], (((1,), (1,)), ((), ())),
+                    preferred_element_type=F32,
                 )
+                cell_ref[target] += one[:tall] + (one[tall:] + two)
 
     for j in range(cells):
         cell = cell_ref[j]
@@ -234,21 +242,19 @@
         flux = scale * (surface_ref[j] - cell)
         flux_ref[j] = flux
         high, low = split(flux)
-        two_ref[j, :tall, :columns] = high
-        two_ref[j, :tall, columns:] = high
-        two_ref[j, tall:, :columns] = low
-        two_ref[j, tall:, columns:] = low
+        two_ref[j, :tall, :] = high
+        two_ref[j, tall:, :] = low
 
     @pl.loop(0, margins // unroll)
     def _(step):
         for u in range(unroll):
             k = step * unroll + u
             target = jnp.where(k < count, slot_ref[k], sources * slots)
-            product = lax.dot_general(
-                two_ref[block_ref[k]], weight_ref[k], (((1,), (0,)), ((), ())),
-                preferred_element_type=F32,
+            one = jnp.dot(two_ref[block_ref[k]], weight_ref[k, :columns], preferred_element_type=F32)
+            two = jnp.dot(
+                two_ref[block_ref[k], :tall], weight_ref[k, columns:], preferred_element_type=F32
             )
-            back_ref[target] += product[:tall] + product[tall:]
+            back_ref[target] += one[:tall] + (one[tall:] + two)
 
     for a in range(sources):
         for p in range(slots):
@@ -258,32 +264,35 @@
                 )
 
 
-def margins_stage(slot, block, count, weights, got, surface, coef, mask, land, groups, rows, slots, gain_row):
+def margins_stage(slot, block, count, weights_a, weights_b, got, surface, coef, mask, land,
+                  groups, rows, slots, gain_row):
+    half, twice, columns = weights_a.shape
+    margins = 2 * half
     owners, _, width = got.shape
     cells, tall, _ = surface.shape
     sources = owners // groups
-    unroll = 4
     chunks = 6
+    unroll = math.gcd(16, margins // chunks)
     return pl.pallas_call(
         functools.partial(margin_kernel, groups, rows, slots, gain_row, unroll),
         out_shape=(
             jax.ShapeDtypeStruct(got.shape, F32),
             jax.ShapeDtypeStruct(surface.shape, F32),
         ),
-        in_specs=[smem()] * 3 + [hbm()] + [vmem()] * 5,
+        in_specs=[smem()] * 3 + [hbm()] * 2 + [vmem()] * 5,
         out_specs=(vmem(), vmem()),
         scratch_shapes=[
-            pltpu.VMEM(weights.shape, BF16),
+            pltpu.VMEM((margins, twice, columns), BF16),
             pltpu.VMEM((sources * slots, 2 * tall, width), BF16),
             pltpu.VMEM((cells + 1, tall, width), F32),
-            pltpu.VMEM((cells, 2 * tall, 2 * width), BF16),
+            pltpu.VMEM((cells, 2 * tall, width), BF16),
             pltpu.VMEM((sources * slots + 1, tall, width), F32),
             pltpu.SemaphoreType.DMA((chunks,)),
         ],
         compiler_params=params(ROOMY),
         cost_estimate=pl.CostEstimate(flops=800000000, bytes_accessed=8000000, transcendentals=0),
         name="margins",
-    )(slot, block, count, weights, got, surface, coef, mask, land)
+    )(slot, block, count, weights_a, weights_b, got, surface, coef, mask, land)
 
 
 def finish_kernel(groups, own, rows, me_ref, place_ref, answer_ref, *refs):
@@ -382,7 +391,8 @@
         blocks,
     ).astype(jnp.int32)
     me = me[None]
-    weights = split_weights(margin_weight[0])
+    weights_a = split_weights(margin_weight[0], 0, 2)
+    weights_b = split_weights(margin_weight[0], 1, 2)
     surface = jnp.pad(
         surface_value.reshape(cells, groups, shares, width),
         ((0, 0), (0, 0), (0, rows - shares), (0, 0)),
@@ -391,7 +401,7 @@
     got = lax.all_to_all(send, ("atm", "xg"), split_axis=0, concat_axis=0, tiled=True)
     seconds = shared(second)
     reply, flux = margins_stage(
-        margin_slot[0], margin_block[0], margin_count, weights, got, surface,
+        margin_slot[0], margin_block[0], margin_count, weights_a, weights_b, got, surface,
         exchange_coef, land_mask, land_gain, groups, rows, slots, shares,
     )
     answer = lax.all_to_all(reply, ("atm", "xg"), split_axis=0, concat_axis=0, tiled=True)

time: 94 us -> 90.2 us (0.960)
  Pallas kernels: 34.9 us -> 29 us
  local copies, waits for them, and re-layouts: 3 us -> 6.29 us
  waiting for transfers between devices: 30 us -> 28.9 us
    pallas_call x1, Pallas kernels: 13.9 us -> 10.2 us  [margins_stage(): pl.pallas_call(functools.partial(margin_kernel, groups, rows, slots, gain...]
    unnamed x19 -> x23, local copies, waits for them, and re-layouts: 1.7 us -> 4.98 us
    pallas_call x1 -> x2, Pallas kernels: 9.49 us -> 7.29 us  [split_weights(): pl.pallas_call(split_kernel, grid=(count // step,), out_shape=jax.ShapeDt...]
    all_to_all x1, waiting for transfers between devices: 3.82 us -> 2.72 us  [per_device(): lax.all_to_all(send, ('atm', 'xg'), split_axis=0, concat_axis=0, tiled=True)]
  transfers between devices with their start and end apart: 8 -> 8, of which waited for: 5 -> 5; matrix products, arithmetic and copies ran while one was open for 2% -> 2% of each run, Pallas kernels for 10% -> 8%
where the time goes in v3:
time: 90.2 us; the launch traced here: 88.5 us
  Pallas kernels  29 us (32%)
  waiting for transfers between devices  28.9 us (32%)
  starting transfers between devices  22.8 us (25%)
  local copies, waits for them, and re-layouts  6.29 us (7%)
  between operations  1.43 us (2%)
    ppermute x6, waiting for transfers between devices, shift(): lax.ppermute(array, 'xg', [(i, (i + by) % groups) for i in range(groups)])  26.2 us
    ppermute x6, starting transfers between devices, shift(): lax.ppermute(array, 'xg', [(i, (i + by) % groups) for i in range(groups)])  12.7 us
    pallas_call x1, Pallas kernels, margins_stage(): pl.pallas_call(functools.partial(margin_kernel, groups, rows, slots, gain...  10.2 us
    pallas_call x2, Pallas kernels, split_weights(): pl.pallas_call(split_kernel, grid=(count // step,), out_shape=jax.ShapeDt...  7.29 us
    all_to_all x1, starting transfers between devices, per_device(): lax.all_to_all(send, ('atm', 'xg'), split_axis=0, concat_axis=0, tiled=True)  5.91 us
    pallas_call x1, Pallas kernels, finish(): pl.pallas_call(functools.partial(finish_kernel, groups, blocks // groups,...  5.23 us
    unnamed x23, local copies, waits for them, and re-layouts  4.98 us
    all_to_all x1, starting transfers between devices, per_device(): lax.all_to_all(reply, ('atm', 'xg'), split_axis=0, concat_axis=0, tiled=T...  4.2 us
  transfers between devices with their start and end apart: 8, of which 5 were waited for; matrix products, arithmetic and copies ran while one was open for 2% of the time, Pallas kernels for 8%

profile of v3, /device:TPU:0, one launch (start us, length us, event | category | flops | bytes accessed | tf_op | source)
XLA Modules:
  0.0 88.5 jit_solution(3872861642931569751)
XLA Ops:
  0.6 2.1 %factors.1 = (f32[49,4,128]{2,1,0:T(4,128)}, f32[96,4,128]{2,1,0:T(4,128)}) custom-call(f32[192,128]{1,0:T(8,128)} %bitcast.24, f32[192,128]{1,0:T(8,128)} %bitcast.25, f32[4,128]{1,0:T(4,128)} %gain_hbm.1), custom_call_target="tpu_custom_call" | custom-call | flops 1000000 | bytes 400000 | tf_op jit(solution)/shard_map/factors/pallas_call | solution.py:76
  2.8 3.1 %collective-permute-start = (f32[49,4,128]{2,1,0:T(4,128)}, f32[49,4,128]{2,1,0:T(4,128)S(1)}, u32[]{:S(2)}, u32[]{:S(2)}) collective-permute-start(f32[49,4,128]{2,1,0:T(4,128)} %get-tuple-element.6.refs_0_.refs_4_), channel_id=1, source_target_pairs={{0,1},{1,2},{2,3},{3,0},{4,5},{5,6},{6,7},{7,4},{8,9},{9,10},{10,1... | collective-permute-start | bytes 301064 | tf_op jit(solution)/shard_map/ppermute | solution.py:379
  5.9 2.6 %collective-permute-start.1 = (f32[49,4,128]{2,1,0:T(4,128)}, f32[49,4,128]{2,1,0:T(4,128)S(1)}, u32[]{:S(2)}, u32[]{:S(2)}) collective-permute-start(f32[49,4,128]{2,1,0:T(4,128)} %get-tuple-element.6.refs_0_.refs_4_), channel_id=1, source_target_pairs={{0,2},{1,3},{2,0},{3,1},{4,6},{5,7},{6,4},{7,5},{8,10},{9,11},{10,... | collective-permute-start | bytes 301064 | tf_op jit(solution)/shard_map/ppermute | solution.py:379
  8.4 1.3 %collective-permute-start.2 = (f32[49,4,128]{2,1,0:T(4,128)}, f32[49,4,128]{2,1,0:T(4,128)S(1)}, u32[]{:S(2)}, u32[]{:S(2)}) collective-permute-start(f32[49,4,128]{2,1,0:T(4,128)} %get-tuple-element.6.refs_0_.refs_4_), channel_id=1, source_target_pairs={{0,3},{1,0},{2,1},{3,2},{4,7},{5,4},{6,5},{7,6},{8,11},{9,8},{10,9... | collective-permute-start | bytes 301064 | tf_op jit(solution)/shard_map/ppermute | solution.py:379
  9.8 0.8 copy.18
  10.6 0.1 reshape_squeeze.3
  10.7 1.1 %collective-permute-done.refs_1_.refs_5_ = f32[49,4,128]{2,1,0:T(4,128)S(1)} collective-permute-done((f32[49,4,128]{2,1,0:T(4,128)}, f32[49,4,128]{2,1,0:T(4,128)S(1)}, u32[]{:S(2)}, u32[]{:S(2)}) %collective-permute-start) | collective-permute-done | bytes 100384 | tf_op jit(solution)/shard_map/ppermute | solution.py:379
  11.8 3.5 %collective-permute-done.1.refs_2_.refs_6_ = f32[49,4,128]{2,1,0:T(4,128)S(1)} collective-permute-done((f32[49,4,128]{2,1,0:T(4,128)}, f32[49,4,128]{2,1,0:T(4,128)S(1)}, u32[]{:S(2)}, u32[]{:S(2)}) %collective-permute-start.1) | collective-permute-done | bytes 100384 | tf_op jit(solution)/shard_map/ppermute | solution.py:379
  15.4 0.0 collective-permute-done.2.refs_3_.refs_7_
  15.4 0.0 copy-start.2
  15.4 0.9 %copy-done.2 = f32[49,4,128]{2,1,0:T(4,128)S(1)} copy-done((f32[49,4,128]{2,1,0:T(4,128)S(1)}, f32[49,4,128]{2,1,0:T(4,128)}, u32[]{:S(2)}) %copy-start.2) | copy-done | bytes 100376
  16.3 0.0 copy-start.10
  16.3 4.2 %bottoms.1 = f32[32,32,128]{2,1,0:T(8,128)} custom-call(s32[1]{0:T(128)} %bitcast.me_ref, s32[64]{0:T(128)S(1)} %compare_select_fusion.2.place_ref, f32[49,4,128]{2,1,0:T(4,128)S(1)} %copy-done.2, f32[49,4,128]{2,1,0:T(4,128)S(1)} %collective-permute-done.refs_1_.refs_5_, f32[49,4,128]{2,1,0:T(4,128)S(1)} %collective-permute-done.1.refs_2_.refs_6_, ...), custom_call_target="tpu_custom_call" | custom-call | flops 4000000 | bytes 7000000 | tf_op jit(solution)/shard_map/bottoms/pallas_call | solution.py:143
  20.5 5.9 %all-to-all-start = ((f32[32,32,128]{2,1,0:T(8,128)}), f32[32,32,128]{2,1,0:T(8,128)S(1)}, u32[]{:S(2)}, u32[]{:S(2)}) async-start(f32[32,32,128]{2,1,0:T(8,128)} %bottoms.1), calls=%async_computation | async-start | bytes 1048576 | tf_op jit(solution)/shard_map/all_to_all | solution.py:401
  26.4 0.0 copy-done.10
  26.4 0.2 copy.19
  27.2 3.6 %split_weights.2.weight_a = bf16[48,256,128]{2,1,0:T(8,128)(2,1)S(1)} custom-call(f32[96,128,128]{2,1,0:T(8,128)} %bitcast.17), custom_call_target="tpu_custom_call" | custom-call | flops 2500000 | bytes 6500000 | tf_op jit(solution)/shard_map/split_weights/pallas_call | solution.py:174
  30.9 0.0 copy-start
  30.9 1.7 %copy-done = bf16[48,256,128]{2,1,0:T(8,128)(2,1)} copy-done((bf16[48,256,128]{2,1,0:T(8,128)(2,1)}, bf16[48,256,128]{2,1,0:T(8,128)(2,1)S(1)}, u32[]{:S(2)}) %copy-start) | copy-done | bytes 3145752
  32.5 0.0 copy-start.5
  32.5 0.0 copy-start.6
  32.5 0.0 copy-start.7
  32.6 0.0 copy-start.8
  32.6 0.0 copy-start.9
  32.6 3.7 %split_weights.3.weight_b = bf16[48,256,128]{2,1,0:T(8,128)(2,1)S(1)} custom-call(f32[96,128,128]{2,1,0:T(8,128)} %bitcast.18), custom_call_target="tpu_custom_call" | custom-call | flops 2500000 | bytes 6500000 | tf_op jit(solution)/shard_map/split_weights/pallas_call | solution.py:174
  36.2 0.0 copy-start.1
  36.3 1.6 %copy-done.1 = bf16[48,256,128]{2,1,0:T(8,128)(2,1)} copy-done((bf16[48,256,128]{2,1,0:T(8,128)(2,1)}, bf16[48,256,128]{2,1,0:T(8,128)(2,1)S(1)}, u32[]{:S(2)}) %copy-start.1) | copy-done | bytes 3145752
  37.9 0.0 copy-start.4
  37.9 0.0 copy-start.3
  37.9 2.7 %all-to-all-done.got_ref = f32[32,32,128]{2,1,0:T(8,128)S(1)} async-done(((f32[32,32,128]{2,1,0:T(8,128)}), f32[32,32,128]{2,1,0:T(8,128)S(1)}, u32[]{:S(2)}, u32[]{:S(2)}) %all-to-all-start) | async-done | bytes 524320 | tf_op jit(solution)/shard_map/all_to_all | solution.py:401
  40.6 0.0 copy-done.5
  40.6 0.0 copy-done.6
  40.6 0.0 copy-done.7
  40.6 0.0 copy-done.8
  40.6 0.0 copy-done.9
  40.6 10.2 %margins.1 = (f32[32,32,128]{2,1,0:T(8,128)}, f32[16,64,128]{2,1,0:T(8,128)S(1)}) custom-call(s32[96]{0:T(128)S(1)} %bitcast.15, s32[96]{0:T(128)S(1)} %bitcast.16, s32[1]{0:T(128)S(6)} %copy.21.count_ref, bf16[48,256,128]{2,1,0:T(8,128)(2,1)} %copy-done, bf16[48,256,128]{2,1,0:T(8,128)(2,1)} %copy-done.1, f32[32,32,128]{2,1,0:T(8,128)S(1)} %all-to-all-done.got_ref, ...), custom_call_target="tpu_custom_call" | custom-call | flops 800000000 | bytes 8000000 | tf_op jit(solution)/shard_map/margins/pallas_call | solution.py:276
  50.8 4.2 %all-to-all-start.1 = ((f32[32,32,128]{2,1,0:T(8,128)}), f32[32,32,128]{2,1,0:T(8,128)S(1)}, u32[]{:S(2)}, u32[]{:S(2)}) async-start(f32[32,32,128]{2,1,0:T(8,128)} %get-tuple-element.7), calls=%async_computation.1 | async-start | bytes 1048576 | tf_op jit(solution)/shard_map/all_to_all | solution.py:407
  55.0 0.0 copy-done.4
  55.0 1.8 %collective-permute-start.3 = (f32[96,4,128]{2,1,0:T(4,128)S(1)}, f32[96,4,128]{2,1,0:T(4,128)S(1)}, u32[]{:S(2)}, u32[]{:S(2)}) collective-permute-start(f32[96,4,128]{2,1,0:T(4,128)S(1)} %copy-done.4), channel_id=1, source_target_pairs={{0,1},{1,2},{2,3},{3,0},{4,5},{5,6},{6,7},{7,4},{8,9},{9,10},{10,1... | collective-permute-start | bytes 589832 | tf_op jit(solution)/shard_map/ppermute | solution.py:379
  56.9 2.4 %collective-permute-start.4 = (f32[96,4,128]{2,1,0:T(4,128)S(1)}, f32[96,4,128]{2,1,0:T(4,128)S(1)}, u32[]{:S(2)}, u32[]{:S(2)}) collective-permute-start(f32[96,4,128]{2,1,0:T(4,128)S(1)} %copy-done.4), channel_id=1, source_target_pairs={{0,2},{1,3},{2,0},{3,1},{4,6},{5,7},{6,4},{7,5},{8,10},{9,11},{10,... | collective-permute-start | bytes 589832 | tf_op jit(solution)/shard_map/ppermute | solution.py:379
  59.3 1.4 %collective-permute-start.5 = (f32[96,4,128]{2,1,0:T(4,128)S(1)}, f32[96,4,128]{2,1,0:T(4,128)S(1)}, u32[]{:S(2)}, u32[]{:S(2)}) collective-permute-start(f32[96,4,128]{2,1,0:T(4,128)S(1)} %copy-done.4), channel_id=1, source_target_pairs={{0,3},{1,0},{2,1},{3,2},{4,7},{5,4},{6,5},{7,6},{8,11},{9,8},{10,9... | collective-permute-start | bytes 589832 | tf_op jit(solution)/shard_map/ppermute | solution.py:379
  60.7 1.0 %copy.20 = f32[16,4,13,128]{3,0,2,1:T(8,128)} copy(f32[16,4,13,128]{3,2,1,0:T(8,128)S(1)} %bitcast.14) | data formatting | bytes 851968 | tf_op jit(solution)/shard_map/slice | solution.py:408
  61.7 11.2 %collective-permute-done.3.refs_1_ = f32[96,4,128]{2,1,0:T(4,128)S(1)} collective-permute-done((f32[96,4,128]{2,1,0:T(4,128)S(1)}, f32[96,4,128]{2,1,0:T(4,128)S(1)}, u32[]{:S(2)}, u32[]{:S(2)}) %collective-permute-start.3) | collective-permute-done | bytes 196640 | tf_op jit(solution)/shard_map/ppermute | solution.py:379
  72.9 10.3 %collective-permute-done.4.refs_2_ = f32[96,4,128]{2,1,0:T(4,128)S(1)} collective-permute-done((f32[96,4,128]{2,1,0:T(4,128)S(1)}, f32[96,4,128]{2,1,0:T(4,128)S(1)}, u32[]{:S(2)}, u32[]{:S(2)}) %collective-permute-start.4) | collective-permute-done | bytes 196640 | tf_op jit(solution)/shard_map/ppermute | solution.py:379
  83.2 0.0 collective-permute-done.5.refs_3_
  83.2 0.0 all-to-all-done.1.answer_ref
  83.2 0.0 copy-done.3
  83.2 5.2 %finish.1 = f32[16,13,48,128]{3,2,1,0:T(8,128)} custom-call(s32[1]{0:T(128)} %bitcast.me_ref, s32[64]{0:T(128)S(1)} %compare_select_fusion.2.place_ref, f32[32,32,128]{2,1,0:T(8,128)S(1)} %all-to-all-done.1.answer_ref, f32[96,4,128]{2,1,0:T(4,128)S(1)} %copy-done.4, f32[96,4,128]{2,1,0:T(4,128)S(1)} %collective-permute-done.3.refs_1_, ...), custom_call_target="tpu_custom_call" | custom-call | flops 8000000 | bytes 12000000 | tf_op jit(solution)/shard_map/finish/pallas_call | solution.py:347
  (2 shorter events, 0.1 us)
Async XLA Ops:
  2.8 9.1 %collective-permute-start = (f32[49,4,128]{2,1,0:T(4,128)}, f32[49,4,128]{2,1,0:T(4,128)S(1)}, u32[]{:S(2)}, u32[]{:S(2)}) collective-permute-start(f32[49,4,128]{2,1,0:T(4,128)} %get-tuple-element.6.refs_0_.refs_4_), channel_id=1, source_target_pairs={{0,1},{1,2},{2,3},{3,0},{4,5},{5,6},{6,7},{7,4},{8,9},{9,10},{10,1... | collective-permute-start | bytes 301064 | tf_op jit(solution)/shard_map/ppermute | solution.py:379
  5.9 9.5 %collective-permute-start.1 = (f32[49,4,128]{2,1,0:T(4,128)}, f32[49,4,128]{2,1,0:T(4,128)S(1)}, u32[]{:S(2)}, u32[]{:S(2)}) collective-permute-start(f32[49,4,128]{2,1,0:T(4,128)} %get-tuple-element.6.refs_0_.refs_4_), channel_id=1, source_target_pairs={{0,2},{1,3},{2,0},{3,1},{4,6},{5,7},{6,4},{7,5},{8,10},{9,11},{10,... | collective-permute-start | bytes 301064 | tf_op jit(solution)/shard_map/ppermute | solution.py:379
  8.4 6.9 %collective-permute-start.2 = (f32[49,4,128]{2,1,0:T(4,128)}, f32[49,4,128]{2,1,0:T(4,128)S(1)}, u32[]{:S(2)}, u32[]{:S(2)}) collective-permute-start(f32[49,4,128]{2,1,0:T(4,128)} %get-tuple-element.6.refs_0_.refs_4_), channel_id=1, source_target_pairs={{0,3},{1,0},{2,1},{3,2},{4,7},{5,4},{6,5},{7,6},{8,11},{9,8},{10,9... | collective-permute-start | bytes 301064 | tf_op jit(solution)/shard_map/ppermute | solution.py:379
  15.4 0.9 %copy-start.2 = (f32[49,4,128]{2,1,0:T(4,128)S(1)}, f32[49,4,128]{2,1,0:T(4,128)}, u32[]{:S(2)}) copy-start(f32[49,4,128]{2,1,0:T(4,128)} %get-tuple-element.6.refs_0_.refs_4_) | copy-start | bytes 301060
  16.3 10.1 %copy-start.10 = (f32[16,52,128]{2,0,1:T(8,128)S(1)}, f32[16,52,128]{2,0,1:T(8,128)}, u32[]{:S(2)}) copy-start(f32[16,52,128]{2,0,1:T(8,128)} %param.22) | copy-start | bytes 1277956
  20.5 20.2 %all-to-all-start = ((f32[32,32,128]{2,1,0:T(8,128)}), f32[32,32,128]{2,1,0:T(8,128)S(1)}, u32[]{:S(2)}, u32[]{:S(2)}) async-start(f32[32,32,128]{2,1,0:T(8,128)} %bottoms.1), calls=%async_computation | async-start | bytes 1048576 | tf_op jit(solution)/shard_map/all_to_all | solution.py:401
  30.9 1.7 %copy-start = (bf16[48,256,128]{2,1,0:T(8,128)(2,1)}, bf16[48,256,128]{2,1,0:T(8,128)(2,1)S(1)}, u32[]{:S(2)}) copy-start(bf16[48,256,128]{2,1,0:T(8,128)(2,1)S(1)} %split_weights.2.weight_a) | copy-start | bytes 9437188
  32.5 8.1 %copy-start.5 = (f32[16,128]{1,0:T(8,128)S(1)}, f32[16,128]{1,0:T(8,128)}, u32[]{:S(2)}) copy-start(f32[16,128]{1,0:T(8,128)} %coef_ref.1) | copy-start | bytes 24580
  32.5 8.1 %copy-start.6 = (s32[16,128]{1,0:T(8,128)S(1)}, s32[16,128]{1,0:T(8,128)}, u32[]{:S(2)}) copy-start(s32[16,128]{1,0:T(8,128)} %mask_ref.1) | copy-start | bytes 24580
  32.5 8.1 %copy-start.7 = (f32[16,128]{1,0:T(8,128)S(1)}, f32[16,128]{1,0:T(8,128)}, u32[]{:S(2)}) copy-start(f32[16,128]{1,0:T(8,128)} %land_ref.1) | copy-start | bytes 24580
  32.6 8.1 %copy-start.8 = (s32[1,96]{1,0:T(1,128)S(1)}, s32[1,96]{1,0:T(1,128)}, u32[]{:S(2)}) copy-start(s32[1,96]{1,0:T(1,128)} %param.18) | copy-start | bytes 1156
  32.6 8.1 %copy-start.9 = (s32[1,96]{1,0:T(1,128)S(1)}, s32[1,96]{1,0:T(1,128)}, u32[]{:S(2)}) copy-start(s32[1,96]{1,0:T(1,128)} %param.19) | copy-start | bytes 1156
  36.2 1.6 %copy-start.1 = (bf16[48,256,128]{2,1,0:T(8,128)(2,1)}, bf16[48,256,128]{2,1,0:T(8,128)(2,1)S(1)}, u32[]{:S(2)}) copy-start(bf16[48,256,128]{2,1,0:T(8,128)(2,1)S(1)} %split_weights.3.weight_b) | copy-start | bytes 9437188
  37.9 17.2 %copy-start.4 = (f32[96,4,128]{2,1,0:T(4,128)S(1)}, f32[96,4,128]{2,1,0:T(4,128)}, u32[]{:S(2)}) copy-start(f32[96,4,128]{2,1,0:T(4,128)} %get-tuple-element.8.refs_0_) | copy-start | bytes 589828
  37.9 45.3 %copy-start.3 = (f32[49,4,128]{2,1,0:T(4,128)S(1)}, f32[49,4,128]{2,1,0:T(4,128)}, u32[]{:S(2)}) copy-start(f32[49,4,128]{2,1,0:T(4,128)} %get-tuple-element.6.refs_0_.refs_4_) | copy-start | bytes 301060
  50.8 32.4 %all-to-all-start.1 = ((f32[32,32,128]{2,1,0:T(8,128)}), f32[32,32,128]{2,1,0:T(8,128)S(1)}, u32[]{:S(2)}, u32[]{:S(2)}) async-start(f32[32,32,128]{2,1,0:T(8,128)} %get-tuple-element.7), calls=%async_computation.1 | async-start | bytes 1048576 | tf_op jit(solution)/shard_map/all_to_all | solution.py:407
  55.0 17.9 %collective-permute-start.3 = (f32[96,4,128]{2,1,0:T(4,128)S(1)}, f32[96,4,128]{2,1,0:T(4,128)S(1)}, u32[]{:S(2)}, u32[]{:S(2)}) collective-permute-start(f32[96,4,128]{2,1,0:T(4,128)S(1)} %copy-done.4), channel_id=1, source_target_pairs={{0,1},{1,2},{2,3},{3,0},{4,5},{5,6},{6,7},{7,4},{8,9},{9,10},{10,1... | collective-permute-start | bytes 589832 | tf_op jit(solution)/shard_map/ppermute | solution.py:379
  56.9 26.3 %collective-permute-start.4 = (f32[96,4,128]{2,1,0:T(4,128)S(1)}, f32[96,4,128]{2,1,0:T(4,128)S(1)}, u32[]{:S(2)}, u32[]{:S(2)}) collective-permute-start(f32[96,4,128]{2,1,0:T(4,128)S(1)} %copy-done.4), channel_id=1, source_target_pairs={{0,2},{1,3},{2,0},{3,1},{4,6},{5,7},{6,4},{7,5},{8,10},{9,11},{10,... | collective-permute-start | bytes 589832 | tf_op jit(solution)/shard_map/ppermute | solution.py:379
  59.3 23.9 %collective-permute-start.5 = (f32[96,4,128]{2,1,0:T(4,128)S(1)}, f32[96,4,128]{2,1,0:T(4,128)S(1)}, u32[]{:S(2)}, u32[]{:S(2)}) collective-permute-start(f32[96,4,128]{2,1,0:T(4,128)S(1)} %copy-done.4), channel_id=1, source_target_pairs={{0,3},{1,0},{2,1},{3,2},{4,7},{5,4},{6,5},{7,6},{8,11},{9,8},{10,9... | collective-permute-start | bytes 589832 | tf_op jit(solution)/shard_map/ppermute | solution.py:379

commit v4 on v3

--- a/solution.py
+++ b/solution.py
@@ -36,13 +36,12 @@
 
 
 def split(value):
-    high = value.astype(BF16)
-    low = (value - high.astype(F32)).astype(BF16)
-    return high, low
+    high = value.astype(BF16).astype(F32)
+    return jnp.concatenate([high, value - high], 0).astype(BF16)
 
 
 def factor_kernel(levels, own, upper_hbm, lower_hbm, gain_hbm, first_ref, second_ref,
-                  upper_ref, lower_ref, gain_ref, inverse_ref, sem):
+                  upper_ref, lower_ref, gain_ref, sem):
     copies = [
         pltpu.make_async_copy(source, target, sem.at[i])
         for i, (source, target) in enumerate(
@@ -54,21 +53,17 @@
     for copy in copies:
         copy.wait()
     carried = jnp.zeros(gain_ref.shape, F32)
+    inverse = carried
     for k in range(levels):
         from_above = upper_ref[pl.ds(k, own, stride=levels), :] if k > 0 else jnp.zeros_like(carried)
         from_below = lower_ref[pl.ds(k, own, stride=levels), :] if k < levels - 1 else jnp.zeros_like(carried)
+        if k > 0:
+            first_ref[k] = from_above * inverse
         inverse = 1.0 / (1.0 + from_above + from_below - from_above * carried)
         carried = from_below * inverse
-        inverse_ref[k] = inverse
-        second_ref[k] = from_above * inverse
-        second_ref[levels + k] = carried
-    product = inverse_ref[levels - 1]
-    first_ref[levels] = gain_ref[...] * product
-    first_ref[levels - 1] = product
-    product = second_ref[levels - 1]
-    for k in range(levels - 2, -1, -1):
-        first_ref[k] = inverse_ref[k] * product
-        product = product * second_ref[k]
+        second_ref[k] = carried
+    first_ref[0] = inverse
+    first_ref[levels] = gain_ref[...] * inverse
 
 
 def factors(upper, lower, surface_gain):
@@ -77,7 +72,7 @@
         functools.partial(factor_kernel, levels, own),
         out_shape=(
             jax.ShapeDtypeStruct((levels + 1, own, width), F32),
-            jax.ShapeDtypeStruct((2 * levels, own, width), F32),
+            jax.ShapeDtypeStruct((levels, own, width), F32),
         ),
         in_specs=[hbm()] * 3,
         out_specs=(vmem(), vmem()),
@@ -85,7 +80,6 @@
             pltpu.VMEM((own * levels, width), F32),
             pltpu.VMEM((own * levels, width), F32),
             pltpu.VMEM((own, width), F32),
-            pltpu.VMEM((levels, own, width), F32),
             pltpu.SemaphoreType.DMA((3,)),
         ],
         compiler_params=params(MOST),
@@ -105,7 +99,7 @@
                 ).start()
 
 
-def bottom_kernel(groups, own, rows, me_ref, place_ref, *refs):
+def bottom_kernel(groups, own, rows, slots, me_ref, place_ref, *refs):
     parts, fields_ref, send_ref, held_ref, weight_ref, value_ref, own_ref, sem, own_sem = (
         refs[:groups], *refs[groups:]
     )
@@ -113,27 +107,31 @@
     fetch.start()
     fetch_fields(me_ref[0], groups, own, fields_ref, held_ref, sem)
     blocks = groups * own
+    pitch = round_up(rows, ROWS)
     levels = held_ref.shape[1]
     shares = held_ref.shape[0]
     for q in range(1, groups):
         weight_ref[:, q * own:(q + 1) * own, :] = parts[q][...]
     fetch.wait()
     weight_ref[:, :own, :] = own_ref[...]
+    weight = weight_ref[0]
+    for k in range(levels - 1, -1, -1):
+        ratio = weight_ref[k]
+        weight_ref[k] = weight
+        weight = weight * ratio
     value_ref[...] = jnp.zeros_like(value_ref)
-    value_ref[pl.ds(shares, blocks, stride=rows), :] = weight_ref[levels]
+    value_ref[pl.ds(shares, blocks, stride=pitch), :] = weight_ref[levels]
     for f in range(shares):
         pltpu.make_async_copy(held_ref.at[f], held_ref.at[f], sem.at[f]).wait()
         sums = [None] * 4
         for k in range(levels):
             term = weight_ref[k] * held_ref[f, k]
             sums[k % 4] = term if sums[k % 4] is None else sums[k % 4] + term
-        value_ref[pl.ds(f, blocks, stride=rows), :] = (sums[0] + sums[1]) + (sums[2] + sums[3])
-    owners, slot_rows = send_ref.shape[:2]
-    slots = slot_rows // rows
-    for d in range(owners):
+        value_ref[pl.ds(f, blocks, stride=pitch), :] = (sums[0] + sums[1]) + (sums[2] + sums[3])
+    for d in range(send_ref.shape[0] // (rows * slots)):
         for p in range(slots):
-            start = pl.multiple_of(place_ref[d * slots + p] * rows, rows)
-            send_ref[d, p * rows:(p + 1) * rows, :] = value_ref[pl.ds(start, rows), :]
+            start = pl.multiple_of(place_ref[d * slots + p] * pitch, pitch)
+            send_ref[pl.ds(d * rows * slots + p, rows, stride=slots), :] = value_ref[pl.ds(start, rows), :]
 
 
 def bottoms(me, place, parts, fields, owners, slots, rows):
@@ -141,14 +139,14 @@
     groups = len(parts)
     own = blocks // groups
     return pl.pallas_call(
-        functools.partial(bottom_kernel, groups, own, rows),
-        out_shape=jax.ShapeDtypeStruct((owners, slots * rows, width), F32),
+        functools.partial(bottom_kernel, groups, own, rows, slots),
+        out_shape=jax.ShapeDtypeStruct((owners * rows * slots, width), F32),
         in_specs=[smem(), smem(), hbm()] + [vmem()] * (groups - 1) + [hbm()],
         out_specs=vmem(),
         scratch_shapes=[
             pltpu.VMEM((shares, levels, blocks, width), F32),
             pltpu.VMEM((levels + 1, blocks, width), F32),
-            pltpu.VMEM(((blocks + 1) * rows, width), F32),
+            pltpu.VMEM(((blocks + 1) * round_up(rows, ROWS), width), F32),
             pltpu.VMEM((levels + 1, own, width), F32),
             pltpu.SemaphoreType.DMA((shares,)),
             pltpu.SemaphoreType.DMA(()),
@@ -160,10 +158,11 @@
 
 
 def split_kernel(weight_ref, out_ref):
-    high, low = split(weight_ref[...])
+    value = weight_ref[...]
     size = weight_ref.shape[1]
+    high = value.astype(BF16)
     out_ref[:, :size, :] = high
-    out_ref[:, size:, :] = low
+    out_ref[:, size:, :] = (value - high.astype(F32)).astype(BF16)
 
 
 def split_weights(weight, part, parts, step=8):
@@ -187,7 +186,7 @@
     groups, rows, slots, gain_row, unroll,
     slot_ref, block_ref, count_ref, weight_a, weight_b, got_ref, surface_ref, coef_ref, mask_ref, land_ref,
     reply_ref, flux_ref,
-    weight_ref, value_ref, cell_ref, two_ref, back_ref, sem,
+    weight_ref, value_ref, cell_ref, two_ref, back_ref, stack_ref, sem,
 ):
     margins = weight_ref.shape[0]
     chunks = sem.shape[0]
@@ -203,6 +202,7 @@
     for c in range(chunks):
         fetch(c).start()
     tall = groups * rows
+    top = round_up(tall, 2 * ROWS)
     columns = weight_ref.shape[2]
     sources = value_ref.shape[0] // slots
     cells = surface_ref.shape[0]
@@ -210,9 +210,11 @@
     for a in range(sources):
         for p in range(slots):
             for g in range(groups):
-                high, low = split(got_ref[a * groups + g, p * rows:(p + 1) * rows, :])
-                value_ref[a * slots + p, g * rows:(g + 1) * rows, :] = high
-                value_ref[a * slots + p, tall + g * rows:tall + (g + 1) * rows, :] = low
+                stack_ref[a * slots + p, g * rows:(g + 1) * rows, :] = (
+                    got_ref[pl.ds((a * groups + g) * rows * slots + p, rows, stride=slots), :]
+                )
+    for s in range(sources * slots):
+        value_ref[s] = split(stack_ref[s])
     cell_ref[...] = jnp.zeros_like(cell_ref)
     back_ref[...] = jnp.zeros_like(back_ref)
 
@@ -229,10 +231,10 @@
                     preferred_element_type=F32,
                 )
                 two = lax.dot_general(
-                    value_ref[slot_ref[k], :tall], weight_ref[k, columns:], (((1,), (1,)), ((), ())),
+                    value_ref[slot_ref[k], :top], weight_ref[k, columns:], (((1,), (1,)), ((), ())),
                     preferred_element_type=F32,
                 )
-                cell_ref[target] += one[:tall] + (one[tall:] + two)
+                cell_ref[target] += one[:tall] + (one[tall:] + two[:tall])
 
     for j in range(cells):
         cell = cell_ref[j]
@@ -241,9 +243,7 @@
         scale = coef / (1.0 + coef * (cell[gain_row:gain_row + 1, :] + land))
         flux = scale * (surface_ref[j] - cell)
         flux_ref[j] = flux
-        high, low = split(flux)
-        two_ref[j, :tall, :] = high
-        two_ref[j, tall:, :] = low
+        two_ref[j] = split(flux)
 
     @pl.loop(0, margins // unroll)
     def _(step):
@@ -252,14 +252,14 @@
             target = jnp.where(k < count, slot_ref[k], sources * slots)
             one = jnp.dot(two_ref[block_ref[k]], weight_ref[k, :columns], preferred_element_type=F32)
             two = jnp.dot(
-                two_ref[block_ref[k], :tall], weight_ref[k, columns:], preferred_element_type=F32
+                two_ref[block_ref[k], :top], weight_ref[k, columns:], preferred_element_type=F32
             )
-            back_ref[target] += one[:tall] + (one[tall:] + two)
+            back_ref[target] += one[:tall] + (one[tall:] + two[:tall])
 
     for a in range(sources):
         for p in range(slots):
             for g in range(groups):
-                reply_ref[a * groups + g, p * rows:(p + 1) * rows, :] = (
+                reply_ref[pl.ds((a * groups + g) * rows * slots + p, rows, stride=slots), :] = (
                     back_ref[a * slots + p, g * rows:(g + 1) * rows, :]
                 )
 
@@ -268,7 +268,8 @@
                   groups, rows, slots, gain_row):
     half, twice, columns = weights_a.shape
     margins = 2 * half
-    owners, _, width = got.shape
+    width = got.shape[1]
+    owners = got.shape[0] // (rows * slots)
     cells, tall, _ = surface.shape
     sources = owners // groups
     chunks = 6
@@ -287,6 +288,7 @@
             pltpu.VMEM((cells + 1, tall, width), F32),
             pltpu.VMEM((cells, 2 * tall, width), BF16),
             pltpu.VMEM((sources * slots + 1, tall, width), F32),
+            pltpu.VMEM((sources * slots, tall, width), F32),
             pltpu.SemaphoreType.DMA((chunks,)),
         ],
         compiler_params=params(ROOMY),
@@ -295,41 +297,68 @@
     )(slot, block, count, weights_a, weights_b, got, surface, coef, mask, land)
 
 
-def finish_kernel(groups, own, rows, me_ref, place_ref, answer_ref, *refs):
-    parts, gains, fields_ref, out_ref, held_ref, factor_ref, gain_ref, flux_ref, sem, out_sem = (
+def unfold_kernel(groups, own, *refs):
+    firsts, seconds, after_ref, factor_ref, gain_ref = (
         refs[:groups], refs[groups:2 * groups], *refs[2 * groups:]
     )
+    levels = factor_ref.shape[0] // 3
+    for q in range(groups):
+        factor_ref[:levels, q * own:(q + 1) * own, :] = firsts[q][:levels]
+        factor_ref[2 * levels:, q * own:(q + 1) * own, :] = seconds[q][...]
+        gain_ref[q * own:(q + 1) * own, :] = firsts[q][levels]
+    above = factor_ref[2 * levels]
+    inverse = 1.0 - above
+    factor_ref[levels] = inverse
+    for k in range(1, levels):
+        carry = factor_ref[2 * levels + k]
+        inverse = (1.0 - carry) * inverse / (inverse + factor_ref[k] * (1.0 - above))
+        factor_ref[levels + k] = inverse
+        above = carry
+
+
+def unfold(firsts, seconds, after):
+    levels, own, width = seconds[0].shape
+    groups = len(seconds)
+    blocks = groups * own
+    return pl.pallas_call(
+        functools.partial(unfold_kernel, groups, own),
+        out_shape=(
+            jax.ShapeDtypeStruct((3 * levels, blocks, width), F32),
+            jax.ShapeDtypeStruct((blocks, width), F32),
+        ),
+        in_specs=[vmem()] * (2 * groups) + [hbm()],
+        out_specs=(vmem(), vmem()),
+        compiler_params=params(ROOMY),
+        cost_estimate=pl.CostEstimate(flops=1000000, bytes_accessed=3000000, transcendentals=100000),
+        name="unfold",
+    )(*firsts, *seconds, after)
+
+
+def finish_kernel(groups, own, rows, slots, me_ref, place_ref, answer_ref, factor_ref, gain_ref,
+                  fields_ref, out_ref, held_ref, flux_ref, sem, out_sem):
     me = me_ref[0]
     fetch_fields(me, groups, own, fields_ref, held_ref, sem)
-    shares, levels, blocks, width = held_ref.shape
-    for q in range(groups):
-        factor_ref[levels:, q * own:(q + 1) * own, :] = parts[q][...]
-        gain_ref[q * own:(q + 1) * own, :] = gains[q][levels]
-    above = jnp.zeros((blocks, width), F32)
-    for k in range(levels):
-        carry = factor_ref[2 * levels + k]
-        factor_ref[k] = 1.0 - carry - factor_ref[levels + k] * (1.0 - above)
-        above = carry
+    shares, levels, blocks, _ = held_ref.shape
     flux_ref[...] = jnp.zeros_like(flux_ref)
-    owners, slot_rows = answer_ref.shape[:2]
-    slots = slot_rows // rows
-    for d in range(owners):
+    pitch = round_up(rows, ROWS)
+    for d in range(answer_ref.shape[0] // (rows * slots)):
         for p in range(slots):
-            start = pl.multiple_of(place_ref[d * slots + p] * rows, rows)
-            flux_ref[pl.ds(start, rows), :] += answer_ref[d, p * rows:(p + 1) * rows, :]
+            start = pl.multiple_of(place_ref[d * slots + p] * pitch, pitch)
+            flux_ref[pl.ds(start, rows), :] += (
+                answer_ref[pl.ds(d * rows * slots + p, rows, stride=slots), :]
+            )
     for f in range(shares):
-        flux = flux_ref[pl.ds(f, blocks, stride=rows), :]
+        flux = flux_ref[pl.ds(f, blocks, stride=pitch), :]
         pltpu.make_async_copy(held_ref.at[f], held_ref.at[f], sem.at[f]).wait()
-        state = factor_ref[0] * held_ref[f, 0]
-        held_ref[f, 0] = state
+        state = held_ref[f, 0]
         for k in range(1, levels):
-            state = factor_ref[k] * held_ref[f, k] + factor_ref[levels + k] * state
+            state = held_ref[f, k] + factor_ref[k] * state
             if k < levels - 1:
                 held_ref[f, k] = state
-        state = state + gain_ref[...] * flux
+        state = factor_ref[2 * levels - 1] * state + gain_ref[...] * flux
         held_ref[f, levels - 1] = state
         for k in range(levels - 2, -1, -1):
-            state = held_ref[f, k] + factor_ref[2 * levels + k] * state
+            state = factor_ref[levels + k] * held_ref[f, k] + factor_ref[2 * levels + k] * state
             held_ref[f, k] = state
         for q in range(groups):
             base = lax.rem(me - q + groups, groups) * own
@@ -341,26 +370,23 @@
         pltpu.make_async_copy(held_ref.at[f], held_ref.at[f], out_sem.at[f]).wait()
 
 
-def finish(me, place, answer, parts, gains, fields, rows):
+def finish(me, place, answer, factor, gain, fields, groups, rows, slots):
     blocks, shares, levels, width = fields.shape
-    groups = len(parts)
-    return pl.pallas_call(
-        functools.partial(finish_kernel, groups, blocks // groups, rows),
+    return pl.pallas_call(
+        functools.partial(finish_kernel, groups, blocks // groups, rows, slots),
         out_shape=jax.ShapeDtypeStruct((blocks, shares, levels, width), F32),
-        in_specs=[smem(), smem(), vmem()] + [vmem()] * (2 * groups) + [hbm()],
+        in_specs=[smem(), smem(), vmem(), vmem(), vmem(), hbm()],
         out_specs=hbm(),
         scratch_shapes=[
             pltpu.VMEM((shares, levels, blocks, width), F32),
-            pltpu.VMEM((3 * levels, blocks, width), F32),
-            pltpu.VMEM((blocks, width), F32),
-            pltpu.VMEM(((blocks + 1) * rows, width), F32),
+            pltpu.VMEM(((blocks + 1) * round_up(rows, ROWS), width), F32),
             pltpu.SemaphoreType.DMA((shares,)),
             pltpu.SemaphoreType.DMA((shares,)),
         ],
         compiler_params=params(ROOMY),
         cost_estimate=pl.CostEstimate(flops=8000000, bytes_accessed=12000000, transcendentals=0),
         name="finish",
-    )(me, place, answer, *parts, *gains, fields)
+    )(me, place, answer, factor, gain, fields)
 
 
 def per_device(
@@ -371,7 +397,7 @@
     me = lax.axis_index("xg").astype(jnp.int32)
     blocks, _, shares, width = fields_now.shape
     own = blocks // groups
-    rows = round_up(shares + 1, ROWS)
+    rows = shares + 1
     owners, slots = route.shape[1:]
     cells = surface_value.shape[0]
 
@@ -380,6 +406,11 @@
 
     def shared(array):
         return [array] + [shift(array, by) for by in range(1, groups)]
+
+    def exchange(array):
+        array = array.reshape(owners, rows, slots, width)
+        array = lax.all_to_all(array, ("atm", "xg"), split_axis=0, concat_axis=0, tiled=True)
+        return array.reshape(owners * rows * slots, width)
 
     fields = fields_now.transpose(0, 2, 1, 3)
     first, second = factors(upper, lower, surface_gain)
@@ -398,17 +429,18 @@
         ((0, 0), (0, 0), (0, rows - shares), (0, 0)),
     ).reshape(cells, groups * rows, width)
     send = bottoms(me, place, firsts, fields, owners, slots, rows)
-    got = lax.all_to_all(send, ("atm", "xg"), split_axis=0, concat_axis=0, tiled=True)
+    got = exchange(send)
     seconds = shared(second)
     reply, flux = margins_stage(
         margin_slot[0], margin_block[0], margin_count, weights_a, weights_b, got, surface,
         exchange_coef, land_mask, land_gain, groups, rows, slots, shares,
     )
-    answer = lax.all_to_all(reply, ("atm", "xg"), split_axis=0, concat_axis=0, tiled=True)
+    answer = exchange(reply)
     surface_flux = flux.reshape(cells, groups, rows, width)[:, :, :shares].reshape(
         cells, groups * shares, width
     )
-    out = finish(me, place, answer, seconds, firsts, fields, rows)
+    factor, gain = unfold(firsts, seconds, reply)
+    out = finish(me, place, answer, factor, gain, fields, groups, rows, slots)
     return out.transpose(0, 2, 1, 3), surface_flux
 
 

time: 90.2 us -> 80.7 us (0.89); the launches traced: 88.5 us -> 80.2 us
  waiting for transfers between devices: 28.9 us -> 20.1 us
    ppermute x6, waiting for transfers between devices: 26.2 us -> 18.6 us  [shift(): lax.ppermute(array, 'xg', [(i, (i + by) % groups) for i in range(groups)])]
    all_to_all x2, waiting for transfers between devices: 2.73 us -> 1.47 us  [exchange(): lax.all_to_all(array, ('atm', 'xg'), split_axis=0, concat_axis=0, tiled=T...]
    pallas_call x1 -> x2, Pallas kernels: 4.18 us -> 4.67 us  [the longest x1 4.17 us: bottoms(): pl.pallas_call(functools.partial(bottom_kernel, groups, own, rows, slots)...]
  transfers between devices with their start and end apart: 8 -> 8, of which waited for: 5 -> 5; matrix products, arithmetic and copies ran while one was open for 2% -> 2% of each run, Pallas kernels for 8% -> 10%
where the time goes in v4:
time: 80.7 us; the launch traced here: 80.2 us
  Pallas kernels  29.5 us (37%)
  starting transfers between devices  23 us (29%)
  waiting for transfers between devices  20.1 us (25%)
  local copies, waits for them, and re-layouts  6.14 us (8%)
  between operations  1.45 us (2%)
    ppermute x6, waiting for transfers between devices, shift(): lax.ppermute(array, 'xg', [(i, (i + by) % groups) for i in range(groups)])  18.6 us
    ppermute x6, starting transfers between devices, shift(): lax.ppermute(array, 'xg', [(i, (i + by) % groups) for i in range(groups)])  12.7 us
    all_to_all x2, starting transfers between devices, exchange(): lax.all_to_all(array, ('atm', 'xg'), split_axis=0, concat_axis=0, tiled=T...  10.3 us
    pallas_call x1, Pallas kernels, margins_stage(): pl.pallas_call(functools.partial(margin_kernel, groups, rows, slots, gain...  10.2 us
    pallas_call x2, Pallas kernels, split_weights(): pl.pallas_call(split_kernel, grid=(count // step,), out_shape=jax.ShapeDt...  7.29 us
    pallas_call x1, Pallas kernels, finish(): pl.pallas_call(functools.partial(finish_kernel, groups, blocks // groups,...  5.26 us
    unnamed x23, local copies, waits for them, and re-layouts  4.98 us
    pallas_call x1, Pallas kernels, bottoms(): pl.pallas_call(functools.partial(bottom_kernel, groups, own, rows, slots)...  4.17 us
  transfers between devices with their start and end apart: 8, of which 5 were waited for; matrix products, arithmetic and copies ran while one was open for 2% of the time, Pallas kernels for 10%

profile of v4, /device:TPU:0, one launch (start us, length us, event | category | flops | bytes accessed | tf_op | source)
XLA Modules:
  0.0 80.2 jit_solution(12916663907874636002)
XLA Ops:
  0.6 2.1 %factors.1 = (f32[49,4,128]{2,1,0:T(4,128)}, f32[48,4,128]{2,1,0:T(4,128)}) custom-call(f32[192,128]{1,0:T(8,128)} %bitcast.29, f32[192,128]{1,0:T(8,128)} %bitcast.30, f32[4,128]{1,0:T(4,128)} %gain_hbm.1), custom_call_target="tpu_custom_call" | custom-call | flops 1000000 | bytes 400000 | tf_op jit(solution)/shard_map/factors/pallas_call | solution.py:71
  2.7 3.1 %collective-permute-start = (f32[49,4,128]{2,1,0:T(4,128)}, f32[49,4,128]{2,1,0:T(4,128)S(1)}, u32[]{:S(2)}, u32[]{:S(2)}) collective-permute-start(f32[49,4,128]{2,1,0:T(4,128)} %get-tuple-element.8.refs_0_), channel_id=1, source_target_pairs={{0,1},{1,2},{2,3},{3,0},{4,5},{5,6},{6,7},{7,4},{8,9},{9,10},{10,1... | collective-permute-start | bytes 301064 | tf_op jit(solution)/shard_map/ppermute | solution.py:405
  5.8 2.6 %collective-permute-start.1 = (f32[49,4,128]{2,1,0:T(4,128)}, f32[49,4,128]{2,1,0:T(4,128)S(1)}, u32[]{:S(2)}, u32[]{:S(2)}) collective-permute-start(f32[49,4,128]{2,1,0:T(4,128)} %get-tuple-element.8.refs_0_), channel_id=1, source_target_pairs={{0,2},{1,3},{2,0},{3,1},{4,6},{5,7},{6,4},{7,5},{8,10},{9,11},{10,... | collective-permute-start | bytes 301064 | tf_op jit(solution)/shard_map/ppermute | solution.py:405
  8.4 1.3 %collective-permute-start.2 = (f32[49,4,128]{2,1,0:T(4,128)}, f32[49,4,128]{2,1,0:T(4,128)S(1)}, u32[]{:S(2)}, u32[]{:S(2)}) collective-permute-start(f32[49,4,128]{2,1,0:T(4,128)} %get-tuple-element.8.refs_0_), channel_id=1, source_target_pairs={{0,3},{1,0},{2,1},{3,2},{4,7},{5,4},{6,5},{7,6},{8,11},{9,8},{10,9... | collective-permute-start | bytes 301064 | tf_op jit(solution)/shard_map/ppermute | solution.py:405
  9.8 0.8 copy.18
  10.5 0.1 reshape_squeeze.3
  10.6 1.1 %collective-permute-done.refs_1_ = f32[49,4,128]{2,1,0:T(4,128)S(1)} collective-permute-done((f32[49,4,128]{2,1,0:T(4,128)}, f32[49,4,128]{2,1,0:T(4,128)S(1)}, u32[]{:S(2)}, u32[]{:S(2)}) %collective-permute-start) | collective-permute-done | bytes 100384 | tf_op jit(solution)/shard_map/ppermute | solution.py:405
  11.8 3.5 %collective-permute-done.1.refs_2_ = f32[49,4,128]{2,1,0:T(4,128)S(1)} collective-permute-done((f32[49,4,128]{2,1,0:T(4,128)}, f32[49,4,128]{2,1,0:T(4,128)S(1)}, u32[]{:S(2)}, u32[]{:S(2)}) %collective-permute-start.1) | collective-permute-done | bytes 100384 | tf_op jit(solution)/shard_map/ppermute | solution.py:405
  15.3 0.0 collective-permute-done.2.refs_3_
  15.3 0.0 copy-start.2
  15.3 0.9 %copy-done.2 = f32[49,4,128]{2,1,0:T(4,128)S(1)} copy-done((f32[49,4,128]{2,1,0:T(4,128)S(1)}, f32[49,4,128]{2,1,0:T(4,128)}, u32[]{:S(2)}) %copy-start.2) | copy-done | bytes 100376
  16.2 0.0 copy-start.10
  16.2 4.2 %bottoms.1 = f32[896,128]{1,0:T(8,128)} custom-call(s32[1]{0:T(128)} %bitcast.me_ref, s32[64]{0:T(128)S(1)} %compare_select_fusion.2.place_ref, f32[49,4,128]{2,1,0:T(4,128)S(1)} %copy-done.2, f32[49,4,128]{2,1,0:T(4,128)S(1)} %collective-permute-done.refs_1_, f32[49,4,128]{2,1,0:T(4,128)S(1)} %collective-permute-done.1.refs_2_, ...), custom_call_target="tpu_custom_call" | custom-call | flops 4000000 | bytes 7000000 | tf_op jit(solution)/shard_map/bottoms/pallas_call | solution.py:141
  20.4 5.9 %all-to-all-start = ((f32[32,14,2,128]{3,2,1,0:T(2,128)}), f32[32,14,2,128]{3,2,1,0:T(2,128)S(1)}, u32[]{:S(2)}, u32[]{:S(2)}) async-start(f32[32,14,2,128]{3,2,1,0:T(2,128)} %bitcast.7), calls=%async_computation | async-start | bytes 917504 | tf_op jit(solution)/shard_map/all_to_all | solution.py:412
  26.3 0.0 copy-done.10
  26.4 0.2 copy.19.surface_ref
  27.2 3.6 %split_weights.2.weight_a = bf16[48,256,128]{2,1,0:T(8,128)(2,1)S(1)} custom-call(f32[96,128,128]{2,1,0:T(8,128)} %bitcast.20), custom_call_target="tpu_custom_call" | custom-call | flops 2500000 | bytes 6500000 | tf_op jit(solution)/shard_map/split_weights/pallas_call | solution.py:173
  30.8 0.0 copy-start
  30.8 1.7 %copy-done = bf16[48,256,128]{2,1,0:T(8,128)(2,1)} copy-done((bf16[48,256,128]{2,1,0:T(8,128)(2,1)}, bf16[48,256,128]{2,1,0:T(8,128)(2,1)S(1)}, u32[]{:S(2)}) %copy-start) | copy-done | bytes 3145752
  32.5 0.0 copy-start.5
  32.5 0.0 copy-start.6
  32.5 0.0 copy-start.7
  32.5 0.0 copy-start.8
  32.5 0.0 copy-start.9
  32.5 3.7 %split_weights.3.weight_b = bf16[48,256,128]{2,1,0:T(8,128)(2,1)S(1)} custom-call(f32[96,128,128]{2,1,0:T(8,128)} %bitcast.21), custom_call_target="tpu_custom_call" | custom-call | flops 2500000 | bytes 6500000 | tf_op jit(solution)/shard_map/split_weights/pallas_call | solution.py:173
  36.2 0.0 copy-start.1
  36.2 1.6 %copy-done.1 = bf16[48,256,128]{2,1,0:T(8,128)(2,1)} copy-done((bf16[48,256,128]{2,1,0:T(8,128)(2,1)}, bf16[48,256,128]{2,1,0:T(8,128)(2,1)S(1)}, u32[]{:S(2)}) %copy-start.1) | copy-done | bytes 3145752
  37.8 0.0 copy-start.4
  37.8 0.0 copy-start.3
  37.8 1.5 %all-to-all-done = f32[32,14,2,128]{3,2,1,0:T(2,128)S(1)} async-done(((f32[32,14,2,128]{3,2,1,0:T(2,128)}), f32[32,14,2,128]{3,2,1,0:T(2,128)S(1)}, u32[]{:S(2)}, u32[]{:S(2)}) %all-to-all-start) | async-done | bytes 458784 | tf_op jit(solution)/shard_map/all_to_all | solution.py:412
  39.3 0.0 copy-done.5
  39.3 0.0 copy-done.6
  39.3 0.0 copy-done.7
  39.3 0.0 copy-done.8
  39.3 0.0 copy-done.9
  39.3 10.2 %margins.1 = (f32[896,128]{1,0:T(8,128)}, f32[16,56,128]{2,1,0:T(8,128)S(1)}) custom-call(s32[96]{0:T(128)S(1)} %bitcast.18, s32[96]{0:T(128)S(1)} %bitcast.19, s32[1]{0:T(128)S(6)} %copy.21.count_ref, bf16[48,256,128]{2,1,0:T(8,128)(2,1)} %copy-done, bf16[48,256,128]{2,1,0:T(8,128)(2,1)} %copy-done.1, f32[896,128]{1,0:T(8,128)S(1)} %bitcast.16, ...), custom_call_target="tpu_custom_call" | custom-call | flops 800000000 | bytes 8000000 | tf_op jit(solution)/shard_map/margins/pallas_call | solution.py:277
  49.6 4.4 %all-to-all-start.1 = ((f32[32,14,2,128]{3,2,1,0:T(2,128)}), f32[32,14,2,128]{3,2,1,0:T(2,128)S(1)}, u32[]{:S(2)}, u32[]{:S(2)}) async-start(f32[32,14,2,128]{3,2,1,0:T(2,128)} %bitcast.11), calls=%async_computation.1 | async-start | bytes 917504 | tf_op jit(solution)/shard_map/all_to_all | solution.py:412
  53.9 0.0 copy-done.4
  53.9 1.8 %collective-permute-start.3 = (f32[48,4,128]{2,1,0:T(4,128)S(1)}, f32[48,4,128]{2,1,0:T(4,128)S(1)}, u32[]{:S(2)}, u32[]{:S(2)}) collective-permute-start(f32[48,4,128]{2,1,0:T(4,128)S(1)} %copy-done.4), channel_id=1, source_target_pairs={{0,1},{1,2},{2,3},{3,0},{4,5},{5,6},{6,7},{7,4},{8,9},{9,10},{10,1... | collective-permute-start | bytes 294920 | tf_op jit(solution)/shard_map/ppermute | solution.py:405
  55.8 2.4 %collective-permute-start.4 = (f32[48,4,128]{2,1,0:T(4,128)S(1)}, f32[48,4,128]{2,1,0:T(4,128)S(1)}, u32[]{:S(2)}, u32[]{:S(2)}) collective-permute-start(f32[48,4,128]{2,1,0:T(4,128)S(1)} %copy-done.4), channel_id=1, source_target_pairs={{0,2},{1,3},{2,0},{3,1},{4,6},{5,7},{6,4},{7,5},{8,10},{9,11},{10,... | collective-permute-start | bytes 294920 | tf_op jit(solution)/shard_map/ppermute | solution.py:405
  58.2 1.4 %collective-permute-start.5 = (f32[48,4,128]{2,1,0:T(4,128)S(1)}, f32[48,4,128]{2,1,0:T(4,128)S(1)}, u32[]{:S(2)}, u32[]{:S(2)}) collective-permute-start(f32[48,4,128]{2,1,0:T(4,128)S(1)} %copy-done.4), channel_id=1, source_target_pairs={{0,3},{1,0},{2,1},{3,2},{4,7},{5,4},{6,5},{7,6},{8,11},{9,8},{10,9... | collective-permute-start | bytes 294920 | tf_op jit(solution)/shard_map/ppermute | solution.py:405
  59.6 0.1 copy.20
  59.7 0.8 slice.4
  60.5 8.2 %collective-permute-done.3.refs_5_ = f32[48,4,128]{2,1,0:T(4,128)S(1)} collective-permute-done((f32[48,4,128]{2,1,0:T(4,128)S(1)}, f32[48,4,128]{2,1,0:T(4,128)S(1)}, u32[]{:S(2)}, u32[]{:S(2)}) %collective-permute-start.3) | collective-permute-done | bytes 98336 | tf_op jit(solution)/shard_map/ppermute | solution.py:405
  68.7 5.7 %collective-permute-done.4.refs_6_ = f32[48,4,128]{2,1,0:T(4,128)S(1)} collective-permute-done((f32[48,4,128]{2,1,0:T(4,128)S(1)}, f32[48,4,128]{2,1,0:T(4,128)S(1)}, u32[]{:S(2)}, u32[]{:S(2)}) %collective-permute-start.4) | collective-permute-done | bytes 98336 | tf_op jit(solution)/shard_map/ppermute | solution.py:405
  74.4 0.0 collective-permute-done.5.refs_7_
  74.4 0.0 copy-done.3
  74.4 0.5 unfold.1
  74.9 0.0 all-to-all-done.1
  74.9 5.3 %finish.1 = f32[16,13,48,128]{3,2,1,0:T(8,128)} custom-call(s32[1]{0:T(128)} %bitcast.me_ref, s32[64]{0:T(128)S(1)} %compare_select_fusion.2.place_ref, f32[896,128]{1,0:T(8,128)S(1)} %bitcast.17, f32[144,16,128]{2,1,0:T(8,128)S(1)} %get-tuple-element.11.factor_ref, f32[16,128]{1,0:T(8,128)S(1)} %get-tuple-element.12.gain_ref, f32[16,13,48,128]{3,2,1,0:T(8,128)} %bitcast.23), custom_call_target="tpu_custom_call" | custom-call | flops 8000000 | bytes 12000000 | tf_op jit(solution)/shard_map/finish/pallas_call | solution.py:375
  (2 shorter events, 0.1 us)
Async XLA Ops:
  2.7 9.1 %collective-permute-start = (f32[49,4,128]{2,1,0:T(4,128)}, f32[49,4,128]{2,1,0:T(4,128)S(1)}, u32[]{:S(2)}, u32[]{:S(2)}) collective-permute-start(f32[49,4,128]{2,1,0:T(4,128)} %get-tuple-element.8.refs_0_), channel_id=1, source_target_pairs={{0,1},{1,2},{2,3},{3,0},{4,5},{5,6},{6,7},{7,4},{8,9},{9,10},{10,1... | collective-permute-start | bytes 301064 | tf_op jit(solution)/shard_map/ppermute | solution.py:405
  5.8 9.5 %collective-permute-start.1 = (f32[49,4,128]{2,1,0:T(4,128)}, f32[49,4,128]{2,1,0:T(4,128)S(1)}, u32[]{:S(2)}, u32[]{:S(2)}) collective-permute-start(f32[49,4,128]{2,1,0:T(4,128)} %get-tuple-element.8.refs_0_), channel_id=1, source_target_pairs={{0,2},{1,3},{2,0},{3,1},{4,6},{5,7},{6,4},{7,5},{8,10},{9,11},{10,... | collective-permute-start | bytes 301064 | tf_op jit(solution)/shard_map/ppermute | solution.py:405
  8.4 6.9 %collective-permute-start.2 = (f32[49,4,128]{2,1,0:T(4,128)}, f32[49,4,128]{2,1,0:T(4,128)S(1)}, u32[]{:S(2)}, u32[]{:S(2)}) collective-permute-start(f32[49,4,128]{2,1,0:T(4,128)} %get-tuple-element.8.refs_0_), channel_id=1, source_target_pairs={{0,3},{1,0},{2,1},{3,2},{4,7},{5,4},{6,5},{7,6},{8,11},{9,8},{10,9... | collective-permute-start | bytes 301064 | tf_op jit(solution)/shard_map/ppermute | solution.py:405
  15.3 0.9 %copy-start.2 = (f32[49,4,128]{2,1,0:T(4,128)S(1)}, f32[49,4,128]{2,1,0:T(4,128)}, u32[]{:S(2)}) copy-start(f32[49,4,128]{2,1,0:T(4,128)} %get-tuple-element.8.refs_0_) | copy-start | bytes 301060
  16.2 10.1 %copy-start.10 = (f32[16,52,128]{2,0,1:T(8,128)S(1)}, f32[16,52,128]{2,0,1:T(8,128)}, u32[]{:S(2)}) copy-start(f32[16,52,128]{2,0,1:T(8,128)} %param.22) | copy-start | bytes 1277956
  20.4 18.9 %all-to-all-start = ((f32[32,14,2,128]{3,2,1,0:T(2,128)}), f32[32,14,2,128]{3,2,1,0:T(2,128)S(1)}, u32[]{:S(2)}, u32[]{:S(2)}) async-start(f32[32,14,2,128]{3,2,1,0:T(2,128)} %bitcast.7), calls=%async_computation | async-start | bytes 917504 | tf_op jit(solution)/shard_map/all_to_all | solution.py:412
  30.8 1.7 %copy-start = (bf16[48,256,128]{2,1,0:T(8,128)(2,1)}, bf16[48,256,128]{2,1,0:T(8,128)(2,1)S(1)}, u32[]{:S(2)}) copy-start(bf16[48,256,128]{2,1,0:T(8,128)(2,1)S(1)} %split_weights.2.weight_a) | copy-start | bytes 9437188
  32.5 6.8 %copy-start.5 = (f32[16,128]{1,0:T(8,128)S(1)}, f32[16,128]{1,0:T(8,128)}, u32[]{:S(2)}) copy-start(f32[16,128]{1,0:T(8,128)} %coef_ref.1) | copy-start | bytes 24580
  32.5 6.8 %copy-start.6 = (s32[16,128]{1,0:T(8,128)S(1)}, s32[16,128]{1,0:T(8,128)}, u32[]{:S(2)}) copy-start(s32[16,128]{1,0:T(8,128)} %mask_ref.1) | copy-start | bytes 24580
  32.5 6.8 %copy-start.7 = (f32[16,128]{1,0:T(8,128)S(1)}, f32[16,128]{1,0:T(8,128)}, u32[]{:S(2)}) copy-start(f32[16,128]{1,0:T(8,128)} %land_ref.1) | copy-start | bytes 24580
  32.5 6.8 %copy-start.8 = (s32[1,96]{1,0:T(1,128)S(1)}, s32[1,96]{1,0:T(1,128)}, u32[]{:S(2)}) copy-start(s32[1,96]{1,0:T(1,128)} %param.18) | copy-start | bytes 1156
  32.5 6.8 %copy-start.9 = (s32[1,96]{1,0:T(1,128)S(1)}, s32[1,96]{1,0:T(1,128)}, u32[]{:S(2)}) copy-start(s32[1,96]{1,0:T(1,128)} %param.19) | copy-start | bytes 1156
  36.2 1.6 %copy-start.1 = (bf16[48,256,128]{2,1,0:T(8,128)(2,1)}, bf16[48,256,128]{2,1,0:T(8,128)(2,1)S(1)}, u32[]{:S(2)}) copy-start(bf16[48,256,128]{2,1,0:T(8,128)(2,1)S(1)} %split_weights.3.weight_b) | copy-start | bytes 9437188
  37.8 16.1 %copy-start.4 = (f32[48,4,128]{2,1,0:T(4,128)S(1)}, f32[48,4,128]{2,1,0:T(4,128)}, u32[]{:S(2)}) copy-start(f32[48,4,128]{2,1,0:T(4,128)} %get-tuple-element.10.refs_4_) | copy-start | bytes 294916
  37.8 36.6 %copy-start.3 = (f32[49,4,128]{2,1,0:T(4,128)S(1)}, f32[49,4,128]{2,1,0:T(4,128)}, u32[]{:S(2)}) copy-start(f32[49,4,128]{2,1,0:T(4,128)} %get-tuple-element.8.refs_0_) | copy-start | bytes 301060
  49.6 25.4 %all-to-all-start.1 = ((f32[32,14,2,128]{3,2,1,0:T(2,128)}), f32[32,14,2,128]{3,2,1,0:T(2,128)S(1)}, u32[]{:S(2)}, u32[]{:S(2)}) async-start(f32[32,14,2,128]{3,2,1,0:T(2,128)} %bitcast.11), calls=%async_computation.1 | async-start | bytes 917504 | tf_op jit(solution)/shard_map/all_to_all | solution.py:412
  53.9 14.7 %collective-permute-start.3 = (f32[48,4,128]{2,1,0:T(4,128)S(1)}, f32[48,4,128]{2,1,0:T(4,128)S(1)}, u32[]{:S(2)}, u32[]{:S(2)}) collective-permute-start(f32[48,4,128]{2,1,0:T(4,128)S(1)} %copy-done.4), channel_id=1, source_target_pairs={{0,1},{1,2},{2,3},{3,0},{4,5},{5,6},{6,7},{7,4},{8,9},{9,10},{10,1... | collective-permute-start | bytes 294920 | tf_op jit(solution)/shard_map/ppermute | solution.py:405
  55.8 18.6 %collective-permute-start.4 = (f32[48,4,128]{2,1,0:T(4,128)S(1)}, f32[48,4,128]{2,1,0:T(4,128)S(1)}, u32[]{:S(2)}, u32[]{:S(2)}) collective-permute-start(f32[48,4,128]{2,1,0:T(4,128)S(1)} %copy-done.4), channel_id=1, source_target_pairs={{0,2},{1,3},{2,0},{3,1},{4,6},{5,7},{6,4},{7,5},{8,10},{9,11},{10,... | collective-permute-start | bytes 294920 | tf_op jit(solution)/shard_map/ppermute | solution.py:405
  58.2 16.2 %collective-permute-start.5 = (f32[48,4,128]{2,1,0:T(4,128)S(1)}, f32[48,4,128]{2,1,0:T(4,128)S(1)}, u32[]{:S(2)}, u32[]{:S(2)}) collective-permute-start(f32[48,4,128]{2,1,0:T(4,128)S(1)} %copy-done.4), channel_id=1, source_target_pairs={{0,3},{1,0},{2,1},{3,2},{4,7},{5,4},{6,5},{7,6},{8,11},{9,8},{10,9... | collective-permute-start | bytes 294920 | tf_op jit(solution)/shard_map/ppermute | solution.py:405

commit v5 on v4

--- a/solution.py
+++ b/solution.py
@@ -430,7 +430,10 @@
     ).reshape(cells, groups * rows, width)
     send = bottoms(me, place, firsts, fields, owners, slots, rows)
     got = exchange(send)
-    seconds = shared(second)
+    up, down = shift(second, 1), shift(second, groups - 1)
+    seconds = [second, up] + [None] * (groups - 3) + [down]
+    for by in range(groups - 2, 1, -1):
+        seconds[by] = shift(seconds[by + 1], groups - 1)
     reply, flux = margins_stage(
         margin_slot[0], margin_block[0], margin_count, weights_a, weights_b, got, surface,
         exchange_coef, land_mask, land_gain, groups, rows, slots, shares,

time: 80.7 us -> 81.2 us (level)
  starting transfers between devices: 23 us -> 24.8 us
  waiting for transfers between devices: 20.1 us -> 18.7 us
    ppermute x6, starting transfers between devices: 12.7 us -> 14.6 us  [shift(): lax.ppermute(array, 'xg', [(i, (i + by) % groups) for i in range(groups)])]
    ppermute x6, waiting for transfers between devices: 18.6 us -> 17.2 us  [shift(): lax.ppermute(array, 'xg', [(i, (i + by) % groups) for i in range(groups)])]
  transfers between devices with their start and end apart: 8 -> 8, of which waited for: 5 -> 6; matrix products, arithmetic and copies ran while one was open for 2% -> 2% of each run, Pallas kernels for 10% -> 10%
where the time goes in v5:
time: 81.2 us; the launch traced here: 80.6 us
  Pallas kernels  29.5 us (36%)
  starting transfers between devices  24.8 us (31%)
  waiting for transfers between devices  18.7 us (23%)
  local copies, waits for them, and re-layouts  6.14 us (8%)
  between operations  1.45 us (2%)
    ppermute x6, waiting for transfers between devices, shift(): lax.ppermute(array, 'xg', [(i, (i + by) % groups) for i in range(groups)])  17.2 us
    ppermute x6, starting transfers between devices, shift(): lax.ppermute(array, 'xg', [(i, (i + by) % groups) for i in range(groups)])  14.6 us
    all_to_all x2, starting transfers between devices, exchange(): lax.all_to_all(array, ('atm', 'xg'), split_axis=0, concat_axis=0, tiled=T...  10.3 us
    pallas_call x1, Pallas kernels, margins_stage(): pl.pallas_call(functools.partial(margin_kernel, groups, rows, slots, gain...  10.2 us
    pallas_call x2, Pallas kernels, split_weights(): pl.pallas_call(split_kernel, grid=(count // step,), out_shape=jax.ShapeDt...  7.29 us
    pallas_call x1, Pallas kernels, finish(): pl.pallas_call(functools.partial(finish_kernel, groups, blocks // groups,...  5.26 us
    unnamed x23, local copies, waits for them, and re-layouts  4.98 us
    pallas_call x1, Pallas kernels, bottoms(): pl.pallas_call(functools.partial(bottom_kernel, groups, own, rows, slots)...  4.17 us
  transfers between devices with their start and end apart: 8, of which 6 were waited for; matrix products, arithmetic and copies ran while one was open for 2% of the time, Pallas kernels for 10%

profile of v5, /device:TPU:0, one launch (start us, length us, event | category | flops | bytes accessed | tf_op | source)
XLA Modules:
  0.0 80.6 jit_solution(13567248863526508738)
XLA Ops:
  0.6 2.1 %factors.1 = (f32[49,4,128]{2,1,0:T(4,128)}, f32[48,4,128]{2,1,0:T(4,128)}) custom-call(f32[192,128]{1,0:T(8,128)} %bitcast.29, f32[192,128]{1,0:T(8,128)} %bitcast.30, f32[4,128]{1,0:T(4,128)} %gain_hbm.1), custom_call_target="tpu_custom_call" | custom-call | flops 1000000 | bytes 400000 | tf_op jit(solution)/shard_map/factors/pallas_call | solution.py:71
  2.7 3.1 %collective-permute-start = (f32[49,4,128]{2,1,0:T(4,128)}, f32[49,4,128]{2,1,0:T(4,128)S(1)}, u32[]{:S(2)}, u32[]{:S(2)}) collective-permute-start(f32[49,4,128]{2,1,0:T(4,128)} %get-tuple-element.8.refs_0_), channel_id=1, source_target_pairs={{0,1},{1,2},{2,3},{3,0},{4,5},{5,6},{6,7},{7,4},{8,9},{9,10},{10,1... | collective-permute-start | bytes 301064 | tf_op jit(solution)/shard_map/ppermute | solution.py:405
  5.8 2.6 %collective-permute-start.1 = (f32[49,4,128]{2,1,0:T(4,128)}, f32[49,4,128]{2,1,0:T(4,128)S(1)}, u32[]{:S(2)}, u32[]{:S(2)}) collective-permute-start(f32[49,4,128]{2,1,0:T(4,128)} %get-tuple-element.8.refs_0_), channel_id=1, source_target_pairs={{0,2},{1,3},{2,0},{3,1},{4,6},{5,7},{6,4},{7,5},{8,10},{9,11},{10,... | collective-permute-start | bytes 301064 | tf_op jit(solution)/shard_map/ppermute | solution.py:405
  8.4 1.3 %collective-permute-start.2 = (f32[49,4,128]{2,1,0:T(4,128)}, f32[49,4,128]{2,1,0:T(4,128)S(1)}, u32[]{:S(2)}, u32[]{:S(2)}) collective-permute-start(f32[49,4,128]{2,1,0:T(4,128)} %get-tuple-element.8.refs_0_), channel_id=1, source_target_pairs={{0,3},{1,0},{2,1},{3,2},{4,7},{5,4},{6,5},{7,6},{8,11},{9,8},{10,9... | collective-permute-start | bytes 301064 | tf_op jit(solution)/shard_map/ppermute | solution.py:405
  9.8 0.8 copy.18
  10.5 0.1 reshape_squeeze.3
  10.6 1.1 %collective-permute-done.refs_1_ = f32[49,4,128]{2,1,0:T(4,128)S(1)} collective-permute-done((f32[49,4,128]{2,1,0:T(4,128)}, f32[49,4,128]{2,1,0:T(4,128)S(1)}, u32[]{:S(2)}, u32[]{:S(2)}) %collective-permute-start) | collective-permute-done | bytes 100384 | tf_op jit(solution)/shard_map/ppermute | solution.py:405
  11.8 3.5 %collective-permute-done.1.refs_2_ = f32[49,4,128]{2,1,0:T(4,128)S(1)} collective-permute-done((f32[49,4,128]{2,1,0:T(4,128)}, f32[49,4,128]{2,1,0:T(4,128)S(1)}, u32[]{:S(2)}, u32[]{:S(2)}) %collective-permute-start.1) | collective-permute-done | bytes 100384 | tf_op jit(solution)/shard_map/ppermute | solution.py:405
  15.3 0.0 collective-permute-done.2.refs_3_
  15.3 0.0 copy-start.2
  15.3 0.9 %copy-done.2 = f32[49,4,128]{2,1,0:T(4,128)S(1)} copy-done((f32[49,4,128]{2,1,0:T(4,128)S(1)}, f32[49,4,128]{2,1,0:T(4,128)}, u32[]{:S(2)}) %copy-start.2) | copy-done | bytes 100376
  16.2 0.0 copy-start.10
  16.2 4.2 %bottoms.1 = f32[896,128]{1,0:T(8,128)} custom-call(s32[1]{0:T(128)} %bitcast.me_ref, s32[64]{0:T(128)S(1)} %compare_select_fusion.2.place_ref, f32[49,4,128]{2,1,0:T(4,128)S(1)} %copy-done.2, f32[49,4,128]{2,1,0:T(4,128)S(1)} %collective-permute-done.refs_1_, f32[49,4,128]{2,1,0:T(4,128)S(1)} %collective-permute-done.1.refs_2_, ...), custom_call_target="tpu_custom_call" | custom-call | flops 4000000 | bytes 7000000 | tf_op jit(solution)/shard_map/bottoms/pallas_call | solution.py:141
  20.4 5.9 %all-to-all-start = ((f32[32,14,2,128]{3,2,1,0:T(2,128)}), f32[32,14,2,128]{3,2,1,0:T(2,128)S(1)}, u32[]{:S(2)}, u32[]{:S(2)}) async-start(f32[32,14,2,128]{3,2,1,0:T(2,128)} %bitcast.7), calls=%async_computation | async-start | bytes 917504 | tf_op jit(solution)/shard_map/all_to_all | solution.py:412
  26.3 0.0 copy-done.10
  26.4 0.2 copy.19.surface_ref
  27.2 3.6 %split_weights.2.weight_a = bf16[48,256,128]{2,1,0:T(8,128)(2,1)S(1)} custom-call(f32[96,128,128]{2,1,0:T(8,128)} %bitcast.20), custom_call_target="tpu_custom_call" | custom-call | flops 2500000 | bytes 6500000 | tf_op jit(solution)/shard_map/split_weights/pallas_call | solution.py:173
  30.8 0.0 copy-start
  30.8 1.7 %copy-done = bf16[48,256,128]{2,1,0:T(8,128)(2,1)} copy-done((bf16[48,256,128]{2,1,0:T(8,128)(2,1)}, bf16[48,256,128]{2,1,0:T(8,128)(2,1)S(1)}, u32[]{:S(2)}) %copy-start) | copy-done | bytes 3145752
  32.5 0.0 copy-start.5
  32.5 0.0 copy-start.6
  32.5 0.0 copy-start.7
  32.5 0.0 copy-start.8
  32.5 0.0 copy-start.9
  32.5 3.7 %split_weights.3.weight_b = bf16[48,256,128]{2,1,0:T(8,128)(2,1)S(1)} custom-call(f32[96,128,128]{2,1,0:T(8,128)} %bitcast.21), custom_call_target="tpu_custom_call" | custom-call | flops 2500000 | bytes 6500000 | tf_op jit(solution)/shard_map/split_weights/pallas_call | solution.py:173
  36.2 0.0 copy-start.1
  36.2 1.6 %copy-done.1 = bf16[48,256,128]{2,1,0:T(8,128)(2,1)} copy-done((bf16[48,256,128]{2,1,0:T(8,128)(2,1)}, bf16[48,256,128]{2,1,0:T(8,128)(2,1)S(1)}, u32[]{:S(2)}) %copy-start.1) | copy-done | bytes 3145752
  37.8 0.0 copy-start.4
  37.8 0.0 copy-start.3
  37.8 1.5 %all-to-all-done = f32[32,14,2,128]{3,2,1,0:T(2,128)S(1)} async-done(((f32[32,14,2,128]{3,2,1,0:T(2,128)}), f32[32,14,2,128]{3,2,1,0:T(2,128)S(1)}, u32[]{:S(2)}, u32[]{:S(2)}) %all-to-all-start) | async-done | bytes 458784 | tf_op jit(solution)/shard_map/all_to_all | solution.py:412
  39.3 0.0 copy-done.5
  39.3 0.0 copy-done.6
  39.3 0.0 copy-done.7
  39.3 0.0 copy-done.8
  39.3 0.0 copy-done.9
  39.3 10.2 %margins.1 = (f32[896,128]{1,0:T(8,128)}, f32[16,56,128]{2,1,0:T(8,128)S(1)}) custom-call(s32[96]{0:T(128)S(1)} %bitcast.18, s32[96]{0:T(128)S(1)} %bitcast.19, s32[1]{0:T(128)S(6)} %copy.21.count_ref, bf16[48,256,128]{2,1,0:T(8,128)(2,1)} %copy-done, bf16[48,256,128]{2,1,0:T(8,128)(2,1)} %copy-done.1, f32[896,128]{1,0:T(8,128)S(1)} %bitcast.16, ...), custom_call_target="tpu_custom_call" | custom-call | flops 800000000 | bytes 8000000 | tf_op jit(solution)/shard_map/margins/pallas_call | solution.py:277
  49.6 4.4 %all-to-all-start.1 = ((f32[32,14,2,128]{3,2,1,0:T(2,128)}), f32[32,14,2,128]{3,2,1,0:T(2,128)S(1)}, u32[]{:S(2)}, u32[]{:S(2)}) async-start(f32[32,14,2,128]{3,2,1,0:T(2,128)} %bitcast.11), calls=%async_computation.1 | async-start | bytes 917504 | tf_op jit(solution)/shard_map/all_to_all | solution.py:412
  53.9 0.0 copy-done.4
  53.9 3.7 %collective-permute-start.4 = (f32[48,4,128]{2,1,0:T(4,128)S(1)}, f32[48,4,128]{2,1,0:T(4,128)S(1)}, u32[]{:S(2)}, u32[]{:S(2)}) collective-permute-start(f32[48,4,128]{2,1,0:T(4,128)S(1)} %copy-done.4), channel_id=1, source_target_pairs={{0,3},{1,0},{2,1},{3,2},{4,7},{5,4},{6,5},{7,6},{8,11},{9,8},{10,9... | collective-permute-start | bytes 294920 | tf_op jit(solution)/shard_map/ppermute | solution.py:405
  57.6 0.0 collective-permute-start.3
  57.6 7.3 %collective-permute-done.4.refs_7_ = f32[48,4,128]{2,1,0:T(4,128)S(1)} collective-permute-done((f32[48,4,128]{2,1,0:T(4,128)S(1)}, f32[48,4,128]{2,1,0:T(4,128)S(1)}, u32[]{:S(2)}, u32[]{:S(2)}) %collective-permute-start.4) | collective-permute-done | bytes 98336 | tf_op jit(solution)/shard_map/ppermute | solution.py:405
  64.9 3.8 %collective-permute-start.5 = (f32[48,4,128]{2,1,0:T(4,128)S(1)}, f32[48,4,128]{2,1,0:T(4,128)S(1)}, u32[]{:S(2)}, u32[]{:S(2)}) collective-permute-start(f32[48,4,128]{2,1,0:T(4,128)S(1)} %collective-permute-done.4.refs_7_), channel_id=1, source_target_pairs={{0,3},{1,0},{2,1},{3,2},{4,7},{5,4},{6,5},{7,6},{8,11},{9,8},{10,9... | collective-permute-start | bytes 294920 | tf_op jit(solution)/shard_map/ppermute | solution.py:405
  68.7 0.1 copy.20
  68.8 0.8 slice.4
  69.6 0.7 collective-permute-done.3.refs_5_
  70.3 4.6 %collective-permute-done.5.refs_6_ = f32[48,4,128]{2,1,0:T(4,128)S(1)} collective-permute-done((f32[48,4,128]{2,1,0:T(4,128)S(1)}, f32[48,4,128]{2,1,0:T(4,128)S(1)}, u32[]{:S(2)}, u32[]{:S(2)}) %collective-permute-start.5) | collective-permute-done | bytes 98336 | tf_op jit(solution)/shard_map/ppermute | solution.py:405
  74.9 0.0 copy-done.3
  74.9 0.5 unfold.1
  75.4 0.0 all-to-all-done.1
  75.4 5.3 %finish.1 = f32[16,13,48,128]{3,2,1,0:T(8,128)} custom-call(s32[1]{0:T(128)} %bitcast.me_ref, s32[64]{0:T(128)S(1)} %compare_select_fusion.2.place_ref, f32[896,128]{1,0:T(8,128)S(1)} %bitcast.17, f32[144,16,128]{2,1,0:T(8,128)S(1)} %get-tuple-element.11.factor_ref, f32[16,128]{1,0:T(8,128)S(1)} %get-tuple-element.12.gain_ref, f32[16,13,48,128]{3,2,1,0:T(8,128)} %bitcast.23), custom_call_target="tpu_custom_call" | custom-call | flops 8000000 | bytes 12000000 | tf_op jit(solution)/shard_map/finish/pallas_call | solution.py:375
  (2 shorter events, 0.1 us)
Async XLA Ops:
  2.7 9.1 %collective-permute-start = (f32[49,4,128]{2,1,0:T(4,128)}, f32[49,4,128]{2,1,0:T(4,128)S(1)}, u32[]{:S(2)}, u32[]{:S(2)}) collective-permute-start(f32[49,4,128]{2,1,0:T(4,128)} %get-tuple-element.8.refs_0_), channel_id=1, source_target_pairs={{0,1},{1,2},{2,3},{3,0},{4,5},{5,6},{6,7},{7,4},{8,9},{9,10},{10,1... | collective-permute-start | bytes 301064 | tf_op jit(solution)/shard_map/ppermute | solution.py:405
  5.8 9.5 %collective-permute-start.1 = (f32[49,4,128]{2,1,0:T(4,128)}, f32[49,4,128]{2,1,0:T(4,128)S(1)}, u32[]{:S(2)}, u32[]{:S(2)}) collective-permute-start(f32[49,4,128]{2,1,0:T(4,128)} %get-tuple-element.8.refs_0_), channel_id=1, source_target_pairs={{0,2},{1,3},{2,0},{3,1},{4,6},{5,7},{6,4},{7,5},{8,10},{9,11},{10,... | collective-permute-start | bytes 301064 | tf_op jit(solution)/shard_map/ppermute | solution.py:405
  8.4 6.9 %collective-permute-start.2 = (f32[49,4,128]{2,1,0:T(4,128)}, f32[49,4,128]{2,1,0:T(4,128)S(1)}, u32[]{:S(2)}, u32[]{:S(2)}) collective-permute-start(f32[49,4,128]{2,1,0:T(4,128)} %get-tuple-element.8.refs_0_), channel_id=1, source_target_pairs={{0,3},{1,0},{2,1},{3,2},{4,7},{5,4},{6,5},{7,6},{8,11},{9,8},{10,9... | collective-permute-start | bytes 301064 | tf_op jit(solution)/shard_map/ppermute | solution.py:405
  15.3 0.9 %copy-start.2 = (f32[49,4,128]{2,1,0:T(4,128)S(1)}, f32[49,4,128]{2,1,0:T(4,128)}, u32[]{:S(2)}) copy-start(f32[49,4,128]{2,1,0:T(4,128)} %get-tuple-element.8.refs_0_) | copy-start | bytes 301060
  16.2 10.1 %copy-start.10 = (f32[16,52,128]{2,0,1:T(8,128)S(1)}, f32[16,52,128]{2,0,1:T(8,128)}, u32[]{:S(2)}) copy-start(f32[16,52,128]{2,0,1:T(8,128)} %param.22) | copy-start | bytes 1277956
  20.4 18.9 %all-to-all-start = ((f32[32,14,2,128]{3,2,1,0:T(2,128)}), f32[32,14,2,128]{3,2,1,0:T(2,128)S(1)}, u32[]{:S(2)}, u32[]{:S(2)}) async-start(f32[32,14,2,128]{3,2,1,0:T(2,128)} %bitcast.7), calls=%async_computation | async-start | bytes 917504 | tf_op jit(solution)/shard_map/all_to_all | solution.py:412
  30.8 1.7 %copy-start = (bf16[48,256,128]{2,1,0:T(8,128)(2,1)}, bf16[48,256,128]{2,1,0:T(8,128)(2,1)S(1)}, u32[]{:S(2)}) copy-start(bf16[48,256,128]{2,1,0:T(8,128)(2,1)S(1)} %split_weights.2.weight_a) | copy-start | bytes 9437188
  32.5 6.8 %copy-start.5 = (f32[16,128]{1,0:T(8,128)S(1)}, f32[16,128]{1,0:T(8,128)}, u32[]{:S(2)}) copy-start(f32[16,128]{1,0:T(8,128)} %coef_ref.1) | copy-start | bytes 24580
  32.5 6.8 %copy-start.6 = (s32[16,128]{1,0:T(8,128)S(1)}, s32[16,128]{1,0:T(8,128)}, u32[]{:S(2)}) copy-start(s32[16,128]{1,0:T(8,128)} %mask_ref.1) | copy-start | bytes 24580
  32.5 6.8 %copy-start.7 = (f32[16,128]{1,0:T(8,128)S(1)}, f32[16,128]{1,0:T(8,128)}, u32[]{:S(2)}) copy-start(f32[16,128]{1,0:T(8,128)} %land_ref.1) | copy-start | bytes 24580
  32.5 6.8 %copy-start.8 = (s32[1,96]{1,0:T(1,128)S(1)}, s32[1,96]{1,0:T(1,128)}, u32[]{:S(2)}) copy-start(s32[1,96]{1,0:T(1,128)} %param.18) | copy-start | bytes 1156
  32.5 6.8 %copy-start.9 = (s32[1,96]{1,0:T(1,128)S(1)}, s32[1,96]{1,0:T(1,128)}, u32[]{:S(2)}) copy-start(s32[1,96]{1,0:T(1,128)} %param.19) | copy-start | bytes 1156
  36.2 1.6 %copy-start.1 = (bf16[48,256,128]{2,1,0:T(8,128)(2,1)}, bf16[48,256,128]{2,1,0:T(8,128)(2,1)S(1)}, u32[]{:S(2)}) copy-start(bf16[48,256,128]{2,1,0:T(8,128)(2,1)S(1)} %split_weights.3.weight_b) | copy-start | bytes 9437188
  37.8 16.1 %copy-start.4 = (f32[48,4,128]{2,1,0:T(4,128)S(1)}, f32[48,4,128]{2,1,0:T(4,128)}, u32[]{:S(2)}) copy-start(f32[48,4,128]{2,1,0:T(4,128)} %get-tuple-element.10.refs_4_) | copy-start | bytes 294916
  37.8 37.0 %copy-start.3 = (f32[49,4,128]{2,1,0:T(4,128)S(1)}, f32[49,4,128]{2,1,0:T(4,128)}, u32[]{:S(2)}) copy-start(f32[49,4,128]{2,1,0:T(4,128)} %get-tuple-element.8.refs_0_) | copy-start | bytes 301060
  49.6 25.8 %all-to-all-start.1 = ((f32[32,14,2,128]{3,2,1,0:T(2,128)}), f32[32,14,2,128]{3,2,1,0:T(2,128)S(1)}, u32[]{:S(2)}, u32[]{:S(2)}) async-start(f32[32,14,2,128]{3,2,1,0:T(2,128)} %bitcast.11), calls=%async_computation.1 | async-start | bytes 917504 | tf_op jit(solution)/shard_map/all_to_all | solution.py:412
  53.9 11.0 %collective-permute-start.4 = (f32[48,4,128]{2,1,0:T(4,128)S(1)}, f32[48,4,128]{2,1,0:T(4,128)S(1)}, u32[]{:S(2)}, u32[]{:S(2)}) collective-permute-start(f32[48,4,128]{2,1,0:T(4,128)S(1)} %copy-done.4), channel_id=1, source_target_pairs={{0,3},{1,0},{2,1},{3,2},{4,7},{5,4},{6,5},{7,6},{8,11},{9,8},{10,9... | collective-permute-start | bytes 294920 | tf_op jit(solution)/shard_map/ppermute | solution.py:405
  57.6 12.7 %collective-permute-start.3 = (f32[48,4,128]{2,1,0:T(4,128)S(1)}, f32[48,4,128]{2,1,0:T(4,128)S(1)}, u32[]{:S(2)}, u32[]{:S(2)}) collective-permute-start(f32[48,4,128]{2,1,0:T(4,128)S(1)} %copy-done.4), channel_id=1, source_target_pairs={{0,1},{1,2},{2,3},{3,0},{4,5},{5,6},{6,7},{7,4},{8,9},{9,10},{10,1... | collective-permute-start | bytes 294920 | tf_op jit(solution)/shard_map/ppermute | solution.py:405
  64.9 10.0 %collective-permute-start.5 = (f32[48,4,128]{2,1,0:T(4,128)S(1)}, f32[48,4,128]{2,1,0:T(4,128)S(1)}, u32[]{:S(2)}, u32[]{:S(2)}) collective-permute-start(f32[48,4,128]{2,1,0:T(4,128)S(1)} %collective-permute-done.4.refs_7_), channel_id=1, source_target_pairs={{0,3},{1,0},{2,1},{3,2},{4,7},{5,4},{6,5},{7,6},{8,11},{9,8},{10,9... | collective-permute-start | bytes 294920 | tf_op jit(solution)/shard_map/ppermute | solution.py:405

commit v6 on v4

--- a/solution.py
+++ b/solution.py
@@ -165,11 +165,11 @@
     out_ref[:, size:, :] = (value - high.astype(F32)).astype(BF16)
 
 
-def split_weights(weight, part, parts, step=8):
-    margins, cells, columns = weight.shape
-    count = margins // parts
-    step = math.gcd(step, count)
-    first = part * (count // step)
+def split_weights(weight, start, stop, step=8):
+    _, cells, columns = weight.shape
+    count = stop - start
+    step = math.gcd(step, math.gcd(start, count))
+    first = start // step
     return pl.pallas_call(
         split_kernel,
         grid=(count // step,),
@@ -191,12 +191,12 @@
     margins = weight_ref.shape[0]
     chunks = sem.shape[0]
     size = margins // chunks
-    half = chunks // 2
+    half = weight_a.shape[0] // size
 
     def fetch(c):
         source = weight_a if c < half else weight_b
         return pltpu.make_async_copy(
-            source.at[pl.ds(c % half * size, size)], weight_ref.at[pl.ds(c * size, size)], sem.at[c]
+            source.at[pl.ds((c if c < half else c - half) * size, size)], weight_ref.at[pl.ds(c * size, size)], sem.at[c]
         )
 
     for c in range(chunks):
@@ -266,8 +266,8 @@
 
 def margins_stage(slot, block, count, weights_a, weights_b, got, surface, coef, mask, land,
                   groups, rows, slots, gain_row):
-    half, twice, columns = weights_a.shape
-    margins = 2 * half
+    part, twice, columns = weights_a.shape
+    margins = part + weights_b.shape[0]
     width = got.shape[1]
     owners = got.shape[0] // (rows * slots)
     cells, tall, _ = surface.shape
@@ -415,6 +415,11 @@
     fields = fields_now.transpose(0, 2, 1, 3)
     first, second = factors(upper, lower, surface_gain)
     firsts = shared(first)
+    relayed = second
+    seconds = [second] + [None] * (groups - 1)
+    for by in range(groups - 1, 0, -1):
+        relayed = shift(relayed, groups - 1)
+        seconds[by] = relayed
     routing = route[0].reshape(owners * slots)
     place = jnp.where(
         routing < blocks,
@@ -422,15 +427,14 @@
         blocks,
     ).astype(jnp.int32)
     me = me[None]
-    weights_a = split_weights(margin_weight[0], 0, 2)
-    weights_b = split_weights(margin_weight[0], 1, 2)
+    weights_a = split_weights(margin_weight[0], 0, margin_weight.shape[1] // 3)
+    weights_b = split_weights(margin_weight[0], margin_weight.shape[1] // 3, margin_weight.shape[1])
     surface = jnp.pad(
         surface_value.reshape(cells, groups, shares, width),
         ((0, 0), (0, 0), (0, rows - shares), (0, 0)),
     ).reshape(cells, groups * rows, width)
     send = bottoms(me, place, firsts, fields, owners, slots, rows)
     got = exchange(send)
-    seconds = shared(second)
     reply, flux = margins_stage(
         margin_slot[0], margin_block[0], margin_count, weights_a, weights_b, got, surface,
         exchange_coef, land_mask, land_gain, groups, rows, slots, shares,

time: 80.7 us -> 87.3 us (1.082)
  starting transfers between devices: 23 us -> 26.3 us
  local copies, waits for them, and re-layouts: 6.14 us -> 7.39 us
  Pallas kernels: 29.5 us -> 30.6 us
    ppermute x6, starting transfers between devices: 12.7 us -> 16.3 us  [shift(): lax.ppermute(array, 'xg', [(i, (i + by) % groups) for i in range(groups)])]
    pallas_call x2, Pallas kernels: 7.29 us -> 9.26 us  [split_weights(): pl.pallas_call(split_kernel, grid=(count // step,), out_shape=jax.ShapeDt...]
    all_to_all x2, waiting for transfers between devices: 1.47 us -> 2.83 us  [exchange(): lax.all_to_all(array, ('atm', 'xg'), split_axis=0, concat_axis=0, tiled=T...]
    unnamed x23 -> x31, local copies, waits for them, and re-layouts: 4.98 us -> 6.23 us
    pallas_call x1, Pallas kernels: 10.2 us -> 9.31 us  [margins_stage(): pl.pallas_call(functools.partial(margin_kernel, groups, rows, slots, gain...]
  transfers between devices with their start and end apart: 8 -> 8, of which waited for: 5 -> 6; matrix products, arithmetic and copies ran while one was open for 2% -> 2% of each run, Pallas kernels for 10% -> 11%
where the time goes in v6:
time: 87.3 us; the launch traced here: 86.6 us
  Pallas kernels  30.6 us (35%)
  starting transfers between devices  26.3 us (30%)
  waiting for transfers between devices  20.8 us (24%)
  local copies, waits for them, and re-layouts  7.39 us (8%)
  between operations  1.45 us (2%)
    ppermute x6, waiting for transfers between devices, shift(): lax.ppermute(array, 'xg', [(i, (i + by) % groups) for i in range(groups)])  18 us
    ppermute x6, starting transfers between devices, shift(): lax.ppermute(array, 'xg', [(i, (i + by) % groups) for i in range(groups)])  16.3 us
    all_to_all x2, starting transfers between devices, exchange(): lax.all_to_all(array, ('atm', 'xg'), split_axis=0, concat_axis=0, tiled=T...  9.98 us
    pallas_call x1, Pallas kernels, margins_stage(): pl.pallas_call(functools.partial(margin_kernel, groups, rows, slots, gain...  9.31 us
    pallas_call x2, Pallas kernels, split_weights(): pl.pallas_call(split_kernel, grid=(count // step,), out_shape=jax.ShapeDt...  9.26 us
    unnamed x31, local copies, waits for them, and re-layouts  6.23 us
    pallas_call x1, Pallas kernels, finish(): pl.pallas_call(functools.partial(finish_kernel, groups, blocks // groups,...  5.26 us
    pallas_call x1, Pallas kernels, bottoms(): pl.pallas_call(functools.partial(bottom_kernel, groups, own, rows, slots)...  4.19 us
  transfers between devices with their start and end apart: 8, of which 6 were waited for; matrix products, arithmetic and copies ran while one was open for 2% of the time, Pallas kernels for 11%

profile of v6, /device:TPU:0, one launch (start us, length us, event | category | flops | bytes accessed | tf_op | source)
XLA Modules:
  0.0 86.6 jit_solution(12801463299729661319)
XLA Ops:
  0.6 2.1 %factors.1 = (f32[49,4,128]{2,1,0:T(4,128)}, f32[48,4,128]{2,1,0:T(4,128)}) custom-call(f32[192,128]{1,0:T(8,128)} %bitcast.29, f32[192,128]{1,0:T(8,128)} %bitcast.30, f32[4,128]{1,0:T(4,128)} %gain_hbm.1), custom_call_target="tpu_custom_call" | custom-call | flops 1000000 | bytes 400000 | tf_op jit(solution)/shard_map/factors/pallas_call | solution.py:71
  2.7 3.1 %collective-permute-start = (f32[49,4,128]{2,1,0:T(4,128)}, f32[49,4,128]{2,1,0:T(4,128)S(1)}, u32[]{:S(2)}, u32[]{:S(2)}) collective-permute-start(f32[49,4,128]{2,1,0:T(4,128)} %get-tuple-element.8.refs_0_), channel_id=1, source_target_pairs={{0,1},{1,2},{2,3},{3,0},{4,5},{5,6},{6,7},{7,4},{8,9},{9,10},{10,1... | collective-permute-start | bytes 301064 | tf_op jit(solution)/shard_map/ppermute | solution.py:405
  5.8 2.6 %collective-permute-start.1 = (f32[49,4,128]{2,1,0:T(4,128)}, f32[49,4,128]{2,1,0:T(4,128)S(1)}, u32[]{:S(2)}, u32[]{:S(2)}) collective-permute-start(f32[49,4,128]{2,1,0:T(4,128)} %get-tuple-element.8.refs_0_), channel_id=1, source_target_pairs={{0,2},{1,3},{2,0},{3,1},{4,6},{5,7},{6,4},{7,5},{8,10},{9,11},{10,... | collective-permute-start | bytes 301064 | tf_op jit(solution)/shard_map/ppermute | solution.py:405
  8.4 1.3 %collective-permute-start.2 = (f32[49,4,128]{2,1,0:T(4,128)}, f32[49,4,128]{2,1,0:T(4,128)S(1)}, u32[]{:S(2)}, u32[]{:S(2)}) collective-permute-start(f32[49,4,128]{2,1,0:T(4,128)} %get-tuple-element.8.refs_0_), channel_id=1, source_target_pairs={{0,3},{1,0},{2,1},{3,2},{4,7},{5,4},{6,5},{7,6},{8,11},{9,8},{10,9... | collective-permute-start | bytes 301064 | tf_op jit(solution)/shard_map/ppermute | solution.py:405
  9.8 0.8 copy.18
  10.5 0.1 reshape_squeeze.3
  10.7 1.1 %collective-permute-done.refs_1_ = f32[49,4,128]{2,1,0:T(4,128)S(1)} collective-permute-done((f32[49,4,128]{2,1,0:T(4,128)}, f32[49,4,128]{2,1,0:T(4,128)S(1)}, u32[]{:S(2)}, u32[]{:S(2)}) %collective-permute-start) | collective-permute-done | bytes 100384 | tf_op jit(solution)/shard_map/ppermute | solution.py:405
  11.8 0.0 copy-start.2
  11.8 3.5 %collective-permute-done.1.refs_2_ = f32[49,4,128]{2,1,0:T(4,128)S(1)} collective-permute-done((f32[49,4,128]{2,1,0:T(4,128)}, f32[49,4,128]{2,1,0:T(4,128)S(1)}, u32[]{:S(2)}, u32[]{:S(2)}) %collective-permute-start.1) | collective-permute-done | bytes 100384 | tf_op jit(solution)/shard_map/ppermute | solution.py:405
  15.4 0.0 copy-start.4
  15.4 0.0 collective-permute-done.2.refs_3_
  15.4 0.0 copy-start.6
  15.4 0.0 copy-start
  15.4 1.0 %copy-done = f32[49,4,128]{2,1,0:T(4,128)S(1)} copy-done((f32[49,4,128]{2,1,0:T(4,128)S(1)}, f32[49,4,128]{2,1,0:T(4,128)}, u32[]{:S(2)}) %copy-start) | copy-done | bytes 100376
  16.3 0.0 copy-start.14
  16.3 4.2 %bottoms.1 = f32[896,128]{1,0:T(8,128)} custom-call(s32[1]{0:T(128)} %bitcast.me_ref, s32[64]{0:T(128)S(1)} %compare_select_fusion.2.place_ref, f32[49,4,128]{2,1,0:T(4,128)S(1)} %copy-done, f32[49,4,128]{2,1,0:T(4,128)S(1)} %collective-permute-done.refs_1_, f32[49,4,128]{2,1,0:T(4,128)S(1)} %collective-permute-done.1.refs_2_, ...), custom_call_target="tpu_custom_call" | custom-call | flops 4000000 | bytes 7000000 | tf_op jit(solution)/shard_map/bottoms/pallas_call | solution.py:141
  20.5 0.0 copy-done.2
  20.5 0.0 copy-done.4
  20.6 0.0 copy-done.6
  20.6 5.9 %all-to-all-start = ((f32[32,14,2,128]{3,2,1,0:T(2,128)}), f32[32,14,2,128]{3,2,1,0:T(2,128)S(1)}, u32[]{:S(2)}, u32[]{:S(2)}) async-start(f32[32,14,2,128]{3,2,1,0:T(2,128)} %bitcast.7), calls=%async_computation | async-start | bytes 917504 | tf_op jit(solution)/shard_map/all_to_all | solution.py:412
  26.5 0.0 copy-done.14
  26.5 0.2 copy.19.surface_ref
  27.3 6.8 %split_weights.3.weight_b = bf16[64,256,128]{2,1,0:T(8,128)(2,1)} custom-call(f32[96,128,128]{2,1,0:T(8,128)} %bitcast.20), custom_call_target="tpu_custom_call" | custom-call | flops 2500000 | bytes 6500000 | tf_op jit(solution)/shard_map/split_weights/pallas_call | solution.py:173
  34.1 0.0 copy-start.9
  34.1 0.0 copy-start.10
  34.1 0.0 copy-start.11
  34.1 0.0 copy-start.12
  34.1 0.0 copy-start.13
  34.1 2.5 %split_weights.2.weight_a = bf16[32,256,128]{2,1,0:T(8,128)(2,1)S(1)} custom-call(f32[96,128,128]{2,1,0:T(8,128)} %bitcast.21), custom_call_target="tpu_custom_call" | custom-call | flops 2500000 | bytes 6500000 | tf_op jit(solution)/shard_map/split_weights/pallas_call | solution.py:173
  36.6 2.8 %all-to-all-done = f32[32,14,2,128]{3,2,1,0:T(2,128)S(1)} async-done(((f32[32,14,2,128]{3,2,1,0:T(2,128)}), f32[32,14,2,128]{3,2,1,0:T(2,128)S(1)}, u32[]{:S(2)}, u32[]{:S(2)}) %all-to-all-start) | async-done | bytes 458784 | tf_op jit(solution)/shard_map/all_to_all | solution.py:412
  39.4 0.0 copy-done.9
  39.5 0.0 copy-done.10
  39.5 0.0 copy-done.11
  39.5 0.0 copy-done.12
  39.5 0.0 copy-done.13
  39.5 9.3 %margins.1 = (f32[896,128]{1,0:T(8,128)}, f32[16,56,128]{2,1,0:T(8,128)S(1)}) custom-call(s32[96]{0:T(128)S(1)} %bitcast.18, s32[96]{0:T(128)S(1)} %bitcast.19, s32[1]{0:T(128)S(6)} %copy.21.count_ref, bf16[32,256,128]{2,1,0:T(8,128)(2,1)S(1)} %split_weights.2.weight_a, bf16[64,256,128]{2,1,0:T(8,128)(2,1)} %split_weights.3.weight_b, ...), custom_call_target="tpu_custom_call" | custom-call | flops 800000000 | bytes 8000000 | tf_op jit(solution)/shard_map/margins/pallas_call | solution.py:277
  48.8 4.1 %all-to-all-start.1 = ((f32[32,14,2,128]{3,2,1,0:T(2,128)}), f32[32,14,2,128]{3,2,1,0:T(2,128)S(1)}, u32[]{:S(2)}, u32[]{:S(2)}) async-start(f32[32,14,2,128]{3,2,1,0:T(2,128)} %bitcast.11), calls=%async_computation.1 | async-start | bytes 917504 | tf_op jit(solution)/shard_map/all_to_all | solution.py:412
  52.9 3.7 %collective-permute-start.3 = (f32[48,4,128]{2,1,0:T(4,128)}, f32[48,4,128]{2,1,0:T(4,128)S(1)}, u32[]{:S(2)}, u32[]{:S(2)}) collective-permute-start(f32[48,4,128]{2,1,0:T(4,128)} %get-tuple-element.10.refs_4_), channel_id=1, source_target_pairs={{0,3},{1,0},{2,1},{3,2},{4,7},{5,4},{6,5},{7,6},{8,11},{9,8},{10,9... | collective-permute-start | bytes 294920 | tf_op jit(solution)/shard_map/ppermute | solution.py:405
  56.5 7.3 %collective-permute-done.3.refs_7_ = f32[48,4,128]{2,1,0:T(4,128)S(1)} collective-permute-done((f32[48,4,128]{2,1,0:T(4,128)}, f32[48,4,128]{2,1,0:T(4,128)S(1)}, u32[]{:S(2)}, u32[]{:S(2)}) %collective-permute-start.3) | collective-permute-done | bytes 98336 | tf_op jit(solution)/shard_map/ppermute | solution.py:405
  63.8 3.5 %collective-permute-start.4 = (f32[48,4,128]{2,1,0:T(4,128)S(1)}, f32[48,4,128]{2,1,0:T(4,128)S(1)}, u32[]{:S(2)}, u32[]{:S(2)}) collective-permute-start(f32[48,4,128]{2,1,0:T(4,128)S(1)} %collective-permute-done.3.refs_7_), channel_id=1, source_target_pairs={{0,3},{1,0},{2,1},{3,2},{4,7},{5,4},{6,5},{7,6},{8,11},{9,8},{10,9... | collective-permute-start | bytes 294920 | tf_op jit(solution)/shard_map/ppermute | solution.py:405
  67.4 4.3 %collective-permute-done.4.refs_6_ = f32[48,4,128]{2,1,0:T(4,128)S(1)} collective-permute-done((f32[48,4,128]{2,1,0:T(4,128)S(1)}, f32[48,4,128]{2,1,0:T(4,128)S(1)}, u32[]{:S(2)}, u32[]{:S(2)}) %collective-permute-start.4) | collective-permute-done | bytes 98336 | tf_op jit(solution)/shard_map/ppermute | solution.py:405
  71.7 2.1 %collective-permute-start.5 = (f32[48,4,128]{2,1,0:T(4,128)S(1)}, f32[48,4,128]{2,1,0:T(4,128)S(1)}, u32[]{:S(2)}, u32[]{:S(2)}) collective-permute-start(f32[48,4,128]{2,1,0:T(4,128)S(1)} %collective-permute-done.4.refs_6_), channel_id=1, source_target_pairs={{0,3},{1,0},{2,1},{3,2},{4,7},{5,4},{6,5},{7,6},{8,11},{9,8},{10,9... | collective-permute-start | bytes 294920 | tf_op jit(solution)/shard_map/ppermute | solution.py:405
  73.8 0.1 copy.20
  73.9 0.8 slice.4
  74.7 1.7 %collective-permute-done.5.refs_5_ = f32[48,4,128]{2,1,0:T(4,128)S(1)} collective-permute-done((f32[48,4,128]{2,1,0:T(4,128)S(1)}, f32[48,4,128]{2,1,0:T(4,128)S(1)}, u32[]{:S(2)}, u32[]{:S(2)}) %collective-permute-start.5) | collective-permute-done | bytes 98336 | tf_op jit(solution)/shard_map/ppermute | solution.py:405
  76.3 0.0 copy-start.1
  76.3 0.9 %copy-done.1 = f32[49,4,128]{2,1,0:T(4,128)S(1)} copy-done((f32[49,4,128]{2,1,0:T(4,128)S(1)}, f32[49,4,128]{2,1,0:T(4,128)}, u32[]{:S(2)}) %copy-start.1) | copy-done | bytes 100376
  77.2 0.0 copy-start.3
  77.2 0.9 %copy-done.3 = f32[49,4,128]{2,1,0:T(4,128)S(1)} copy-done((f32[49,4,128]{2,1,0:T(4,128)S(1)}, f32[49,4,128]{2,1,0:T(4,128)}, u32[]{:S(2)}) %copy-start.3) | copy-done | bytes 100376
  78.1 0.0 copy-start.5
  78.1 0.9 %copy-done.5 = f32[49,4,128]{2,1,0:T(4,128)S(1)} copy-done((f32[49,4,128]{2,1,0:T(4,128)S(1)}, f32[49,4,128]{2,1,0:T(4,128)}, u32[]{:S(2)}) %copy-start.5) | copy-done | bytes 100376
  79.0 0.0 copy-start.7
  79.0 0.9 %copy-done.7 = f32[49,4,128]{2,1,0:T(4,128)S(1)} copy-done((f32[49,4,128]{2,1,0:T(4,128)S(1)}, f32[49,4,128]{2,1,0:T(4,128)}, u32[]{:S(2)}) %copy-start.7) | copy-done | bytes 100376
  79.9 0.0 copy-start.8
  79.9 0.9 %copy-done.8 = f32[48,4,128]{2,1,0:T(4,128)S(1)} copy-done((f32[48,4,128]{2,1,0:T(4,128)S(1)}, f32[48,4,128]{2,1,0:T(4,128)}, u32[]{:S(2)}) %copy-start.8) | copy-done | bytes 98328
  80.8 0.5 unfold.1
  81.3 0.0 all-to-all-done.1
  81.3 5.3 %finish.1 = f32[16,13,48,128]{3,2,1,0:T(8,128)} custom-call(s32[1]{0:T(128)} %bitcast.me_ref, s32[64]{0:T(128)S(1)} %compare_select_fusion.2.place_ref, f32[896,128]{1,0:T(8,128)S(1)} %bitcast.17, f32[144,16,128]{2,1,0:T(8,128)S(1)} %get-tuple-element.11.factor_ref, f32[16,128]{1,0:T(8,128)S(1)} %get-tuple-element.12.gain_ref, f32[16,13,48,128]{3,2,1,0:T(8,128)} %bitcast.23), custom_call_target="tpu_custom_call" | custom-call | flops 8000000 | bytes 12000000 | tf_op jit(solution)/shard_map/finish/pallas_call | solution.py:375
  (2 shorter events, 0.1 us)
Async XLA Ops:
  2.7 9.1 %collective-permute-start = (f32[49,4,128]{2,1,0:T(4,128)}, f32[49,4,128]{2,1,0:T(4,128)S(1)}, u32[]{:S(2)}, u32[]{:S(2)}) collective-permute-start(f32[49,4,128]{2,1,0:T(4,128)} %get-tuple-element.8.refs_0_), channel_id=1, source_target_pairs={{0,1},{1,2},{2,3},{3,0},{4,5},{5,6},{6,7},{7,4},{8,9},{9,10},{10,1... | collective-permute-start | bytes 301064 | tf_op jit(solution)/shard_map/ppermute | solution.py:405
  5.8 9.5 %collective-permute-start.1 = (f32[49,4,128]{2,1,0:T(4,128)}, f32[49,4,128]{2,1,0:T(4,128)S(1)}, u32[]{:S(2)}, u32[]{:S(2)}) collective-permute-start(f32[49,4,128]{2,1,0:T(4,128)} %get-tuple-element.8.refs_0_), channel_id=1, source_target_pairs={{0,2},{1,3},{2,0},{3,1},{4,6},{5,7},{6,4},{7,5},{8,10},{9,11},{10,... | collective-permute-start | bytes 301064 | tf_op jit(solution)/shard_map/ppermute | solution.py:405
  8.4 6.9 %collective-permute-start.2 = (f32[49,4,128]{2,1,0:T(4,128)}, f32[49,4,128]{2,1,0:T(4,128)S(1)}, u32[]{:S(2)}, u32[]{:S(2)}) collective-permute-start(f32[49,4,128]{2,1,0:T(4,128)} %get-tuple-element.8.refs_0_), channel_id=1, source_target_pairs={{0,3},{1,0},{2,1},{3,2},{4,7},{5,4},{6,5},{7,6},{8,11},{9,8},{10,9... | collective-permute-start | bytes 301064 | tf_op jit(solution)/shard_map/ppermute | solution.py:405
  11.8 8.7 %copy-start.2 = (f32[49,4,128]{2,1,0:T(4,128)}, f32[49,4,128]{2,1,0:T(4,128)S(1)}, u32[]{:S(2)}) copy-start(f32[49,4,128]{2,1,0:T(4,128)S(1)} %collective-permute-done.refs_1_) | copy-start | bytes 301060
  15.4 5.2 %copy-start.4 = (f32[49,4,128]{2,1,0:T(4,128)}, f32[49,4,128]{2,1,0:T(4,128)S(1)}, u32[]{:S(2)}) copy-start(f32[49,4,128]{2,1,0:T(4,128)S(1)} %collective-permute-done.1.refs_2_) | copy-start | bytes 301060
  15.4 5.2 %copy-start.6 = (f32[49,4,128]{2,1,0:T(4,128)}, f32[49,4,128]{2,1,0:T(4,128)S(1)}, u32[]{:S(2)}) copy-start(f32[49,4,128]{2,1,0:T(4,128)S(1)} %collective-permute-done.2.refs_3_) | copy-start | bytes 301060
  15.4 1.0 %copy-start = (f32[49,4,128]{2,1,0:T(4,128)S(1)}, f32[49,4,128]{2,1,0:T(4,128)}, u32[]{:S(2)}) copy-start(f32[49,4,128]{2,1,0:T(4,128)} %get-tuple-element.8.refs_0_) | copy-start | bytes 301060
  16.3 10.1 %copy-start.14 = (f32[16,52,128]{2,0,1:T(8,128)S(1)}, f32[16,52,128]{2,0,1:T(8,128)}, u32[]{:S(2)}) copy-start(f32[16,52,128]{2,0,1:T(8,128)} %param.22) | copy-start | bytes 1277956
  20.6 18.9 %all-to-all-start = ((f32[32,14,2,128]{3,2,1,0:T(2,128)}), f32[32,14,2,128]{3,2,1,0:T(2,128)S(1)}, u32[]{:S(2)}, u32[]{:S(2)}) async-start(f32[32,14,2,128]{3,2,1,0:T(2,128)} %bitcast.7), calls=%async_computation | async-start | bytes 917504 | tf_op jit(solution)/shard_map/all_to_all | solution.py:412
  34.1 5.4 %copy-start.9 = (f32[16,128]{1,0:T(8,128)S(1)}, f32[16,128]{1,0:T(8,128)}, u32[]{:S(2)}) copy-start(f32[16,128]{1,0:T(8,128)} %coef_ref.1) | copy-start | bytes 24580
  34.1 5.4 %copy-start.10 = (s32[16,128]{1,0:T(8,128)S(1)}, s32[16,128]{1,0:T(8,128)}, u32[]{:S(2)}) copy-start(s32[16,128]{1,0:T(8,128)} %mask_ref.1) | copy-start | bytes 24580
  34.1 5.4 %copy-start.11 = (f32[16,128]{1,0:T(8,128)S(1)}, f32[16,128]{1,0:T(8,128)}, u32[]{:S(2)}) copy-start(f32[16,128]{1,0:T(8,128)} %land_ref.1) | copy-start | bytes 24580
  34.1 5.4 %copy-start.12 = (s32[1,96]{1,0:T(1,128)S(1)}, s32[1,96]{1,0:T(1,128)}, u32[]{:S(2)}) copy-start(s32[1,96]{1,0:T(1,128)} %param.18) | copy-start | bytes 1156
  34.1 5.4 %copy-start.13 = (s32[1,96]{1,0:T(1,128)S(1)}, s32[1,96]{1,0:T(1,128)}, u32[]{:S(2)}) copy-start(s32[1,96]{1,0:T(1,128)} %param.19) | copy-start | bytes 1156
  48.8 32.5 %all-to-all-start.1 = ((f32[32,14,2,128]{3,2,1,0:T(2,128)}), f32[32,14,2,128]{3,2,1,0:T(2,128)S(1)}, u32[]{:S(2)}, u32[]{:S(2)}) async-start(f32[32,14,2,128]{3,2,1,0:T(2,128)} %bitcast.11), calls=%async_computation.1 | async-start | bytes 917504 | tf_op jit(solution)/shard_map/all_to_all | solution.py:412
  52.9 11.0 %collective-permute-start.3 = (f32[48,4,128]{2,1,0:T(4,128)}, f32[48,4,128]{2,1,0:T(4,128)S(1)}, u32[]{:S(2)}, u32[]{:S(2)}) collective-permute-start(f32[48,4,128]{2,1,0:T(4,128)} %get-tuple-element.10.refs_4_), channel_id=1, source_target_pairs={{0,3},{1,0},{2,1},{3,2},{4,7},{5,4},{6,5},{7,6},{8,11},{9,8},{10,9... | collective-permute-start | bytes 294920 | tf_op jit(solution)/shard_map/ppermute | solution.py:405
  63.8 7.9 %collective-permute-start.4 = (f32[48,4,128]{2,1,0:T(4,128)S(1)}, f32[48,4,128]{2,1,0:T(4,128)S(1)}, u32[]{:S(2)}, u32[]{:S(2)}) collective-permute-start(f32[48,4,128]{2,1,0:T(4,128)S(1)} %collective-permute-done.3.refs_7_), channel_id=1, source_target_pairs={{0,3},{1,0},{2,1},{3,2},{4,7},{5,4},{6,5},{7,6},{8,11},{9,8},{10,9... | collective-permute-start | bytes 294920 | tf_op jit(solution)/shard_map/ppermute | solution.py:405
  71.7 4.6 %collective-permute-start.5 = (f32[48,4,128]{2,1,0:T(4,128)S(1)}, f32[48,4,128]{2,1,0:T(4,128)S(1)}, u32[]{:S(2)}, u32[]{:S(2)}) collective-permute-start(f32[48,4,128]{2,1,0:T(4,128)S(1)} %collective-permute-done.4.refs_6_), channel_id=1, source_target_pairs={{0,3},{1,0},{2,1},{3,2},{4,7},{5,4},{6,5},{7,6},{8,11},{9,8},{10,9... | collective-permute-start | bytes 294920 | tf_op jit(solution)/shard_map/ppermute | solution.py:405
  76.3 0.9 %copy-start.1 = (f32[49,4,128]{2,1,0:T(4,128)S(1)}, f32[49,4,128]{2,1,0:T(4,128)}, u32[]{:S(2)}) copy-start(f32[49,4,128]{2,1,0:T(4,128)} %get-tuple-element.8.refs_0_) | copy-start | bytes 301060
  77.2 0.9 %copy-start.3 = (f32[49,4,128]{2,1,0:T(4,128)S(1)}, f32[49,4,128]{2,1,0:T(4,128)}, u32[]{:S(2)}) copy-start(f32[49,4,128]{2,1,0:T(4,128)} %copy-done.2) | copy-start | bytes 301060
  78.1 0.9 %copy-start.5 = (f32[49,4,128]{2,1,0:T(4,128)S(1)}, f32[49,4,128]{2,1,0:T(4,128)}, u32[]{:S(2)}) copy-start(f32[49,4,128]{2,1,0:T(4,128)} %copy-done.4) | copy-start | bytes 301060
  79.0 0.9 %copy-start.7 = (f32[49,4,128]{2,1,0:T(4,128)S(1)}, f32[49,4,128]{2,1,0:T(4,128)}, u32[]{:S(2)}) copy-start(f32[49,4,128]{2,1,0:T(4,128)} %copy-done.6) | copy-start | bytes 301060
  79.9 0.9 %copy-start.8 = (f32[48,4,128]{2,1,0:T(4,128)S(1)}, f32[48,4,128]{2,1,0:T(4,128)}, u32[]{:S(2)}) copy-start(f32[48,4,128]{2,1,0:T(4,128)} %get-tuple-element.10.refs_4_) | copy-start | bytes 294916

commit v7 on v6

--- a/solution.py
+++ b/solution.py
@@ -11,6 +11,7 @@
 F32 = jnp.float32
 BF16 = jnp.bfloat16
 ROWS = 8
+PIECES = 5
 MOST = 67043328
 ROOMY = 50 << 20
 
@@ -88,15 +89,35 @@
     )(upper.reshape(own * levels, width), lower.reshape(own * levels, width), surface_gain)
 
 
+def bundles(shares):
+    pieces = min(PIECES, shares)
+    edges = [i * shares // pieces for i in range(pieces + 1)]
+    return list(zip(edges[:-1], edges[1:]))
+
+
+def field_copies(me, groups, own, fields_ref, held_ref, sem, piece, out):
+    low, high = bundles(held_ref.shape[0])[piece]
+    copies = []
+    for q in range(groups):
+        base = lax.rem(me - q + groups, groups) * own
+        for i in range(own):
+            far = fields_ref.at[base + i, pl.ds(low, high - low)]
+            near = held_ref.at[pl.ds(low, high - low), :, q * own + i, :]
+            pair = (near, far) if out else (far, near)
+            copies.append(pltpu.make_async_copy(*pair, sem.at[piece]))
+    return copies
+
+
 def fetch_fields(me, groups, own, fields_ref, held_ref, sem):
-    shares = fields_ref.shape[1]
-    for f in range(shares):
-        for q in range(groups):
-            base = lax.rem(me - q + groups, groups) * own
-            for i in range(own):
-                pltpu.make_async_copy(
-                    fields_ref.at[base + i, f], held_ref.at[f, :, q * own + i, :], sem.at[f]
-                ).start()
+    for piece in range(len(bundles(held_ref.shape[0]))):
+        for copy in field_copies(me, groups, own, fields_ref, held_ref, sem, piece, False):
+            copy.start()
+
+
+def wait_piece(held_ref, sem, piece):
+    low, high = bundles(held_ref.shape[0])[piece]
+    part = held_ref.at[pl.ds(low, high - low)]
+    pltpu.make_async_copy(part, part, sem.at[piece]).wait()
 
 
 def bottom_kernel(groups, own, rows, slots, me_ref, place_ref, *refs):
@@ -121,13 +142,17 @@
         weight = weight * ratio
     value_ref[...] = jnp.zeros_like(value_ref)
     value_ref[pl.ds(shares, blocks, stride=pitch), :] = weight_ref[levels]
-    for f in range(shares):
-        pltpu.make_async_copy(held_ref.at[f], held_ref.at[f], sem.at[f]).wait()
-        sums = [None] * 4
+    for piece, (low, high) in enumerate(bundles(shares)):
+        wait_piece(held_ref, sem, piece)
+        sums = {}
         for k in range(levels):
-            term = weight_ref[k] * held_ref[f, k]
-            sums[k % 4] = term if sums[k % 4] is None else sums[k % 4] + term
-        value_ref[pl.ds(f, blocks, stride=pitch), :] = (sums[0] + sums[1]) + (sums[2] + sums[3])
+            weight = weight_ref[k]
+            for f in range(low, high):
+                term = weight * held_ref[f, k]
+                slot = (f, k % 2)
+                sums[slot] = sums[slot] + term if slot in sums else term
+        for f in range(low, high):
+            value_ref[pl.ds(f, blocks, stride=pitch), :] = sums[f, 0] + sums[f, 1]
     for d in range(send_ref.shape[0] // (rows * slots)):
         for p in range(slots):
             start = pl.multiple_of(place_ref[d * slots + p] * pitch, pitch)
@@ -148,7 +173,7 @@
             pltpu.VMEM((levels + 1, blocks, width), F32),
             pltpu.VMEM(((blocks + 1) * round_up(rows, ROWS), width), F32),
             pltpu.VMEM((levels + 1, own, width), F32),
-            pltpu.SemaphoreType.DMA((shares,)),
+            pltpu.SemaphoreType.DMA((len(bundles(shares)),)),
             pltpu.SemaphoreType.DMA(()),
         ],
         compiler_params=params(ROOMY),
@@ -347,27 +372,30 @@
             flux_ref[pl.ds(start, rows), :] += (
                 answer_ref[pl.ds(d * rows * slots + p, rows, stride=slots), :]
             )
-    for f in range(shares):
-        flux = flux_ref[pl.ds(f, blocks, stride=pitch), :]
-        pltpu.make_async_copy(held_ref.at[f], held_ref.at[f], sem.at[f]).wait()
-        state = held_ref[f, 0]
+    for piece, (low, high) in enumerate(bundles(shares)):
+        wait_piece(held_ref, sem, piece)
+        span = range(low, high)
+        state = {f: held_ref[f, 0] for f in span}
         for k in range(1, levels):
-            state = held_ref[f, k] + factor_ref[k] * state
-            if k < levels - 1:
-                held_ref[f, k] = state
-        state = factor_ref[2 * levels - 1] * state + gain_ref[...] * flux
-        held_ref[f, levels - 1] = state
+            ratio = factor_ref[k]
+            for f in span:
+                state[f] = held_ref[f, k] + ratio * state[f]
+                if k < levels - 1:
+                    held_ref[f, k] = state[f]
+        inverse = factor_ref[2 * levels - 1]
+        for f in span:
+            flux = flux_ref[pl.ds(f, blocks, stride=pitch), :]
+            state[f] = inverse * state[f] + gain_ref[...] * flux
+            held_ref[f, levels - 1] = state[f]
         for k in range(levels - 2, -1, -1):
-            state = factor_ref[levels + k] * held_ref[f, k] + factor_ref[2 * levels + k] * state
-            held_ref[f, k] = state
-        for q in range(groups):
-            base = lax.rem(me - q + groups, groups) * own
-            for i in range(own):
-                pltpu.make_async_copy(
-                    held_ref.at[f, :, q * own + i, :], out_ref.at[base + i, f], out_sem.at[f]
-                ).start()
-    for f in range(shares):
-        pltpu.make_async_copy(held_ref.at[f], held_ref.at[f], out_sem.at[f]).wait()
+            inverse, carry = factor_ref[levels + k], factor_ref[2 * levels + k]
+            for f in span:
+                state[f] = inverse * held_ref[f, k] + carry * state[f]
+                held_ref[f, k] = state[f]
+        for copy in field_copies(me, groups, own, out_ref, held_ref, out_sem, piece, True):
+            copy.start()
+    for piece in range(len(bundles(shares))):
+        wait_piece(held_ref, out_sem, piece)
 
 
 def finish(me, place, answer, factor, gain, fields, groups, rows, slots):
@@ -380,8 +408,8 @@
         scratch_shapes=[
             pltpu.VMEM((shares, levels, blocks, width), F32),
             pltpu.VMEM(((blocks + 1) * round_up(rows, ROWS), width), F32),
-            pltpu.SemaphoreType.DMA((shares,)),
-            pltpu.SemaphoreType.DMA((shares,)),
+            pltpu.SemaphoreType.DMA((len(bundles(shares)),)),
+            pltpu.SemaphoreType.DMA((len(bundles(shares)),)),
         ],
         compiler_params=params(ROOMY),
         cost_estimate=pl.CostEstimate(flops=8000000, bytes_accessed=12000000, transcendentals=0),

time: 87.3 us -> 86.9 us (level)
  no operation moved by 1% of the time
where the time goes in v7:
time: 86.9 us; the launch traced here: 86.1 us
  Pallas kernels  30.1 us (35%)
  starting transfers between devices  26.3 us (30%)
  waiting for transfers between devices  20.8 us (24%)
  local copies, waits for them, and re-layouts  7.39 us (9%)
  between operations  1.45 us (2%)
    ppermute x6, waiting for transfers between devices, shift(): lax.ppermute(array, 'xg', [(i, (i + by) % groups) for i in range(groups)])  18 us
    ppermute x6, starting transfers between devices, shift(): lax.ppermute(array, 'xg', [(i, (i + by) % groups) for i in range(groups)])  16.3 us
    all_to_all x2, starting transfers between devices, exchange(): lax.all_to_all(array, ('atm', 'xg'), split_axis=0, concat_axis=0, tiled=T...  9.98 us
    pallas_call x1, Pallas kernels, margins_stage(): pl.pallas_call(functools.partial(margin_kernel, groups, rows, slots, gain...  9.3 us
    pallas_call x2, Pallas kernels, split_weights(): pl.pallas_call(split_kernel, grid=(count // step,), out_shape=jax.ShapeDt...  9.26 us
    unnamed x31, local copies, waits for them, and re-layouts  6.23 us
    pallas_call x1, Pallas kernels, finish(): pl.pallas_call(functools.partial(finish_kernel, groups, blocks // groups,...  4.8 us
    pallas_call x1, Pallas kernels, bottoms(): pl.pallas_call(functools.partial(bottom_kernel, groups, own, rows, slots)...  4.19 us
  transfers between devices with their start and end apart: 8, of which 6 were waited for; matrix products, arithmetic and copies ran while one was open for 2% of the time, Pallas kernels for 11%

profile of v7, /device:TPU:0, one launch (start us, length us, event | category | flops | bytes accessed | tf_op | source)
XLA Modules:
  0.0 86.1 jit_solution(812163583798895495)
XLA Ops:
  0.6 2.1 %factors.1 = (f32[49,4,128]{2,1,0:T(4,128)}, f32[48,4,128]{2,1,0:T(4,128)}) custom-call(f32[192,128]{1,0:T(8,128)} %bitcast.29, f32[192,128]{1,0:T(8,128)} %bitcast.30, f32[4,128]{1,0:T(4,128)} %gain_hbm.1), custom_call_target="tpu_custom_call" | custom-call | flops 1000000 | bytes 400000 | tf_op jit(solution)/shard_map/factors/pallas_call | solution.py:72
  2.7 3.1 %collective-permute-start = (f32[49,4,128]{2,1,0:T(4,128)}, f32[49,4,128]{2,1,0:T(4,128)S(1)}, u32[]{:S(2)}, u32[]{:S(2)}) collective-permute-start(f32[49,4,128]{2,1,0:T(4,128)} %get-tuple-element.8.refs_0_), channel_id=1, source_target_pairs={{0,1},{1,2},{2,3},{3,0},{4,5},{5,6},{6,7},{7,4},{8,9},{9,10},{10,1... | collective-permute-start | bytes 301064 | tf_op jit(solution)/shard_map/ppermute | solution.py:433
  5.8 2.6 %collective-permute-start.1 = (f32[49,4,128]{2,1,0:T(4,128)}, f32[49,4,128]{2,1,0:T(4,128)S(1)}, u32[]{:S(2)}, u32[]{:S(2)}) collective-permute-start(f32[49,4,128]{2,1,0:T(4,128)} %get-tuple-element.8.refs_0_), channel_id=1, source_target_pairs={{0,2},{1,3},{2,0},{3,1},{4,6},{5,7},{6,4},{7,5},{8,10},{9,11},{10,... | collective-permute-start | bytes 301064 | tf_op jit(solution)/shard_map/ppermute | solution.py:433
  8.4 1.3 %collective-permute-start.2 = (f32[49,4,128]{2,1,0:T(4,128)}, f32[49,4,128]{2,1,0:T(4,128)S(1)}, u32[]{:S(2)}, u32[]{:S(2)}) collective-permute-start(f32[49,4,128]{2,1,0:T(4,128)} %get-tuple-element.8.refs_0_), channel_id=1, source_target_pairs={{0,3},{1,0},{2,1},{3,2},{4,7},{5,4},{6,5},{7,6},{8,11},{9,8},{10,9... | collective-permute-start | bytes 301064 | tf_op jit(solution)/shard_map/ppermute | solution.py:433
  9.8 0.8 copy.18
  10.5 0.1 reshape_squeeze.3
  10.7 1.1 %collective-permute-done.refs_1_ = f32[49,4,128]{2,1,0:T(4,128)S(1)} collective-permute-done((f32[49,4,128]{2,1,0:T(4,128)}, f32[49,4,128]{2,1,0:T(4,128)S(1)}, u32[]{:S(2)}, u32[]{:S(2)}) %collective-permute-start) | collective-permute-done | bytes 100384 | tf_op jit(solution)/shard_map/ppermute | solution.py:433
  11.8 0.0 copy-start.2
  11.8 3.5 %collective-permute-done.1.refs_2_ = f32[49,4,128]{2,1,0:T(4,128)S(1)} collective-permute-done((f32[49,4,128]{2,1,0:T(4,128)}, f32[49,4,128]{2,1,0:T(4,128)S(1)}, u32[]{:S(2)}, u32[]{:S(2)}) %collective-permute-start.1) | collective-permute-done | bytes 100384 | tf_op jit(solution)/shard_map/ppermute | solution.py:433
  15.4 0.0 copy-start.4
  15.4 0.0 collective-permute-done.2.refs_3_
  15.4 0.0 copy-start.6
  15.4 0.0 copy-start
  15.4 1.0 %copy-done = f32[49,4,128]{2,1,0:T(4,128)S(1)} copy-done((f32[49,4,128]{2,1,0:T(4,128)S(1)}, f32[49,4,128]{2,1,0:T(4,128)}, u32[]{:S(2)}) %copy-start) | copy-done | bytes 100376
  16.3 0.0 copy-start.14
  16.3 4.2 %bottoms.1 = f32[896,128]{1,0:T(8,128)} custom-call(s32[1]{0:T(128)} %bitcast.me_ref, s32[64]{0:T(128)S(1)} %compare_select_fusion.2.place_ref, f32[49,4,128]{2,1,0:T(4,128)S(1)} %copy-done, f32[49,4,128]{2,1,0:T(4,128)S(1)} %collective-permute-done.refs_1_, f32[49,4,128]{2,1,0:T(4,128)S(1)} %collective-permute-done.1.refs_2_, ...), custom_call_target="tpu_custom_call" | custom-call | flops 4000000 | bytes 7000000 | tf_op jit(solution)/shard_map/bottoms/pallas_call | solution.py:166
  20.5 0.0 copy-done.2
  20.5 0.0 copy-done.4
  20.6 0.0 copy-done.6
  20.6 5.9 %all-to-all-start = ((f32[32,14,2,128]{3,2,1,0:T(2,128)}), f32[32,14,2,128]{3,2,1,0:T(2,128)S(1)}, u32[]{:S(2)}, u32[]{:S(2)}) async-start(f32[32,14,2,128]{3,2,1,0:T(2,128)} %bitcast.7), calls=%async_computation | async-start | bytes 917504 | tf_op jit(solution)/shard_map/all_to_all | solution.py:440
  26.5 0.0 copy-done.14
  26.5 0.2 copy.19.surface_ref
  27.3 6.8 %split_weights.3.weight_b = bf16[64,256,128]{2,1,0:T(8,128)(2,1)} custom-call(f32[96,128,128]{2,1,0:T(8,128)} %bitcast.20), custom_call_target="tpu_custom_call" | custom-call | flops 2500000 | bytes 6500000 | tf_op jit(solution)/shard_map/split_weights/pallas_call | solution.py:198
  34.1 0.0 copy-start.9
  34.1 0.0 copy-start.10
  34.1 0.0 copy-start.11
  34.1 0.0 copy-start.12
  34.1 0.0 copy-start.13
  34.1 2.5 %split_weights.2.weight_a = bf16[32,256,128]{2,1,0:T(8,128)(2,1)S(1)} custom-call(f32[96,128,128]{2,1,0:T(8,128)} %bitcast.21), custom_call_target="tpu_custom_call" | custom-call | flops 2500000 | bytes 6500000 | tf_op jit(solution)/shard_map/split_weights/pallas_call | solution.py:198
  36.6 2.8 %all-to-all-done = f32[32,14,2,128]{3,2,1,0:T(2,128)S(1)} async-done(((f32[32,14,2,128]{3,2,1,0:T(2,128)}), f32[32,14,2,128]{3,2,1,0:T(2,128)S(1)}, u32[]{:S(2)}, u32[]{:S(2)}) %all-to-all-start) | async-done | bytes 458784 | tf_op jit(solution)/shard_map/all_to_all | solution.py:440
  39.5 0.0 copy-done.9
  39.5 0.0 copy-done.10
  39.5 0.0 copy-done.11
  39.5 0.0 copy-done.12
  39.5 0.0 copy-done.13
  39.5 9.3 %margins.1 = (f32[896,128]{1,0:T(8,128)}, f32[16,56,128]{2,1,0:T(8,128)S(1)}) custom-call(s32[96]{0:T(128)S(1)} %bitcast.18, s32[96]{0:T(128)S(1)} %bitcast.19, s32[1]{0:T(128)S(6)} %copy.21.count_ref, bf16[32,256,128]{2,1,0:T(8,128)(2,1)S(1)} %split_weights.2.weight_a, bf16[64,256,128]{2,1,0:T(8,128)(2,1)} %split_weights.3.weight_b, ...), custom_call_target="tpu_custom_call" | custom-call | flops 800000000 | bytes 8000000 | tf_op jit(solution)/shard_map/margins/pallas_call | solution.py:302
  48.8 4.1 %all-to-all-start.1 = ((f32[32,14,2,128]{3,2,1,0:T(2,128)}), f32[32,14,2,128]{3,2,1,0:T(2,128)S(1)}, u32[]{:S(2)}, u32[]{:S(2)}) async-start(f32[32,14,2,128]{3,2,1,0:T(2,128)} %bitcast.11), calls=%async_computation.1 | async-start | bytes 917504 | tf_op jit(solution)/shard_map/all_to_all | solution.py:440
  52.9 3.7 %collective-permute-start.3 = (f32[48,4,128]{2,1,0:T(4,128)}, f32[48,4,128]{2,1,0:T(4,128)S(1)}, u32[]{:S(2)}, u32[]{:S(2)}) collective-permute-start(f32[48,4,128]{2,1,0:T(4,128)} %get-tuple-element.10.refs_4_), channel_id=1, source_target_pairs={{0,3},{1,0},{2,1},{3,2},{4,7},{5,4},{6,5},{7,6},{8,11},{9,8},{10,9... | collective-permute-start | bytes 294920 | tf_op jit(solution)/shard_map/ppermute | solution.py:433
  56.5 7.3 %collective-permute-done.3.refs_7_ = f32[48,4,128]{2,1,0:T(4,128)S(1)} collective-permute-done((f32[48,4,128]{2,1,0:T(4,128)}, f32[48,4,128]{2,1,0:T(4,128)S(1)}, u32[]{:S(2)}, u32[]{:S(2)}) %collective-permute-start.3) | collective-permute-done | bytes 98336 | tf_op jit(solution)/shard_map/ppermute | solution.py:433
  63.8 3.5 %collective-permute-start.4 = (f32[48,4,128]{2,1,0:T(4,128)S(1)}, f32[48,4,128]{2,1,0:T(4,128)S(1)}, u32[]{:S(2)}, u32[]{:S(2)}) collective-permute-start(f32[48,4,128]{2,1,0:T(4,128)S(1)} %collective-permute-done.3.refs_7_), channel_id=1, source_target_pairs={{0,3},{1,0},{2,1},{3,2},{4,7},{5,4},{6,5},{7,6},{8,11},{9,8},{10,9... | collective-permute-start | bytes 294920 | tf_op jit(solution)/shard_map/ppermute | solution.py:433
  67.4 4.3 %collective-permute-done.4.refs_6_ = f32[48,4,128]{2,1,0:T(4,128)S(1)} collective-permute-done((f32[48,4,128]{2,1,0:T(4,128)S(1)}, f32[48,4,128]{2,1,0:T(4,128)S(1)}, u32[]{:S(2)}, u32[]{:S(2)}) %collective-permute-start.4) | collective-permute-done | bytes 98336 | tf_op jit(solution)/shard_map/ppermute | solution.py:433
  71.7 2.1 %collective-permute-start.5 = (f32[48,4,128]{2,1,0:T(4,128)S(1)}, f32[48,4,128]{2,1,0:T(4,128)S(1)}, u32[]{:S(2)}, u32[]{:S(2)}) collective-permute-start(f32[48,4,128]{2,1,0:T(4,128)S(1)} %collective-permute-done.4.refs_6_), channel_id=1, source_target_pairs={{0,3},{1,0},{2,1},{3,2},{4,7},{5,4},{6,5},{7,6},{8,11},{9,8},{10,9... | collective-permute-start | bytes 294920 | tf_op jit(solution)/shard_map/ppermute | solution.py:433
  73.8 0.1 copy.20
  73.9 0.8 slice.4
  74.7 1.7 %collective-permute-done.5.refs_5_ = f32[48,4,128]{2,1,0:T(4,128)S(1)} collective-permute-done((f32[48,4,128]{2,1,0:T(4,128)S(1)}, f32[48,4,128]{2,1,0:T(4,128)S(1)}, u32[]{:S(2)}, u32[]{:S(2)}) %collective-permute-start.5) | collective-permute-done | bytes 98336 | tf_op jit(solution)/shard_map/ppermute | solution.py:433
  76.3 0.0 copy-start.1
  76.3 0.9 %copy-done.1 = f32[49,4,128]{2,1,0:T(4,128)S(1)} copy-done((f32[49,4,128]{2,1,0:T(4,128)S(1)}, f32[49,4,128]{2,1,0:T(4,128)}, u32[]{:S(2)}) %copy-start.1) | copy-done | bytes 100376
  77.2 0.0 copy-start.3
  77.2 0.9 %copy-done.3 = f32[49,4,128]{2,1,0:T(4,128)S(1)} copy-done((f32[49,4,128]{2,1,0:T(4,128)S(1)}, f32[49,4,128]{2,1,0:T(4,128)}, u32[]{:S(2)}) %copy-start.3) | copy-done | bytes 100376
  78.1 0.0 copy-start.5
  78.1 0.9 %copy-done.5 = f32[49,4,128]{2,1,0:T(4,128)S(1)} copy-done((f32[49,4,128]{2,1,0:T(4,128)S(1)}, f32[49,4,128]{2,1,0:T(4,128)}, u32[]{:S(2)}) %copy-start.5) | copy-done | bytes 100376
  79.0 0.0 copy-start.7
  79.0 0.9 %copy-done.7 = f32[49,4,128]{2,1,0:T(4,128)S(1)} copy-done((f32[49,4,128]{2,1,0:T(4,128)S(1)}, f32[49,4,128]{2,1,0:T(4,128)}, u32[]{:S(2)}) %copy-start.7) | copy-done | bytes 100376
  79.9 0.0 copy-start.8
  79.9 0.9 %copy-done.8 = f32[48,4,128]{2,1,0:T(4,128)S(1)} copy-done((f32[48,4,128]{2,1,0:T(4,128)S(1)}, f32[48,4,128]{2,1,0:T(4,128)}, u32[]{:S(2)}) %copy-start.8) | copy-done | bytes 98328
  80.8 0.5 unfold.1
  81.3 0.0 all-to-all-done.1
  81.3 4.8 %finish.1 = f32[16,13,48,128]{3,2,1,0:T(8,128)} custom-call(s32[1]{0:T(128)} %bitcast.me_ref, s32[64]{0:T(128)S(1)} %compare_select_fusion.2.place_ref, f32[896,128]{1,0:T(8,128)S(1)} %bitcast.17, f32[144,16,128]{2,1,0:T(8,128)S(1)} %get-tuple-element.11.factor_ref, f32[16,128]{1,0:T(8,128)S(1)} %get-tuple-element.12.gain_ref, f32[16,13,48,128]{3,2,1,0:T(8,128)} %bitcast.23), custom_call_target="tpu_custom_call" | custom-call | flops 8000000 | bytes 12000000 | tf_op jit(solution)/shard_map/finish/pallas_call | solution.py:403
  (2 shorter events, 0.1 us)
Async XLA Ops:
  2.7 9.1 %collective-permute-start = (f32[49,4,128]{2,1,0:T(4,128)}, f32[49,4,128]{2,1,0:T(4,128)S(1)}, u32[]{:S(2)}, u32[]{:S(2)}) collective-permute-start(f32[49,4,128]{2,1,0:T(4,128)} %get-tuple-element.8.refs_0_), channel_id=1, source_target_pairs={{0,1},{1,2},{2,3},{3,0},{4,5},{5,6},{6,7},{7,4},{8,9},{9,10},{10,1... | collective-permute-start | bytes 301064 | tf_op jit(solution)/shard_map/ppermute | solution.py:433
  5.8 9.5 %collective-permute-start.1 = (f32[49,4,128]{2,1,0:T(4,128)}, f32[49,4,128]{2,1,0:T(4,128)S(1)}, u32[]{:S(2)}, u32[]{:S(2)}) collective-permute-start(f32[49,4,128]{2,1,0:T(4,128)} %get-tuple-element.8.refs_0_), channel_id=1, source_target_pairs={{0,2},{1,3},{2,0},{3,1},{4,6},{5,7},{6,4},{7,5},{8,10},{9,11},{10,... | collective-permute-start | bytes 301064 | tf_op jit(solution)/shard_map/ppermute | solution.py:433
  8.4 6.9 %collective-permute-start.2 = (f32[49,4,128]{2,1,0:T(4,128)}, f32[49,4,128]{2,1,0:T(4,128)S(1)}, u32[]{:S(2)}, u32[]{:S(2)}) collective-permute-start(f32[49,4,128]{2,1,0:T(4,128)} %get-tuple-element.8.refs_0_), channel_id=1, source_target_pairs={{0,3},{1,0},{2,1},{3,2},{4,7},{5,4},{6,5},{7,6},{8,11},{9,8},{10,9... | collective-permute-start | bytes 301064 | tf_op jit(solution)/shard_map/ppermute | solution.py:433
  11.8 8.7 %copy-start.2 = (f32[49,4,128]{2,1,0:T(4,128)}, f32[49,4,128]{2,1,0:T(4,128)S(1)}, u32[]{:S(2)}) copy-start(f32[49,4,128]{2,1,0:T(4,128)S(1)} %collective-permute-done.refs_1_) | copy-start | bytes 301060
  15.4 5.2 %copy-start.4 = (f32[49,4,128]{2,1,0:T(4,128)}, f32[49,4,128]{2,1,0:T(4,128)S(1)}, u32[]{:S(2)}) copy-start(f32[49,4,128]{2,1,0:T(4,128)S(1)} %collective-permute-done.1.refs_2_) | copy-start | bytes 301060
  15.4 5.2 %copy-start.6 = (f32[49,4,128]{2,1,0:T(4,128)}, f32[49,4,128]{2,1,0:T(4,128)S(1)}, u32[]{:S(2)}) copy-start(f32[49,4,128]{2,1,0:T(4,128)S(1)} %collective-permute-done.2.refs_3_) | copy-start | bytes 301060
  15.4 1.0 %copy-start = (f32[49,4,128]{2,1,0:T(4,128)S(1)}, f32[49,4,128]{2,1,0:T(4,128)}, u32[]{:S(2)}) copy-start(f32[49,4,128]{2,1,0:T(4,128)} %get-tuple-element.8.refs_0_) | copy-start | bytes 301060
  16.3 10.1 %copy-start.14 = (f32[16,52,128]{2,0,1:T(8,128)S(1)}, f32[16,52,128]{2,0,1:T(8,128)}, u32[]{:S(2)}) copy-start(f32[16,52,128]{2,0,1:T(8,128)} %param.22) | copy-start | bytes 1277956
  20.6 18.9 %all-to-all-start = ((f32[32,14,2,128]{3,2,1,0:T(2,128)}), f32[32,14,2,128]{3,2,1,0:T(2,128)S(1)}, u32[]{:S(2)}, u32[]{:S(2)}) async-start(f32[32,14,2,128]{3,2,1,0:T(2,128)} %bitcast.7), calls=%async_computation | async-start | bytes 917504 | tf_op jit(solution)/shard_map/all_to_all | solution.py:440
  34.1 5.4 %copy-start.9 = (f32[16,128]{1,0:T(8,128)S(1)}, f32[16,128]{1,0:T(8,128)}, u32[]{:S(2)}) copy-start(f32[16,128]{1,0:T(8,128)} %coef_ref.1) | copy-start | bytes 24580
  34.1 5.4 %copy-start.10 = (s32[16,128]{1,0:T(8,128)S(1)}, s32[16,128]{1,0:T(8,128)}, u32[]{:S(2)}) copy-start(s32[16,128]{1,0:T(8,128)} %mask_ref.1) | copy-start | bytes 24580
  34.1 5.4 %copy-start.11 = (f32[16,128]{1,0:T(8,128)S(1)}, f32[16,128]{1,0:T(8,128)}, u32[]{:S(2)}) copy-start(f32[16,128]{1,0:T(8,128)} %land_ref.1) | copy-start | bytes 24580
  34.1 5.4 %copy-start.12 = (s32[1,96]{1,0:T(1,128)S(1)}, s32[1,96]{1,0:T(1,128)}, u32[]{:S(2)}) copy-start(s32[1,96]{1,0:T(1,128)} %param.18) | copy-start | bytes 1156
  34.1 5.4 %copy-start.13 = (s32[1,96]{1,0:T(1,128)S(1)}, s32[1,96]{1,0:T(1,128)}, u32[]{:S(2)}) copy-start(s32[1,96]{1,0:T(1,128)} %param.19) | copy-start | bytes 1156
  48.8 32.5 %all-to-all-start.1 = ((f32[32,14,2,128]{3,2,1,0:T(2,128)}), f32[32,14,2,128]{3,2,1,0:T(2,128)S(1)}, u32[]{:S(2)}, u32[]{:S(2)}) async-start(f32[32,14,2,128]{3,2,1,0:T(2,128)} %bitcast.11), calls=%async_computation.1 | async-start | bytes 917504 | tf_op jit(solution)/shard_map/all_to_all | solution.py:440
  52.9 11.0 %collective-permute-start.3 = (f32[48,4,128]{2,1,0:T(4,128)}, f32[48,4,128]{2,1,0:T(4,128)S(1)}, u32[]{:S(2)}, u32[]{:S(2)}) collective-permute-start(f32[48,4,128]{2,1,0:T(4,128)} %get-tuple-element.10.refs_4_), channel_id=1, source_target_pairs={{0,3},{1,0},{2,1},{3,2},{4,7},{5,4},{6,5},{7,6},{8,11},{9,8},{10,9... | collective-permute-start | bytes 294920 | tf_op jit(solution)/shard_map/ppermute | solution.py:433
  63.8 7.9 %collective-permute-start.4 = (f32[48,4,128]{2,1,0:T(4,128)S(1)}, f32[48,4,128]{2,1,0:T(4,128)S(1)}, u32[]{:S(2)}, u32[]{:S(2)}) collective-permute-start(f32[48,4,128]{2,1,0:T(4,128)S(1)} %collective-permute-done.3.refs_7_), channel_id=1, source_target_pairs={{0,3},{1,0},{2,1},{3,2},{4,7},{5,4},{6,5},{7,6},{8,11},{9,8},{10,9... | collective-permute-start | bytes 294920 | tf_op jit(solution)/shard_map/ppermute | solution.py:433
  71.7 4.6 %collective-permute-start.5 = (f32[48,4,128]{2,1,0:T(4,128)S(1)}, f32[48,4,128]{2,1,0:T(4,128)S(1)}, u32[]{:S(2)}, u32[]{:S(2)}) collective-permute-start(f32[48,4,128]{2,1,0:T(4,128)S(1)} %collective-permute-done.4.refs_6_), channel_id=1, source_target_pairs={{0,3},{1,0},{2,1},{3,2},{4,7},{5,4},{6,5},{7,6},{8,11},{9,8},{10,9... | collective-permute-start | bytes 294920 | tf_op jit(solution)/shard_map/ppermute | solution.py:433
  76.3 0.9 %copy-start.1 = (f32[49,4,128]{2,1,0:T(4,128)S(1)}, f32[49,4,128]{2,1,0:T(4,128)}, u32[]{:S(2)}) copy-start(f32[49,4,128]{2,1,0:T(4,128)} %get-tuple-element.8.refs_0_) | copy-start | bytes 301060
  77.2 0.9 %copy-start.3 = (f32[49,4,128]{2,1,0:T(4,128)S(1)}, f32[49,4,128]{2,1,0:T(4,128)}, u32[]{:S(2)}) copy-start(f32[49,4,128]{2,1,0:T(4,128)} %copy-done.2) | copy-start | bytes 301060
  78.1 0.9 %copy-start.5 = (f32[49,4,128]{2,1,0:T(4,128)S(1)}, f32[49,4,128]{2,1,0:T(4,128)}, u32[]{:S(2)}) copy-start(f32[49,4,128]{2,1,0:T(4,128)} %copy-done.4) | copy-start | bytes 301060
  79.0 0.9 %copy-start.7 = (f32[49,4,128]{2,1,0:T(4,128)S(1)}, f32[49,4,128]{2,1,0:T(4,128)}, u32[]{:S(2)}) copy-start(f32[49,4,128]{2,1,0:T(4,128)} %copy-done.6) | copy-start | bytes 301060
  79.9 0.9 %copy-start.8 = (f32[48,4,128]{2,1,0:T(4,128)S(1)}, f32[48,4,128]{2,1,0:T(4,128)}, u32[]{:S(2)}) copy-start(f32[48,4,128]{2,1,0:T(4,128)} %get-tuple-element.10.refs_4_) | copy-start | bytes 294916
